TPU v7x, 512 devices: a whole 4x8x8 slice. The times are simulated.
512 devices in a mesh: ta: 8 (over z_hi, x), gx: 16 (over y, core), gy: 4 (over z_lo).
Axes of the slice: x: 4, y: 8, z: 8 (z_hi: 2, z_lo: 4; z = z_hi * 4 + z_lo), core: 2. Of those that a mesh axis runs over, the one named last changes fastest.
Arguments:
- frames: bfloat16 [8, 32, 256, 512], P('ta', None, 'gx', 'gy'), may hold values from -6 to 6
- trailing: bfloat16 [32, 256, 512], P(None, 'gx', 'gy'), may hold values from -6 to 6
Outputs:
- velocity: float32 [8, 3, 32, 256, 512], P('ta', None, None, 'gx', 'gy')
All inputs are finite; a program needn't handle non-finite values.
Results may differ from a plain program's by a relative error of at most 0.0003.
Values may be sent and summed in bfloat16 or wider, within the bound.
No kernel may reach another device: no remote copies, remote signals or barrier semaphores. Data moves between devices by JAX's collectives and lax.ppermute only.
A program may use at most 64 MiB of HBM per device.

v0:
```python
import jax
import jax.numpy as jnp
from jax import lax
from jax.sharding import PartitionSpec as P

ITERS = 3


gauss_taps = (0.0625, 0.25, 0.375, 0.25, 0.0625)
smoothness = 0.01


def passed_along(value, axis, steps):
    count = lax.axis_size(axis)
    initial, last = (max(0, -steps), min(count, count - steps))
    return lax.ppermute(value, axis, [(source, source + steps) for source in range(initial, last)])


def padded_2(block, sides, width):
    for axis, dim in sides:
        count = lax.axis_size(axis)
        forward = [(i, i + 1) for i in range(count - 1)]
        backward = [(target, source) for source, target in forward]
        low = lax.ppermute(
            lax.slice_in_dim(block, block.shape[dim] - width, None, axis=dim), axis, forward
        )
        high = lax.ppermute(lax.slice_in_dim(block, 0, width, axis=dim), axis, backward)
        block = jnp.concatenate([low, block, high], axis=dim)
    return block


def crop_rim(volume, amount):
    if amount == 0:
        return volume
    return volume[..., amount : volume.shape[-2] - amount, amount : volume.shape[-1] - amount]


def volume_mask(margin, width_x, width_y):
    x_index = (
        lax.axis_index("gx") * width_x - margin + jnp.arange(width_x + 2 * margin, dtype=jnp.int32)
    )
    y_index = (
        lax.axis_index("gy") * width_y - margin + jnp.arange(width_y + 2 * margin, dtype=jnp.int32)
    )
    inside_x = (x_index >= 0) & (x_index < width_x * lax.axis_size("gx"))
    inside_y = (y_index >= 0) & (y_index < width_y * lax.axis_size("gy"))
    return (inside_x[:, None] & inside_y[None, :]).astype(jnp.float32)


def smooth_block(volume):
    z_cells = volume.shape[0]
    padded = jnp.pad(volume, ((2, 2), (0, 0), (0, 0)))
    summed = jnp.zeros_like(volume)
    for tap_index in range(5):
        summed = summed + gauss_taps[tap_index] * padded[tap_index : tap_index + z_cells]
    length_x = summed.shape[1] - 4
    along_x = jnp.zeros((z_cells, length_x, summed.shape[2]), jnp.float32)
    for tap_index in range(5):
        along_x = along_x + gauss_taps[tap_index] * summed[:, tap_index : tap_index + length_x, :]
    length_y = along_x.shape[2] - 4
    along_y = jnp.zeros((z_cells, length_x, length_y), jnp.float32)
    for tap_index in range(5):
        along_y = along_y + gauss_taps[tap_index] * along_x[:, :, tap_index : tap_index + length_y]
    return along_y


def gradients(first_frame, second_frame):
    summed = first_frame + second_frame
    z_padded = jnp.pad(summed, ((1, 1), (0, 0), (0, 0)))
    slope_x = 0.25 * (summed[:, 2:, 1:-1] - summed[:, :-2, 1:-1])
    slope_y = 0.25 * (summed[:, 1:-1, 2:] - summed[:, 1:-1, :-2])
    slope_z = 0.25 * crop_rim(z_padded[2:] - z_padded[:-2], 1)
    return (jnp.stack([slope_x, slope_y, slope_z]), crop_rim(second_frame - first_frame, 1))


def neighbour_mean(velocity):
    z_padded = jnp.pad(velocity, ((0, 0), (1, 1), (0, 0), (0, 0)))
    summed = velocity[:, :, 2:, 1:-1] + velocity[:, :, :-2, 1:-1]
    summed = summed + velocity[:, :, 1:-1, 2:] + velocity[:, :, 1:-1, :-2]
    summed = summed + crop_rim(z_padded[:, 2:], 1) + crop_rim(z_padded[:, :-2], 1)
    return summed / 6.0


def on_device(frames, trailing):
    own_frame = frames[0]
    width_x = own_frame.shape[1]
    width_y = own_frame.shape[2]
    is_last = lax.axis_index("ta") == lax.axis_size("ta") - 1
    rim_width = 2
    arriving = passed_along(own_frame, "ta", -1)
    next_frame = jnp.where(is_last, trailing, arriving)
    near_first, near_second = (
        padded_2(own_frame, (("gx", 1), ("gy", 2)), rim_width),
        padded_2(next_frame, (("gx", 1), ("gy", 2)), rim_width),
    )
    inside = volume_mask(rim_width - 2, width_x, width_y)
    first_smooth = smooth_block(near_first.astype(jnp.float32)) * inside
    second_smooth = smooth_block(near_second.astype(jnp.float32)) * inside
    first_smooth, second_smooth = (
        padded_2(first_smooth, (("gx", 1), ("gy", 2)), 1),
        padded_2(second_smooth, (("gx", 1), ("gy", 2)), 1),
    )
    gradient, change = gradients(first_smooth, second_smooth)
    denominator = smoothness + jnp.sum(gradient * gradient, axis=0)
    velocity = jnp.zeros(gradient.shape, jnp.float32)
    for iteration in range(ITERS):
        if iteration == 0:
            mean_flow = jnp.zeros(gradient.shape, jnp.float32)
        else:
            velocity = padded_2(velocity, (("gx", 2), ("gy", 3)), 1)
            mean_flow = neighbour_mean(velocity)
        trim_by = (gradient.shape[2] - mean_flow.shape[2]) // 2
        margin_now = (mean_flow.shape[2] - width_x) // 2
        local_grad = crop_rim(gradient, trim_by)
        residual_term = (
            jnp.sum(local_grad * mean_flow, axis=0) + crop_rim(change, trim_by)
        ) / crop_rim(denominator, trim_by)
        velocity = (mean_flow - local_grad * residual_term[None]) * volume_mask(
            margin_now, width_x, width_y
        )
    return velocity[None]


def solution(mesh):
    return jax.shard_map(
        on_device,
        mesh=mesh,
        in_specs=(P("ta", None, "gx", "gy"), P(None, "gx", "gy")),
        out_specs=P("ta", None, None, "gx", "gy"),
        check_vma=False,
    )
```

profile of v0, /device:TPU:31, one launch (start us, length us, event | category | flops | bytes accessed | tf_op | source)
XLA Modules:
  0.0 141.3 jit_solution(970578570986254447)
XLA Ops:
  0.9 2.5 %collective-permute-start.8 = (bf16[32,16,128]{2,0,1:T(8,128)(2,1)S(1)}, bf16[32,16,128]{2,0,1:T(8,128)(2,1)S(1)}, u32[]{:S(2)}, u32[]{:S(2)}) collective-permute-start(bf16[32,16,128]{2,0,1:T(8,128)(2,1)S(1)} %bitcast.15), channel_id=1, source_target_pairs={{64,0},{128,64},{192,128},{256,192},{320,256},{384,320},{448,384},... | collective-permute-start | bytes 393224 | tf_op jit(solution)/shard_map/ppermute | solution.py:16
  3.4 5.3 %collective-permute-start = (bf16[32,2,128]{2,0,1:T(8,128)(2,1)S(1)}, bf16[32,2,128]{2,0,1:T(8,128)(2,1)S(1)}, u32[]{:S(2)}, u32[]{:S(2)}) collective-permute-start(bf16[32,2,128]{2,0,1:T(8,128)(2,1)S(1)} %get-tuple-element.35), channel_id=1, source_target_pairs={{0,4},{4,8},{8,12},{12,16},{16,20},{20,24},{24,28},{28,32},{32,36}... | collective-permute-start | bytes 49160 | tf_op jit(solution)/shard_map/ppermute | solution.py:24
  10.7 4.6 %collective-permute-done.1 = bf16[32,2,128]{2,0,1:T(8,128)(2,1)S(1)} collective-permute-done((bf16[32,2,128]{2,0,1:T(8,128)(2,1)S(1)}, bf16[32,2,128]{2,0,1:T(8,128)(2,1)S(1)}, u32[]{:S(2)}, u32[]{:S(2)}) %collective-permute-start.1) | collective-permute-done | bytes 16416 | tf_op jit(solution)/shard_map/ppermute | solution.py:27
  15.4 3.7 %collective-permute-start.2 = (bf16[32,20,2]{2,0,1:T(8,128)(2,1)S(1)}, bf16[32,20,2]{2,0,1:T(8,128)(2,1)S(1)}, u32[]{:S(2)}, u32[]{:S(2)}) collective-permute-start(bf16[32,20,2]{2,0,1:T(8,128)(2,1)S(1)} %get-tuple-element.31), channel_id=1, source_target_pairs={{0,1},{1,2},{2,3},{4,5},{5,6},{6,7},{8,9},{9,10},{10,11},{12,13},{... | collective-permute-start | bytes 7688 | tf_op jit(solution)/shard_map/ppermute | solution.py:24
  21.3 4.8 %collective-permute-done.3 = bf16[32,20,2]{2,0,1:T(8,128)(2,1)S(1)} collective-permute-done((bf16[32,20,2]{2,0,1:T(8,128)(2,1)S(1)}, bf16[32,20,2]{2,0,1:T(8,128)(2,1)S(1)}, u32[]{:S(2)}, u32[]{:S(2)}) %collective-permute-start.3) | collective-permute-done | bytes 2592 | tf_op jit(solution)/shard_map/ppermute | solution.py:27
  27.3 3.1 %collective-permute-start.9 = (bf16[32,2,128]{2,0,1:T(8,128)(2,1)S(1)}, bf16[32,2,128]{2,0,1:T(8,128)(2,1)S(1)}, u32[]{:S(2)}, u32[]{:S(2)}) collective-permute-start(bf16[32,2,128]{2,0,1:T(8,128)(2,1)S(1)} %get-tuple-element.37), channel_id=1, source_target_pairs={{0,4},{4,8},{8,12},{12,16},{16,20},{20,24},{24,28},{28,32},{32,36}... | collective-permute-start | bytes 49160 | tf_op jit(solution)/shard_map/ppermute | solution.py:24
  32.6 4.1 %collective-permute-done.10 = bf16[32,2,128]{2,0,1:T(8,128)(2,1)S(1)} collective-permute-done((bf16[32,2,128]{2,0,1:T(8,128)(2,1)S(1)}, bf16[32,2,128]{2,0,1:T(8,128)(2,1)S(1)}, u32[]{:S(2)}, u32[]{:S(2)}) %collective-permute-start.10) | collective-permute-done | bytes 16416 | tf_op jit(solution)/shard_map/ppermute | solution.py:27
  36.9 4.3 %collective-permute-start.11 = (bf16[32,20,2]{2,0,1:T(8,128)(2,1)S(1)}, bf16[32,20,2]{2,0,1:T(8,128)(2,1)S(1)}, u32[]{:S(2)}, u32[]{:S(2)}) collective-permute-start(bf16[32,20,2]{2,0,1:T(8,128)(2,1)S(1)} %get-tuple-element.33), channel_id=1, source_target_pairs={{0,1},{1,2},{2,3},{4,5},{5,6},{6,7},{8,9},{9,10},{10,11},{12,13},{... | collective-permute-start | bytes 7688 | tf_op jit(solution)/shard_map/ppermute | solution.py:24
  43.4 3.8 %collective-permute-done.12 = bf16[32,20,2]{2,0,1:T(8,128)(2,1)S(1)} collective-permute-done((bf16[32,20,2]{2,0,1:T(8,128)(2,1)S(1)}, bf16[32,20,2]{2,0,1:T(8,128)(2,1)S(1)}, u32[]{:S(2)}, u32[]{:S(2)}) %collective-permute-start.12) | collective-permute-done | bytes 2592 | tf_op jit(solution)/shard_map/ppermute | solution.py:27
  49.1 3.4 %collective-permute-start.13 = (f32[32,1,128]{2,1,0:T(1,128)S(1)}, f32[32,1,128]{2,1,0:T(1,128)S(1)}, u32[]{:S(2)}, u32[]{:S(2)}) collective-permute-start(f32[32,1,128]{2,1,0:T(1,128)S(1)} %get-tuple-element.29), channel_id=1, source_target_pairs={{0,4},{4,8},{8,12},{12,16},{16,20},{20,24},{24,28},{28,32},{32,36}... | collective-permute-start | bytes 49160 | tf_op jit(solution)/shard_map/ppermute | solution.py:24
  54.7 4.9 %collective-permute-start.4 = (f32[32,1,128]{2,1,0:T(1,128)S(1)}, f32[32,1,128]{2,1,0:T(1,128)S(1)}, u32[]{:S(2)}, u32[]{:S(2)}) collective-permute-start(f32[32,1,128]{2,1,0:T(1,128)S(1)} %get-tuple-element.27), channel_id=1, source_target_pairs={{0,4},{4,8},{8,12},{12,16},{16,20},{20,24},{24,28},{28,32},{32,36}... | collective-permute-start | bytes 49160 | tf_op jit(solution)/shard_map/ppermute | solution.py:24
  61.7 3.4 %collective-permute-start.15 = (f32[32,18,1]{2,0,1:T(8,128)S(1)}, f32[32,18,1]{2,0,1:T(8,128)S(1)}, u32[]{:S(2)}, u32[]{:S(2)}) collective-permute-start(f32[32,18,1]{2,0,1:T(8,128)S(1)} %get-tuple-element.25), channel_id=1, source_target_pairs={{0,1},{1,2},{2,3},{4,5},{5,6},{6,7},{8,9},{9,10},{10,11},{12,13},{... | collective-permute-start | bytes 6920 | tf_op jit(solution)/shard_map/ppermute | solution.py:24
  66.6 4.0 %collective-permute-start.6 = (f32[32,18,1]{2,0,1:T(8,128)S(1)}, f32[32,18,1]{2,0,1:T(8,128)S(1)}, u32[]{:S(2)}, u32[]{:S(2)}) collective-permute-start(f32[32,18,1]{2,0,1:T(8,128)S(1)} %get-tuple-element.23), channel_id=1, source_target_pairs={{0,1},{1,2},{2,3},{4,5},{5,6},{6,7},{8,9},{9,10},{10,11},{12,13},{... | collective-permute-start | bytes 6920 | tf_op jit(solution)/shard_map/ppermute | solution.py:24
  71.9 2.9 %collective-permute-done.16 = f32[32,18,1]{2,0,1:T(8,128)S(1)} collective-permute-done((f32[32,18,1]{2,0,1:T(8,128)S(1)}, f32[32,18,1]{2,0,1:T(8,128)S(1)}, u32[]{:S(2)}, u32[]{:S(2)}) %collective-permute-start.16) | collective-permute-done | bytes 2336 | tf_op jit(solution)/shard_map/ppermute | solution.py:27
  76.4 4.1 %collective-permute-done.7 = f32[32,18,1]{2,0,1:T(8,128)S(1)} collective-permute-done((f32[32,18,1]{2,0,1:T(8,128)S(1)}, f32[32,18,1]{2,0,1:T(8,128)S(1)}, u32[]{:S(2)}, u32[]{:S(2)}) %collective-permute-start.7) | collective-permute-done | bytes 2336 | tf_op jit(solution)/shard_map/ppermute | solution.py:27
  82.8 4.6 %collective-permute-start.18 = (f32[3,32,1,128]{3,2,1,0:T(1,128)S(1)}, f32[3,32,1,128]{3,2,1,0:T(1,128)S(1)}, u32[]{:S(2)}, u32[]{:S(2)}) collective-permute-start(f32[3,32,1,128]{3,2,1,0:T(1,128)S(1)} %get-tuple-element.17), channel_id=1, source_target_pairs={{0,4},{4,8},{8,12},{12,16},{16,20},{20,24},{24,28},{28,32},{32,36}... | collective-permute-start | bytes 147464 | tf_op jit(solution)/shard_map/ppermute | solution.py:24
  89.4 4.7 %collective-permute-done.17 = f32[3,32,1,128]{3,2,1,0:T(1,128)S(1)} collective-permute-done((f32[3,32,1,128]{3,2,1,0:T(1,128)S(1)}, f32[3,32,1,128]{3,2,1,0:T(1,128)S(1)}, u32[]{:S(2)}, u32[]{:S(2)}) %collective-permute-start.17) | collective-permute-done | bytes 49184 | tf_op jit(solution)/shard_map/ppermute | solution.py:27
  101.6 2.7 %collective-permute-done.19 = f32[3,32,18,1]{1,3,2,0:T(1,128)} collective-permute-done((f32[3,32,18,1]{1,3,2,0:T(1,128)S(1)}, f32[3,32,18,1]{1,3,2,0:T(1,128)}, u32[]{:S(2)}, u32[]{:S(2)}) %collective-permute-start.19) | collective-permute-done | bytes 6944 | tf_op jit(solution)/shard_map/ppermute | solution.py:27
  104.3 2.3 %copy.151 = f32[3,32,18,1]{3,2,1,0:T(8,128)} copy(f32[3,32,18,1]{1,3,2,0:T(1,128)} %collective-permute-done.19) | data formatting | bytes 13824 | tf_op jit(solution)/shard_map/ppermute | solution.py:27
  106.6 2.8 %select_maximum_fusion.4 = f32[3,34,18,130]{3,2,1,0:T(8,128)S(1)} fusion(f32[3,32,18,1]{3,2,1,0:T(8,128)} %copy.151, f32[3,32,18,1]{3,2,1,0:T(8,128)S(1)} %copy.153, f32[3,32,1,128]{3,2,1,0:T(1,128)S(1)} %collective-permute-done.17, f32[3,32,16,128]{3,2,1,0:T(8,128)S(1)} %subtract_multiply_fusion.1, f32[3,32,1,128]{3,2,1,0:T(1,128)S(1)} %collective-permute-done.18), kind=kLoop, calls=%fused_computation.6 | loop fusion | flops 2864160 | bytes 1853280 | tf_op jit(solution)/shard_map/concatenate | solution.py:28
  112.4 3.3 %collective-permute-start.22 = (f32[3,32,1,128]{3,2,1,0:T(1,128)S(1)}, f32[3,32,1,128]{3,2,1,0:T(1,128)S(1)}, u32[]{:S(2)}, u32[]{:S(2)}) collective-permute-start(f32[3,32,1,128]{3,2,1,0:T(1,128)S(1)} %get-tuple-element.15), channel_id=1, source_target_pairs={{0,4},{4,8},{8,12},{12,16},{16,20},{20,24},{24,28},{28,32},{32,36}... | collective-permute-start | bytes 147464 | tf_op jit(solution)/shard_map/ppermute | solution.py:24
  117.7 4.7 %collective-permute-done.21 = f32[3,32,1,128]{3,2,1,0:T(1,128)S(1)} collective-permute-done((f32[3,32,1,128]{3,2,1,0:T(1,128)S(1)}, f32[3,32,1,128]{3,2,1,0:T(1,128)S(1)}, u32[]{:S(2)}, u32[]{:S(2)}) %collective-permute-start.21) | collective-permute-done | bytes 49184 | tf_op jit(solution)/shard_map/ppermute | solution.py:27
  129.5 2.9 %collective-permute-done.23 = f32[3,32,18,1]{1,3,2,0:T(1,128)} collective-permute-done((f32[3,32,18,1]{1,3,2,0:T(1,128)S(1)}, f32[3,32,18,1]{1,3,2,0:T(1,128)}, u32[]{:S(2)}, u32[]{:S(2)}) %collective-permute-start.23) | collective-permute-done | bytes 6944 | tf_op jit(solution)/shard_map/ppermute | solution.py:27
  134.7 2.8 %select_maximum_fusion = f32[3,34,18,130]{3,2,1,0:T(8,128)S(1)} fusion(f32[3,32,18,1]{3,2,1,0:T(8,128)} %copy.159, f32[3,32,18,1]{3,2,1,0:T(8,128)S(1)} %copy.161, f32[3,32,1,128]{3,2,1,0:T(1,128)S(1)} %collective-permute-done.21, f32[3,32,16,128]{3,2,1,0:T(8,128)S(1)} %subtract_multiply_fusion, f32[3,32,1,128]{3,2,1,0:T(1,128)S(1)} %collective-permute-done.22), kind=kLoop, calls=%fused_computation.2 | loop fusion | flops 2864160 | bytes 1853280 | tf_op jit(solution)/shard_map/concatenate | solution.py:28
  (99 shorter events, 51.2 us)
Async XLA Ops:
  0.9 25.4 %collective-permute-start.8 = (bf16[32,16,128]{2,0,1:T(8,128)(2,1)S(1)}, bf16[32,16,128]{2,0,1:T(8,128)(2,1)S(1)}, u32[]{:S(2)}, u32[]{:S(2)}) collective-permute-start(bf16[32,16,128]{2,0,1:T(8,128)(2,1)S(1)} %bitcast.15), channel_id=1, source_target_pairs={{64,0},{128,64},{192,128},{256,192},{320,256},{384,320},{448,384},... | collective-permute-start | bytes 393224 | tf_op jit(solution)/shard_map/ppermute | solution.py:16
  3.4 7.2 %collective-permute-start = (bf16[32,2,128]{2,0,1:T(8,128)(2,1)S(1)}, bf16[32,2,128]{2,0,1:T(8,128)(2,1)S(1)}, u32[]{:S(2)}, u32[]{:S(2)}) collective-permute-start(bf16[32,2,128]{2,0,1:T(8,128)(2,1)S(1)} %get-tuple-element.35), channel_id=1, source_target_pairs={{0,4},{4,8},{8,12},{12,16},{16,20},{20,24},{24,28},{28,32},{32,36}... | collective-permute-start | bytes 49160 | tf_op jit(solution)/shard_map/ppermute | solution.py:24
  8.7 6.6 %collective-permute-start.1 = (bf16[32,2,128]{2,0,1:T(8,128)(2,1)S(1)}, bf16[32,2,128]{2,0,1:T(8,128)(2,1)S(1)}, u32[]{:S(2)}, u32[]{:S(2)}) collective-permute-start(bf16[32,2,128]{2,0,1:T(8,128)(2,1)S(1)} %get-tuple-element.36), channel_id=1, source_target_pairs={{4,0},{8,4},{12,8},{16,12},{20,16},{24,20},{28,24},{32,28},{36,32}... | collective-permute-start | bytes 49160 | tf_op jit(solution)/shard_map/ppermute | solution.py:27
  15.4 6.0 %collective-permute-start.2 = (bf16[32,20,2]{2,0,1:T(8,128)(2,1)S(1)}, bf16[32,20,2]{2,0,1:T(8,128)(2,1)S(1)}, u32[]{:S(2)}, u32[]{:S(2)}) collective-permute-start(bf16[32,20,2]{2,0,1:T(8,128)(2,1)S(1)} %get-tuple-element.31), channel_id=1, source_target_pairs={{0,1},{1,2},{2,3},{4,5},{5,6},{6,7},{8,9},{9,10},{10,11},{12,13},{... | collective-permute-start | bytes 7688 | tf_op jit(solution)/shard_map/ppermute | solution.py:24
  19.1 7.0 %collective-permute-start.3 = (bf16[32,20,2]{2,0,1:T(8,128)(2,1)S(1)}, bf16[32,20,2]{2,0,1:T(8,128)(2,1)S(1)}, u32[]{:S(2)}, u32[]{:S(2)}) collective-permute-start(bf16[32,20,2]{2,0,1:T(8,128)(2,1)S(1)} %get-tuple-element.32), channel_id=1, source_target_pairs={{1,0},{2,1},{3,2},{5,4},{6,5},{7,6},{9,8},{10,9},{11,10},{13,12},{... | collective-permute-start | bytes 7688 | tf_op jit(solution)/shard_map/ppermute | solution.py:27
  27.3 5.3 %collective-permute-start.9 = (bf16[32,2,128]{2,0,1:T(8,128)(2,1)S(1)}, bf16[32,2,128]{2,0,1:T(8,128)(2,1)S(1)}, u32[]{:S(2)}, u32[]{:S(2)}) collective-permute-start(bf16[32,2,128]{2,0,1:T(8,128)(2,1)S(1)} %get-tuple-element.37), channel_id=1, source_target_pairs={{0,4},{4,8},{8,12},{12,16},{16,20},{20,24},{24,28},{28,32},{32,36}... | collective-permute-start | bytes 49160 | tf_op jit(solution)/shard_map/ppermute | solution.py:24
  30.4 6.3 %collective-permute-start.10 = (bf16[32,2,128]{2,0,1:T(8,128)(2,1)S(1)}, bf16[32,2,128]{2,0,1:T(8,128)(2,1)S(1)}, u32[]{:S(2)}, u32[]{:S(2)}) collective-permute-start(bf16[32,2,128]{2,0,1:T(8,128)(2,1)S(1)} %get-tuple-element.38), channel_id=1, source_target_pairs={{4,0},{8,4},{12,8},{16,12},{20,16},{24,20},{28,24},{32,28},{36,32}... | collective-permute-start | bytes 49160 | tf_op jit(solution)/shard_map/ppermute | solution.py:27
  36.9 6.5 %collective-permute-start.11 = (bf16[32,20,2]{2,0,1:T(8,128)(2,1)S(1)}, bf16[32,20,2]{2,0,1:T(8,128)(2,1)S(1)}, u32[]{:S(2)}, u32[]{:S(2)}) collective-permute-start(bf16[32,20,2]{2,0,1:T(8,128)(2,1)S(1)} %get-tuple-element.33), channel_id=1, source_target_pairs={{0,1},{1,2},{2,3},{4,5},{5,6},{6,7},{8,9},{9,10},{10,11},{12,13},{... | collective-permute-start | bytes 7688 | tf_op jit(solution)/shard_map/ppermute | solution.py:24
  41.2 6.1 %collective-permute-start.12 = (bf16[32,20,2]{2,0,1:T(8,128)(2,1)S(1)}, bf16[32,20,2]{2,0,1:T(8,128)(2,1)S(1)}, u32[]{:S(2)}, u32[]{:S(2)}) collective-permute-start(bf16[32,20,2]{2,0,1:T(8,128)(2,1)S(1)} %get-tuple-element.34), channel_id=1, source_target_pairs={{1,0},{2,1},{3,2},{5,4},{6,5},{7,6},{9,8},{10,9},{11,10},{13,12},{... | collective-permute-start | bytes 7688 | tf_op jit(solution)/shard_map/ppermute | solution.py:27
  49.1 12.4 %collective-permute-start.13 = (f32[32,1,128]{2,1,0:T(1,128)S(1)}, f32[32,1,128]{2,1,0:T(1,128)S(1)}, u32[]{:S(2)}, u32[]{:S(2)}) collective-permute-start(f32[32,1,128]{2,1,0:T(1,128)S(1)} %get-tuple-element.29), channel_id=1, source_target_pairs={{0,4},{4,8},{8,12},{12,16},{16,20},{20,24},{24,28},{28,32},{32,36}... | collective-permute-start | bytes 49160 | tf_op jit(solution)/shard_map/ppermute | solution.py:24
  52.5 9.0 %collective-permute-start.14 = (f32[32,1,128]{2,1,0:T(1,128)S(1)}, f32[32,1,128]{2,1,0:T(1,128)S(1)}, u32[]{:S(2)}, u32[]{:S(2)}) collective-permute-start(f32[32,1,128]{2,1,0:T(1,128)S(1)} %get-tuple-element.30), channel_id=1, source_target_pairs={{4,0},{8,4},{12,8},{16,12},{20,16},{24,20},{28,24},{32,28},{36,32}... | collective-permute-start | bytes 49160 | tf_op jit(solution)/shard_map/ppermute | solution.py:27
  54.7 11.7 %collective-permute-start.4 = (f32[32,1,128]{2,1,0:T(1,128)S(1)}, f32[32,1,128]{2,1,0:T(1,128)S(1)}, u32[]{:S(2)}, u32[]{:S(2)}) collective-permute-start(f32[32,1,128]{2,1,0:T(1,128)S(1)} %get-tuple-element.27), channel_id=1, source_target_pairs={{0,4},{4,8},{8,12},{12,16},{16,20},{20,24},{24,28},{28,32},{32,36}... | collective-permute-start | bytes 49160 | tf_op jit(solution)/shard_map/ppermute | solution.py:24
  59.5 6.8 %collective-permute-start.5 = (f32[32,1,128]{2,1,0:T(1,128)S(1)}, f32[32,1,128]{2,1,0:T(1,128)S(1)}, u32[]{:S(2)}, u32[]{:S(2)}) collective-permute-start(f32[32,1,128]{2,1,0:T(1,128)S(1)} %get-tuple-element.28), channel_id=1, source_target_pairs={{4,0},{8,4},{12,8},{16,12},{20,16},{24,20},{28,24},{32,28},{36,32}... | collective-permute-start | bytes 49160 | tf_op jit(solution)/shard_map/ppermute | solution.py:27
  61.7 10.2 %collective-permute-start.15 = (f32[32,18,1]{2,0,1:T(8,128)S(1)}, f32[32,18,1]{2,0,1:T(8,128)S(1)}, u32[]{:S(2)}, u32[]{:S(2)}) collective-permute-start(f32[32,18,1]{2,0,1:T(8,128)S(1)} %get-tuple-element.25), channel_id=1, source_target_pairs={{0,1},{1,2},{2,3},{4,5},{5,6},{6,7},{8,9},{9,10},{10,11},{12,13},{... | collective-permute-start | bytes 6920 | tf_op jit(solution)/shard_map/ppermute | solution.py:24
  65.1 9.7 %collective-permute-start.16 = (f32[32,18,1]{2,0,1:T(8,128)S(1)}, f32[32,18,1]{2,0,1:T(8,128)S(1)}, u32[]{:S(2)}, u32[]{:S(2)}) collective-permute-start(f32[32,18,1]{2,0,1:T(8,128)S(1)} %get-tuple-element.26), channel_id=1, source_target_pairs={{1,0},{2,1},{3,2},{5,4},{6,5},{7,6},{9,8},{10,9},{11,10},{13,12},{... | collective-permute-start | bytes 6920 | tf_op jit(solution)/shard_map/ppermute | solution.py:27
  66.6 9.9 %collective-permute-start.6 = (f32[32,18,1]{2,0,1:T(8,128)S(1)}, f32[32,18,1]{2,0,1:T(8,128)S(1)}, u32[]{:S(2)}, u32[]{:S(2)}) collective-permute-start(f32[32,18,1]{2,0,1:T(8,128)S(1)} %get-tuple-element.23), channel_id=1, source_target_pairs={{0,1},{1,2},{2,3},{4,5},{5,6},{6,7},{8,9},{9,10},{10,11},{12,13},{... | collective-permute-start | bytes 6920 | tf_op jit(solution)/shard_map/ppermute | solution.py:24
  70.6 10.0 %collective-permute-start.7 = (f32[32,18,1]{2,0,1:T(8,128)S(1)}, f32[32,18,1]{2,0,1:T(8,128)S(1)}, u32[]{:S(2)}, u32[]{:S(2)}) collective-permute-start(f32[32,18,1]{2,0,1:T(8,128)S(1)} %get-tuple-element.24), channel_id=1, source_target_pairs={{1,0},{2,1},{3,2},{5,4},{6,5},{7,6},{9,8},{10,9},{11,10},{13,12},{... | collective-permute-start | bytes 6920 | tf_op jit(solution)/shard_map/ppermute | solution.py:27
  82.8 6.5 %collective-permute-start.18 = (f32[3,32,1,128]{3,2,1,0:T(1,128)S(1)}, f32[3,32,1,128]{3,2,1,0:T(1,128)S(1)}, u32[]{:S(2)}, u32[]{:S(2)}) collective-permute-start(f32[3,32,1,128]{3,2,1,0:T(1,128)S(1)} %get-tuple-element.17), channel_id=1, source_target_pairs={{0,4},{4,8},{8,12},{12,16},{16,20},{20,24},{24,28},{28,32},{32,36}... | collective-permute-start | bytes 147464 | tf_op jit(solution)/shard_map/ppermute | solution.py:24
  87.4 6.6 %collective-permute-start.17 = (f32[3,32,1,128]{3,2,1,0:T(1,128)S(1)}, f32[3,32,1,128]{3,2,1,0:T(1,128)S(1)}, u32[]{:S(2)}, u32[]{:S(2)}) collective-permute-start(f32[3,32,1,128]{3,2,1,0:T(1,128)S(1)} %get-tuple-element.18), channel_id=1, source_target_pairs={{4,0},{8,4},{12,8},{16,12},{20,16},{24,20},{28,24},{32,28},{36,32}... | collective-permute-start | bytes 147464 | tf_op jit(solution)/shard_map/ppermute | solution.py:27
  97.3 3.8 %collective-permute-start.20 = (f32[3,32,18,1]{1,3,2,0:T(1,128)S(1)}, f32[3,32,18,1]{1,3,2,0:T(1,128)S(1)}, u32[]{:S(2)}, u32[]{:S(2)}) collective-permute-start(f32[3,32,18,1]{1,3,2,0:T(1,128)S(1)} %copy.152), channel_id=1, source_target_pairs={{0,1},{1,2},{2,3},{4,5},{5,6},{6,7},{8,9},{9,10},{10,11},{12,13},{... | collective-permute-start | bytes 20744 | tf_op jit(solution)/shard_map/ppermute | solution.py:24
  99.6 4.7 %collective-permute-start.19 = (f32[3,32,18,1]{1,3,2,0:T(1,128)S(1)}, f32[3,32,18,1]{1,3,2,0:T(1,128)}, u32[]{:S(2)}, u32[]{:S(2)}) collective-permute-start(f32[3,32,18,1]{1,3,2,0:T(1,128)S(1)} %copy.150), channel_id=1, source_target_pairs={{1,0},{2,1},{3,2},{5,4},{6,5},{7,6},{9,8},{10,9},{11,10},{13,12},{... | collective-permute-start | bytes 20744 | tf_op jit(solution)/shard_map/ppermute | solution.py:27
  112.4 5.3 %collective-permute-start.22 = (f32[3,32,1,128]{3,2,1,0:T(1,128)S(1)}, f32[3,32,1,128]{3,2,1,0:T(1,128)S(1)}, u32[]{:S(2)}, u32[]{:S(2)}) collective-permute-start(f32[3,32,1,128]{3,2,1,0:T(1,128)S(1)} %get-tuple-element.15), channel_id=1, source_target_pairs={{0,4},{4,8},{8,12},{12,16},{16,20},{20,24},{24,28},{28,32},{32,36}... | collective-permute-start | bytes 147464 | tf_op jit(solution)/shard_map/ppermute | solution.py:24
  115.8 6.6 %collective-permute-start.21 = (f32[3,32,1,128]{3,2,1,0:T(1,128)S(1)}, f32[3,32,1,128]{3,2,1,0:T(1,128)S(1)}, u32[]{:S(2)}, u32[]{:S(2)}) collective-permute-start(f32[3,32,1,128]{3,2,1,0:T(1,128)S(1)} %get-tuple-element.16), channel_id=1, source_target_pairs={{4,0},{8,4},{12,8},{16,12},{20,16},{24,20},{28,24},{32,28},{36,32}... | collective-permute-start | bytes 147464 | tf_op jit(solution)/shard_map/ppermute | solution.py:27
  127.7 4.7 %collective-permute-start.23 = (f32[3,32,18,1]{1,3,2,0:T(1,128)S(1)}, f32[3,32,18,1]{1,3,2,0:T(1,128)}, u32[]{:S(2)}, u32[]{:S(2)}) collective-permute-start(f32[3,32,18,1]{1,3,2,0:T(1,128)S(1)} %copy.158), channel_id=1, source_target_pairs={{1,0},{2,1},{3,2},{5,4},{6,5},{7,6},{9,8},{10,9},{11,10},{13,12},{... | collective-permute-start | bytes 20744 | tf_op jit(solution)/shard_map/ppermute | solution.py:27
  (7 other events, 20.2 us)
where the time goes:
time: 142 us; the launch traced here: 141 us
  starting transfers between devices  65.4 us (46%)
  waiting for transfers between devices  42.2 us (30%)
  other arithmetic  18.1 us (13%)
  local copies, waits for them, and re-layouts  14.9 us (10%)
    ppermute x12, starting transfers between devices, padded_2(): lax.ppermute(lax.slice_in_dim(block, block.shape[dim] - width, None, axis...  43.5 us
    ppermute x12, waiting for transfers between devices, padded_2(): lax.ppermute(lax.slice_in_dim(block, 0, width, axis=dim), axis, backward)  39.2 us
    ppermute x12, starting transfers between devices, padded_2(): lax.ppermute(lax.slice_in_dim(block, 0, width, axis=dim), axis, backward)  19.4 us
    concatenate x12, other arithmetic, padded_2(): block = jnp.concatenate([low, block, high], axis=dim)  7.02 us
    slice x14, local copies, waits for them, and re-layouts, padded_2(): lax.slice_in_dim(block, block.shape[dim] - width, None, axis=dim)  6.89 us
    ppermute x2, local copies, waits for them, and re-layouts, padded_2(): lax.ppermute(lax.slice_in_dim(block, 0, width, axis=dim), axis, backward)  4.53 us
    ppermute x12, waiting for transfers between devices, padded_2(): lax.ppermute(lax.slice_in_dim(block, block.shape[dim] - width, None, axis...  2.98 us
  transfers between devices with their start and end apart: 25, of which 13 were waited for; matrix products, arithmetic and copies ran while one was open for 2% of the time, Pallas kernels for 0%

commit v1 on v0

v1 whole, which is shorter than its diff:
```python
import jax
import jax.numpy as jnp
from jax import lax
from jax.experimental import pallas as pl
from jax.experimental.pallas import tpu as pltpu
from jax.sharding import PartitionSpec as P

NZ = 32
WX = 16
LANES = 128
EDGE = 8
F32, BF16 = jnp.float32, jnp.bfloat16


def iota(shape, dim):
    return lax.broadcasted_iota(jnp.int32, shape, dim)


def group_rows(group, own, nxt, low, high):
    frame, block = divmod(group, 8)
    zs = pl.ds(4 * block, 4)
    centre = (own, nxt)[frame][zs].astype(F32)
    before, after = low[frame, zs].astype(F32), high[frame, zs].astype(F32)
    return jnp.concatenate([before, centre, after], axis=1).reshape(128, LANES)


def pack_kernel(own, nxt, low, high, to_right, to_left):
    row, lane = iota((LANES, 256), 0), iota((LANES, 256), 1)
    right = jnp.where(row >= LANES - EDGE, lane - row + LANES - EDGE, -1)
    right = jnp.where(lane < 128, right, -1)
    left = jnp.where(row < EDGE, lane - 128 - row, -1)
    left = jnp.where(lane < 128, -1, left)
    place = jnp.maximum(right, left)
    packed = jnp.zeros((128, 256), F32)
    for group in range(16):
        rows = group_rows(group, own, nxt, low, high).astype(BF16)
        pick = jnp.where(place == 8 * group, 1.0, 0.0).astype(BF16)
        packed = packed + jnp.dot(rows, pick, preferred_element_type=F32)
    to_right[...] = packed[:, :128].astype(BF16)
    to_left[...] = packed[:, 128:].astype(BF16)


def y_taps(distance):
    d = jnp.minimum(distance & 255, (-distance) & 255)
    tap = jnp.where(d == 0, 6.0, jnp.where(d == 1, 4.0, jnp.where(d == 2, 1.0, 0.0)))
    return tap * (1.0 / 4096.0)


def z_next(v, row):
    return jnp.where(row == NZ - 1, 0.0, pltpu.roll(v, NZ - 1, 0))


def z_prev(v, row):
    return jnp.where(row == 0, 0.0, pltpu.roll(v, 1, 0))


def y_next(v, other, lane):
    return pltpu.roll(jnp.where(lane == 0, other, v), LANES - 1, 1)


def y_prev(v, other, lane):
    return pltpu.roll(jnp.where(lane == LANES - 1, other, v), 1, 1)


def flow_kernel(own, nxt, low, high, from_left, from_right, out, p_ref, q_ref, s_ref, c_ref, h_ref, u_ref, v_ref):
    gx, gy = lax.axis_index("gx"), lax.axis_index("gy")
    n_gx, n_gy = lax.axis_size("gx"), lax.axis_size("gy")
    row, lane = iota((NZ, LANES), 0), iota((NZ, LANES), 1)

    main_taps = y_taps(iota((LANES, 256), 1) - iota((LANES, 256), 0)).astype(BF16)
    column = iota((EDGE, 256), 1)
    left_taps = y_taps(column - (iota((EDGE, 256), 0) + 248))
    right_taps = y_taps(column - (iota((EDGE, 256), 0) + 128))
    edges = jnp.concatenate([from_left[...], from_right[...]], axis=1)

    def smooth_y(group):
        rows = group_rows(group, own, nxt, low, high).astype(BF16)
        parts = []
        for taps in (left_taps, right_taps):
            if group > 0:
                parts.append(jnp.zeros((8 * group, 256), F32))
            parts.append(taps)
            if group < 15:
                parts.append(jnp.zeros((120 - 8 * group, 256), F32))
        edge_taps = jnp.concatenate(parts, axis=0).astype(BF16)
        return jnp.dot(rows, main_taps, preferred_element_type=F32) + jnp.dot(
            edges, edge_taps, preferred_element_type=F32
        )

    for block in range(8):
        first, second = smooth_y(block), smooth_y(8 + block)
        total, change = (first + second) * 0.25, second - first
        for i in range(4):
            z = 4 * block + i
            for tile in range(2):
                part = (slice(32 * i, 32 * i + 32), slice(128 * tile, 128 * tile + 128))
                p_ref[tile, pl.ds(z, 32, stride=NZ), :] = total[part]
                q_ref[tile, pl.ds(z, 32, stride=NZ), :] = change[part]

    def smooth_z(v):
        near = z_next(v, row) + z_prev(v, row)
        far = jnp.where(row >= NZ - 2, 0.0, pltpu.roll(v, NZ - 2, 0)) + jnp.where(
            row < 2, 0.0, pltpu.roll(v, 2, 0)
        )
        return 6.0 * v + 4.0 * near + far

    def plane_z(k, _):
        at = pl.ds(pl.multiple_of(k * NZ, NZ), NZ)
        for ref in (p_ref, q_ref):
            for tile in range(2):
                ref[tile, at, :] = smooth_z(ref[tile, at, :])
        return 0

    lax.fori_loop(3, 29, plane_z, 0)

    inside_y = jnp.where(
        lane < 64, jnp.where(gy == n_gy - 1, 0.0, 1.0), jnp.where(gy == 0, 0.0, 1.0)
    )

    def inside_x(x):
        low_out = (x < 0) & (gx == 0)
        high_out = (x >= WX) & (gx == n_gx - 1)
        return jnp.where(low_out | high_out, 0.0, 1.0)

    def plane_x(k, _):
        weight = inside_x(k - 3)
        for source, ref in ((p_ref, s_ref), (q_ref, c_ref)):
            for tile in range(2):
                planes = [
                    source[tile, pl.ds(pl.multiple_of((k + 3 + j) * NZ, NZ), NZ), :] for j in range(5)
                ]
                v = 6.0 * planes[2] + 4.0 * (planes[1] + planes[3]) + (planes[0] + planes[4])
                ref[tile, k] = v * (weight * inside_y if tile else weight)
        return 0

    lax.fori_loop(0, 22, plane_x, 0)

    def plane_h(k, _):
        for tile in range(2):
            v, other = s_ref[tile, k + 1], s_ref[1 - tile, k + 1]
            grad_x = s_ref[tile, k + 2] - s_ref[tile, k]
            grad_y = y_next(v, other, lane) - y_prev(v, other, lane)
            grad_z = z_next(v, row) - z_prev(v, row)
            denom = 0.01 + grad_x * grad_x + grad_y * grad_y + grad_z * grad_z
            scale = lax.rsqrt(denom)
            scale = scale * (1.5 - 0.5 * denom * scale * scale)
            change = c_ref[tile, k + 1] * scale
            h_ref[3, tile, k] = change
            for c, grad in enumerate((grad_x, grad_y, grad_z)):
                h = grad * scale
                h_ref[c, tile, k] = h
                u_ref[c, tile, k] = -h * change
        return 0

    lax.fori_loop(0, 20, plane_h, 0)

    def step(ref, k, k_h, tile):
        means, common = [], h_ref[3, tile, k_h]
        for c in range(3):
            v, other = ref[c, tile, k], ref[c, 1 - tile, k]
            total = ref[c, tile, k - 1] + ref[c, tile, k + 1]
            total = total + (y_next(v, other, lane) + y_prev(v, other, lane))
            total = total + (z_next(v, row) + z_prev(v, row))
            means.append(total * (1.0 / 6.0))
            common = common + h_ref[c, tile, k_h] * means[c]
        return [mean - h_ref[c, tile, k_h] * common for c, mean in enumerate(means)]

    def plane_v(k, _):
        weight = inside_x(k - 1)
        for tile in range(2):
            for c, value in enumerate(step(u_ref, k + 1, k + 1, tile)):
                v_ref[c, tile, k] = value * (weight * inside_y if tile else weight)
        return 0

    lax.fori_loop(0, 18, plane_v, 0)

    for x in range(WX):
        for c, value in enumerate(step(v_ref, x + 1, x + 2, 0)):
            out[c, pl.ds(x, NZ, stride=WX), :] = value


def whole(count):
    return [pl.BlockSpec(memory_space=pltpu.VMEM)] * count


def on_device(frames, trailing):
    own = frames[0]
    n_ta, n_gx, n_gy = (lax.axis_size(a) for a in ("ta", "gx", "gy"))

    def passed(value, axis, step):
        count = lax.axis_size(axis)
        pairs = [(i, i + step) for i in range(count) if 0 <= i + step < count]
        return lax.ppermute(value, axis, pairs)

    arriving = passed(own, "ta", -1)
    nxt = jnp.where(lax.axis_index("ta") == n_ta - 1, trailing, arriving)
    low = passed(jnp.stack([own[:, WX - EDGE :], nxt[:, WX - EDGE :]]), "gx", 1)
    high = passed(jnp.stack([own[:, :EDGE], nxt[:, :EDGE]]), "gx", -1)
    message = jax.ShapeDtypeStruct((128, 128), BF16)
    to_right, to_left = pl.pallas_call(
        pack_kernel, out_shape=(message, message), in_specs=whole(4), out_specs=tuple(whole(2)), name="pack"
    )(own, nxt, low, high)
    from_left, from_right = passed(to_right, "gy", 1), passed(to_left, "gy", -1)
    plane = (NZ, LANES)
    flow = pl.pallas_call(
        flow_kernel,
        out_shape=jax.ShapeDtypeStruct((3, NZ * WX, LANES), F32),
        in_specs=whole(6),
        out_specs=whole(1)[0],
        scratch_shapes=[
            pltpu.VMEM((2, 32 * NZ, LANES), F32),
            pltpu.VMEM((2, 32 * NZ, LANES), F32),
            pltpu.VMEM((2, 22) + plane, F32),
            pltpu.VMEM((2, 22) + plane, F32),
            pltpu.VMEM((4, 2, 20) + plane, F32),
            pltpu.VMEM((3, 2, 20) + plane, F32),
            pltpu.VMEM((3, 2, 18) + plane, F32),
        ],
        name="flow",
    )(own, nxt, low, high, from_left, from_right)
    return flow.reshape(1, 3, NZ, WX, LANES)


def solution(mesh):
    return jax.shard_map(
        on_device,
        mesh=mesh,
        in_specs=(P("ta", None, "gx", "gy"), P(None, "gx", "gy")),
        out_specs=P("ta", None, None, "gx", "gy"),
        check_vma=False,
    )
```

time: 142 us -> 53.3 us (0.38)
  starting transfers between devices: 65.4 us -> 14.3 us
  waiting for transfers between devices: 42.2 us -> 22.2 us
  other arithmetic: 18.1 us -> 0.05 us
  Pallas kernels: 0 us -> 13.5 us
  local copies, waits for them, and re-layouts: 14.9 us -> 2.82 us
    ppermute x25 -> x5, starting transfers between devices: 65.4 us -> 14.3 us  [passed(): return lax.ppermute(value, axis, pairs)]
    ppermute x25 -> x5, waiting for transfers between devices: 42.2 us -> 22.2 us  [passed(): return lax.ppermute(value, axis, pairs)]
    pallas_call x0 -> x2, Pallas kernels: none -> 13.5 us  [the longest x1 11.4 us: on_device(): pl.pallas_call(flow_kernel, out_shape=jax.ShapeDtypeStruct((3, NZ * WX, L...]
    slice x17 -> x0, local copies, waits for them, and re-layouts: 7.81 us -> none  [the longest x14 6.89 us: padded_2(): lax.slice_in_dim(block, block.shape[dim] - width, None, axis=dim)]
    concatenate x12 -> x0, other arithmetic: 7.02 us -> none  [padded_2(): block = jnp.concatenate([low, block, high], axis=dim)]
    ppermute x4 -> x0, local copies, waits for them, and re-layouts: 5.53 us -> none  [the longest x2 4.53 us: padded_2(): lax.ppermute(lax.slice_in_dim(block, 0, width, axis=dim), axis, backward)]
    reduce_sum x3 -> x0, other arithmetic: 2.86 us -> none  [the longest x2 2.76 us: on_device(): jnp.sum(local_grad * mean_flow, axis=0) + crop_rim(change, trim_by)]
    div x3 -> x0, other arithmetic: 2.82 us -> none  [on_device(): (jnp.sum(local_grad * mean_flow, axis=0) + crop_rim(change, trim_by)) / c...]
  transfers between devices with their start and end apart: 25 -> 5, of which waited for: 13 -> 3; matrix products, arithmetic and copies ran while one was open for 2% -> 2% of each run, Pallas kernels for 0% -> 0%
where the time goes in v1:
time: 53.3 us; the launch traced here: 53 us
  waiting for transfers between devices  22.2 us (42%)
  starting transfers between devices  14.3 us (27%)
  Pallas kernels  13.5 us (25%)
  local copies, waits for them, and re-layouts  2.82 us (5%)
    ppermute x5, waiting for transfers between devices, passed(): return lax.ppermute(value, axis, pairs)  22.2 us
    ppermute x5, starting transfers between devices, passed(): return lax.ppermute(value, axis, pairs)  14.3 us
    pallas_call x1, Pallas kernels, on_device(): pl.pallas_call(flow_kernel, out_shape=jax.ShapeDtypeStruct((3, NZ * WX, L...  11.4 us
    pallas_call x1, Pallas kernels, on_device(): pl.pallas_call(pack_kernel, out_shape=(message, message), in_specs=whole(...  2.13 us
    unnamed x12, local copies, waits for them, and re-layouts  1.89 us
  transfers between devices with their start and end apart: 5, of which 3 were waited for; matrix products, arithmetic and copies ran while one was open for 2% of the time, Pallas kernels for 0%

profile of v1, /device:TPU:31, one launch (start us, length us, event | category | flops | bytes accessed | tf_op | source)
XLA Modules:
  0.0 53.0 jit_solution(11169543816791667946)
XLA Ops:
  0.0 2.4 %collective-permute-start = (bf16[32,16,128]{2,1,0:T(8,128)(2,1)}, bf16[32,16,128]{2,1,0:T(8,128)(2,1)S(1)}, u32[]{:S(2)}, u32[]{:S(2)}) collective-permute-start(bf16[32,16,128]{2,1,0:T(8,128)(2,1)} %bitcast.10), channel_id=1, source_target_pairs={{64,0},{128,64},{192,128},{256,192},{320,256},{384,320},{448,384},... | collective-permute-start | bytes 393224 | tf_op jit(solution)/shard_map/ppermute | solution.py:193
  2.5 0.0 copy-start.3
  2.5 0.9 %slice_bitcast_fusion.1 = (bf16[1,32,8,128]{3,2,1,0:T(8,128)(2,1)S(1)}, bf16[1,32,8,128]{3,2,1,0:T(8,128)(2,1)S(1)}) fusion(bf16[32,16,128]{2,1,0:T(8,128)(2,1)} %bitcast.11), kind=kLoop, calls=%fused_computation.4 | loop fusion | bytes 262144 | tf_op jit(solution)/shard_map/stack | solution.py:198
  3.4 10.6 %collective-permute-done = bf16[32,16,128]{2,1,0:T(8,128)(2,1)S(1)} collective-permute-done((bf16[32,16,128]{2,1,0:T(8,128)(2,1)}, bf16[32,16,128]{2,1,0:T(8,128)(2,1)S(1)}, u32[]{:S(2)}, u32[]{:S(2)}) %collective-permute-start) | collective-permute-done | bytes 131104 | tf_op jit(solution)/shard_map/ppermute | solution.py:193
  13.9 0.0 copy-done.3
  14.0 0.0 copy-start
  14.0 0.6 %copy-done = bf16[32,16,128]{2,1,0:T(8,128)(2,1)} copy-done((bf16[32,16,128]{2,1,0:T(8,128)(2,1)}, bf16[32,16,128]{2,1,0:T(8,128)(2,1)S(1)}, u32[]{:S(2)}) %copy-start) | copy-done | bytes 131096
  14.6 5.7 %collective-permute-start.1 = (bf16[2,32,8,128]{3,2,1,0:T(8,128)(2,1)S(1)}, bf16[2,32,8,128]{3,2,1,0:T(8,128)(2,1)S(1)}, u32[]{:S(2)}, u32[]{:S(2)}) collective-permute-start(bf16[2,32,8,128]{3,2,1,0:T(8,128)(2,1)S(1)} %pad_maximum_fusion), channel_id=1, source_target_pairs={{0,4},{4,8},{8,12},{12,16},{16,20},{20,24},{24,28},{28,32},{32,36}... | collective-permute-start | bytes 393224 | tf_op jit(solution)/shard_map/ppermute | solution.py:193
  20.3 1.9 %collective-permute-start.2 = (bf16[2,32,8,128]{3,2,1,0:T(8,128)(2,1)S(1)}, bf16[2,32,8,128]{3,2,1,0:T(8,128)(2,1)S(1)}, u32[]{:S(2)}, u32[]{:S(2)}) collective-permute-start(bf16[2,32,8,128]{3,2,1,0:T(8,128)(2,1)S(1)} %pad_maximum_fusion.1), channel_id=1, source_target_pairs={{4,0},{8,4},{12,8},{16,12},{20,16},{24,20},{28,24},{32,28},{36,32}... | collective-permute-start | bytes 393224 | tf_op jit(solution)/shard_map/ppermute | solution.py:193
  22.2 0.0 collective-permute-done.1.low
  22.3 0.0 copy-start.1
  22.3 5.5 %collective-permute-done.2.high = bf16[2,32,8,128]{3,2,1,0:T(8,128)(2,1)S(1)} collective-permute-done((bf16[2,32,8,128]{3,2,1,0:T(8,128)(2,1)S(1)}, bf16[2,32,8,128]{3,2,1,0:T(8,128)(2,1)S(1)}, u32[]{:S(2)}, u32[]{:S(2)}) %collective-permute-start.2) | collective-permute-done | bytes 131104 | tf_op jit(solution)/shard_map/ppermute | solution.py:193
  27.8 0.0 copy-done.1
  27.8 0.0 copy-start.2
  27.8 0.6 %copy-done.2 = bf16[2,32,8,128]{3,2,1,0:T(8,128)(2,1)} copy-done((bf16[2,32,8,128]{3,2,1,0:T(8,128)(2,1)}, bf16[2,32,8,128]{3,2,1,0:T(8,128)(2,1)S(1)}, u32[]{:S(2)}) %copy-start.2) | copy-done | bytes 131096
  28.5 2.1 %pack.1 = (bf16[128,128]{1,0:T(8,128)(2,1)}, bf16[128,128]{1,0:T(8,128)(2,1)}) custom-call(bf16[32,16,128]{2,1,0:T(8,128)(2,1)} %bitcast.12, bf16[32,16,128]{2,1,0:T(8,128)(2,1)} %copy-done, bf16[2,32,8,128]{3,2,1,0:T(8,128)(2,1)} %copy-done.1, bf16[2,32,8,128]{3,2,1,0:T(8,128)(2,1)} %copy-done.2), custom_call_target="tpu_custom_call" | custom-call | tf_op jit(solution)/shard_map/pack/pallas_call | solution.py:200
  30.6 3.0 %collective-permute-start.3 = (bf16[128,128]{1,0:T(8,128)(2,1)}, bf16[128,128]{1,0:T(8,128)(2,1)S(1)}, u32[]{:S(2)}, u32[]{:S(2)}) collective-permute-start(bf16[128,128]{1,0:T(8,128)(2,1)} %get-tuple-element.7), channel_id=1, source_target_pairs={{0,1},{1,2},{2,3},{4,5},{5,6},{6,7},{8,9},{9,10},{10,11},{12,13},{... | collective-permute-start | bytes 98312 | tf_op jit(solution)/shard_map/ppermute | solution.py:193
  33.6 1.3 %collective-permute-start.4 = (bf16[128,128]{1,0:T(8,128)(2,1)}, bf16[128,128]{1,0:T(8,128)(2,1)S(1)}, u32[]{:S(2)}, u32[]{:S(2)}) collective-permute-start(bf16[128,128]{1,0:T(8,128)(2,1)} %get-tuple-element.8), channel_id=1, source_target_pairs={{1,0},{2,1},{3,2},{5,4},{6,5},{7,6},{9,8},{10,9},{11,10},{13,12},{... | collective-permute-start | bytes 98312 | tf_op jit(solution)/shard_map/ppermute | solution.py:193
  34.9 0.0 collective-permute-done.3.from_left
  34.9 0.0 copy-start.4
  34.9 6.1 %collective-permute-done.4.from_right = bf16[128,128]{1,0:T(8,128)(2,1)S(1)} collective-permute-done((bf16[128,128]{1,0:T(8,128)(2,1)}, bf16[128,128]{1,0:T(8,128)(2,1)S(1)}, u32[]{:S(2)}, u32[]{:S(2)}) %collective-permute-start.4) | collective-permute-done | bytes 32800 | tf_op jit(solution)/shard_map/ppermute | solution.py:193
  41.0 0.0 copy-done.4
  41.0 0.6 %copy-done.5 = bf16[128,128]{1,0:T(8,128)(2,1)} copy-done((bf16[128,128]{1,0:T(8,128)(2,1)}, bf16[128,128]{1,0:T(8,128)(2,1)S(1)}, u32[]{:S(2)}) %copy-start.5) | copy-done | bytes 32792
  41.6 11.4 %flow.1 = f32[3,512,128]{2,1,0:T(8,128)} custom-call(bf16[32,16,128]{2,1,0:T(8,128)(2,1)} %bitcast.13, bf16[32,16,128]{2,1,0:T(8,128)(2,1)} %copy-done, bf16[2,32,8,128]{3,2,1,0:T(8,128)(2,1)} %copy-done.1, bf16[2,32,8,128]{3,2,1,0:T(8,128)(2,1)} %copy-done.2, bf16[128,128]{1,0:T(8,128)(2,1)} %copy-done.4, bf16[128,128]{1,0:T(8,128)(2,1)} %copy-done.5), custom_call_target="tpu_custom_call" | custom-call | tf_op jit(solution)/shard_map/flow/pallas_call | solution.py:205
  (5 shorter events, 0.1 us)
Async XLA Ops:
  0.0 13.9 %collective-permute-start = (bf16[32,16,128]{2,1,0:T(8,128)(2,1)}, bf16[32,16,128]{2,1,0:T(8,128)(2,1)S(1)}, u32[]{:S(2)}, u32[]{:S(2)}) collective-permute-start(bf16[32,16,128]{2,1,0:T(8,128)(2,1)} %bitcast.10), channel_id=1, source_target_pairs={{64,0},{128,64},{192,128},{256,192},{320,256},{384,320},{448,384},... | collective-permute-start | bytes 393224 | tf_op jit(solution)/shard_map/ppermute | solution.py:193
  2.5 11.5 %copy-start.3 = (bf16[32,16,128]{2,1,0:T(8,128)(2,1)S(1)}, bf16[32,16,128]{2,1,0:T(8,128)(2,1)}, u32[]{:S(2)}) copy-start(bf16[32,16,128]{2,1,0:T(8,128)(2,1)} %param.3) | copy-start | bytes 393220
  14.0 0.7 %copy-start = (bf16[32,16,128]{2,1,0:T(8,128)(2,1)}, bf16[32,16,128]{2,1,0:T(8,128)(2,1)S(1)}, u32[]{:S(2)}) copy-start(bf16[32,16,128]{2,1,0:T(8,128)(2,1)S(1)} %broadcast_select_fusion.nxt) | copy-start | bytes 393220
  14.6 7.6 %collective-permute-start.1 = (bf16[2,32,8,128]{3,2,1,0:T(8,128)(2,1)S(1)}, bf16[2,32,8,128]{3,2,1,0:T(8,128)(2,1)S(1)}, u32[]{:S(2)}, u32[]{:S(2)}) collective-permute-start(bf16[2,32,8,128]{3,2,1,0:T(8,128)(2,1)S(1)} %pad_maximum_fusion), channel_id=1, source_target_pairs={{0,4},{4,8},{8,12},{12,16},{16,20},{20,24},{24,28},{28,32},{32,36}... | collective-permute-start | bytes 393224 | tf_op jit(solution)/shard_map/ppermute | solution.py:193
  20.3 7.5 %collective-permute-start.2 = (bf16[2,32,8,128]{3,2,1,0:T(8,128)(2,1)S(1)}, bf16[2,32,8,128]{3,2,1,0:T(8,128)(2,1)S(1)}, u32[]{:S(2)}, u32[]{:S(2)}) collective-permute-start(bf16[2,32,8,128]{3,2,1,0:T(8,128)(2,1)S(1)} %pad_maximum_fusion.1), channel_id=1, source_target_pairs={{4,0},{8,4},{12,8},{16,12},{20,16},{24,20},{28,24},{32,28},{36,32}... | collective-permute-start | bytes 393224 | tf_op jit(solution)/shard_map/ppermute | solution.py:193
  22.3 5.6 %copy-start.1 = (bf16[2,32,8,128]{3,2,1,0:T(8,128)(2,1)}, bf16[2,32,8,128]{3,2,1,0:T(8,128)(2,1)S(1)}, u32[]{:S(2)}) copy-start(bf16[2,32,8,128]{3,2,1,0:T(8,128)(2,1)S(1)} %collective-permute-done.1.low) | copy-start | bytes 393220
  27.8 0.7 %copy-start.2 = (bf16[2,32,8,128]{3,2,1,0:T(8,128)(2,1)}, bf16[2,32,8,128]{3,2,1,0:T(8,128)(2,1)S(1)}, u32[]{:S(2)}) copy-start(bf16[2,32,8,128]{3,2,1,0:T(8,128)(2,1)S(1)} %collective-permute-done.2.high) | copy-start | bytes 393220
  30.6 4.3 %collective-permute-start.3 = (bf16[128,128]{1,0:T(8,128)(2,1)}, bf16[128,128]{1,0:T(8,128)(2,1)S(1)}, u32[]{:S(2)}, u32[]{:S(2)}) collective-permute-start(bf16[128,128]{1,0:T(8,128)(2,1)} %get-tuple-element.7), channel_id=1, source_target_pairs={{0,1},{1,2},{2,3},{4,5},{5,6},{6,7},{8,9},{9,10},{10,11},{12,13},{... | collective-permute-start | bytes 98312 | tf_op jit(solution)/shard_map/ppermute | solution.py:193
  33.6 7.4 %collective-permute-start.4 = (bf16[128,128]{1,0:T(8,128)(2,1)}, bf16[128,128]{1,0:T(8,128)(2,1)S(1)}, u32[]{:S(2)}, u32[]{:S(2)}) collective-permute-start(bf16[128,128]{1,0:T(8,128)(2,1)} %get-tuple-element.8), channel_id=1, source_target_pairs={{1,0},{2,1},{3,2},{5,4},{6,5},{7,6},{9,8},{10,9},{11,10},{13,12},{... | collective-permute-start | bytes 98312 | tf_op jit(solution)/shard_map/ppermute | solution.py:193
  34.9 6.1 %copy-start.4 = (bf16[128,128]{1,0:T(8,128)(2,1)}, bf16[128,128]{1,0:T(8,128)(2,1)S(1)}, u32[]{:S(2)}) copy-start(bf16[128,128]{1,0:T(8,128)(2,1)S(1)} %collective-permute-done.3.from_left) | copy-start | bytes 98308
  41.0 0.6 %copy-start.5 = (bf16[128,128]{1,0:T(8,128)(2,1)}, bf16[128,128]{1,0:T(8,128)(2,1)S(1)}, u32[]{:S(2)}) copy-start(bf16[128,128]{1,0:T(8,128)(2,1)S(1)} %collective-permute-done.4.from_right) | copy-start | bytes 98308

commit v2 on v0

v2 whole, which is shorter than its diff:
```python
import jax
import jax.numpy as jnp
from jax import lax
from jax.experimental import pallas as pl
from jax.experimental.pallas import tpu as pltpu
from jax.sharding import PartitionSpec as P

NZ = 32
WX = 16
WY = 128
EDGE = 8
PITCH = 40
F32, BF16 = jnp.float32, jnp.bfloat16


def iota(shape, dim):
    return lax.broadcasted_iota(jnp.int32, shape, dim)


def dot(a, b):
    return jnp.dot(a, b, preferred_element_type=F32)


def y_taps(distance):
    d = jnp.abs(distance)
    tap = jnp.where(d == 0, 6.0, jnp.where(d == 1, 4.0, jnp.where(d == 2, 1.0, 0.0)))
    return tap * (1.0 / 4096.0)


def octet_rows(source, z_half):
    return source[16 * z_half : 16 * z_half + 16].astype(F32).reshape(128, WY).astype(BF16)


def strip_column(lane):
    place = lane & 31
    return jnp.where(place < 16, place - 5, place + 101)


def edge_columns(blocks):
    row, lane = iota((WY, 256), 0), iota((WY, 256), 1)
    column = (lane & 7) + jnp.where(lane < 128, WY - EDGE, 0)
    pick = jnp.where(row == column, 1.0, 0.0).astype(BF16)
    group = (iota((128, 256), 1) & 127) >> 3
    packed = jnp.zeros((128, 256), F32)
    for (octet, frame), block in blocks.items():
        for z_half in range(2):
            found = dot(octet_rows(block, z_half), pick)
            packed = jnp.where(group == (octet * 2 + frame) * 2 + z_half, found, packed)
    return packed.astype(BF16)


def pack_own_kernel(own, nxt, packed):
    packed[...] = edge_columns(
        {
            (octet, frame): block[:, 8 * octet - 8 : 8 * octet, :]
            for octet in (1, 2)
            for frame, block in enumerate((own, nxt))
        }
    )


def pack_rim_kernel(low, high, packed, to_right, to_left):
    rim = edge_columns(
        {(octet, frame): block[frame] for octet, block in ((0, low), (3, high)) for frame in range(2)}
    )
    both = packed[...] + rim
    to_right[...] = both[:, :128]
    to_left[...] = both[:, 128:]


class Planes:
    def __init__(self, ref, index=None):
        self.ref, self.index = ref, index

    def rows(self, start, count, stride=None):
        rows = pl.ds(start, count) if stride is None else pl.ds(start, count, stride=stride)
        return (rows, slice(None)) if self.index is None else (self.index, rows, slice(None))

    def get(self, plane, shift=0):
        return self.ref[self.rows(8 + PITCH * plane + shift, NZ)]

    def put(self, plane, value):
        self.ref[self.rows(8 + PITCH * plane, NZ)] = value

    def put_z(self, plane, z, values):
        self.ref[self.rows(8 + PITCH * plane + z, values.shape[0], PITCH)] = values

    def clear(self, first, last):
        for plane in range(first, last + 2):
            self.ref[self.rows(PITCH * plane, 8)] = jnp.zeros((8, WY), F32)


def planes_of(count):
    return pltpu.VMEM((8 + PITCH * count, WY), F32)


def planes_of_3(count):
    return pltpu.VMEM((3, 8 + PITCH * count, WY), F32)


def smooth_z(planes, k):
    near = planes.get(k, 1) + planes.get(k, -1)
    far = planes.get(k, 2) + planes.get(k, -2)
    return 6.0 * planes.get(k) + 4.0 * near + far


def smooth_x(planes, k):
    near = planes.get(k + 1) + planes.get(k - 1)
    far = planes.get(k + 2) + planes.get(k - 2)
    return 6.0 * planes.get(k) + 4.0 * near + far


def y_pair(v):
    return pltpu.roll(v, WY - 1, 1), pltpu.roll(v, 1, 1)


def gradient_terms(s, k, change):
    y_next, y_prev = y_pair(s.get(k))
    grads = (s.get(k + 1) - s.get(k - 1), y_next - y_prev, s.get(k, 1) - s.get(k, -1))
    denom = 0.01 + grads[0] * grads[0] + grads[1] * grads[1] + grads[2] * grads[2]
    scale = lax.rsqrt(denom)
    scale = scale * (1.5 - 0.5 * denom * scale * scale)
    return [grad * scale for grad in grads], change * scale


def jacobi(velocity, k, terms):
    means = []
    for planes in velocity:
        y_next, y_prev = y_pair(planes.get(k))
        total = (planes.get(k + 1) + planes.get(k - 1)) + (y_next + y_prev)
        total = total + (planes.get(k, 1) + planes.get(k, -1))
        means.append(total * (1.0 / 6.0))
    common = terms[3] + terms[0] * means[0] + terms[1] * means[1] + terms[2] * means[2]
    return [mean - term * common for mean, term in zip(means, terms)]


def inside():
    faces = []
    for axis in ("gx", "gy"):
        at = lax.axis_index(axis)
        faces += [jnp.where(at == 0, 0.0, 1.0), jnp.where(at == lax.axis_size(axis) - 1, 0.0, 1.0)]
    return faces


def inner_kernel(own, nxt, low, high, inner, part, edge_taps, p_ref, q_ref, s_ref, c_ref, h_ref, u_ref, v_ref):
    x_low, x_high, _, _ = inside()

    def weight(x):
        return x_low if x < 0 else x_high if x >= WX else None

    def weighed(value, x):
        return value if weight(x) is None else value * weight(x)

    p, q, s = Planes(p_ref), Planes(q_ref), Planes(s_ref)
    u, v = [Planes(u_ref, c) for c in range(3)], [Planes(v_ref, c) for c in range(3)]
    p.clear(3, 28)
    q.clear(3, 28)
    s.clear(1, 20)
    for c in range(3):
        u[c].clear(1, 18)
        v[c].clear(1, 16)

    row, lane = iota((WY, WY), 0), iota((WY, WY), 1)
    taps = y_taps(lane - row).astype(BF16)
    strip_taps = y_taps(strip_column(lane) - row)
    octet_taps = jnp.concatenate(
        [jnp.where((lane >> 5) == octet, strip_taps, 0.0) for octet in range(4)], axis=0
    ).astype(BF16)

    row, lane = iota((256, WY), 0), iota((256, WY), 1)
    column = (row & 7) + jnp.where(row < 128, -EDGE, WY)
    edge = jnp.where(((row & 127) >> 5) == (lane >> 5), y_taps(strip_column(lane) - column), 0.0)
    for group in range(4):
        edge_taps[group] = jnp.where(((row >> 3) & 3) == group, edge, 0.0).astype(BF16)

    for z_half in range(2):
        octets = [[], []]
        for octet in range(4):
            found = []
            for frame, centre in enumerate((own, nxt)):
                block = (
                    (low if octet == 0 else high)[frame, 16 * z_half : 16 * z_half + 16]
                    if octet in (0, 3)
                    else centre[16 * z_half : 16 * z_half + 16, 8 * octet - 8 : 8 * octet, :]
                )
                rows = block.astype(F32).reshape(128, WY).astype(BF16)
                octets[frame].append(rows)
                found.append(dot(rows, taps))
            total, change = (found[0] + found[1]) * 0.25, found[1] - found[0]
            for i in range(16):
                p.put_z(8 * octet, 16 * z_half + i, total[8 * i : 8 * i + 8])
                q.put_z(8 * octet, 16 * z_half + i, change[8 * i : 8 * i + 8])
        for frame in range(2):
            part[frame, z_half] = dot(jnp.concatenate(octets[frame], axis=1), octet_taps)

    for k in range(3, 29):
        p.put(k, smooth_z(p, k))
        q.put(k, smooth_z(q, k))
    for k in range(22):
        s.put(k, weighed(smooth_x(p, k + 5), k - 3))
        if 1 <= k <= 20:
            c_ref[k - 1] = weighed(smooth_x(q, k + 5), k - 3)

    for k in range(20):
        terms, change = gradient_terms(s, k + 1, c_ref[k])
        h_ref[3, k] = change
        for c in range(3):
            h_ref[c, k] = terms[c]
            u[c].put(k, -terms[c] * change)

    for k in range(18):
        for c, value in enumerate(jacobi(u, k + 1, [h_ref[c, k + 1] for c in range(4)])):
            v[c].put(k, weighed(value, k - 1))
    for x in range(WX):
        for c, value in enumerate(jacobi(v, x + 1, [h_ref[c, x + 2] for c in range(4)])):
            inner[c, x] = value


def strip_kernel(inner, part, edge_taps, from_left, from_right, out, p_ref, q_ref, s_ref, c_ref, h_ref, u_ref, v_ref):
    x_low, x_high, y_low, y_high = inside()
    lane = iota((1, WY), 1)
    column = strip_column(lane)
    weight = (
        jnp.where(lane < 32, x_low, 1.0)
        * jnp.where(lane >= 96, x_high, 1.0)
        * jnp.where(column < 0, y_low, 1.0)
        * jnp.where(column >= WY, y_high, 1.0)
    )
    p, q, s = Planes(p_ref), Planes(q_ref), Planes(s_ref)
    u, v = [Planes(u_ref, c) for c in range(3)], [Planes(v_ref, c) for c in range(3)]
    for planes, first in [(p, 2), (q, 2), (s, 1)] + [(planes, 1) for planes in u + v]:
        planes.clear(first, first + 7)

    def put(planes, i, value, rim):
        planes.put(i + rim, value)
        if i < rim:
            planes.put(i + rim + 8, pltpu.roll(value, 96, 1))
        if i >= 8 - rim:
            planes.put(i + rim - 8, pltpu.roll(value, 32, 1))

    edges = jnp.concatenate([from_left[...], from_right[...]], axis=1)
    for z_half in range(2):
        found = [part[frame, z_half] + dot(edges, edge_taps[2 * frame + z_half]) for frame in range(2)]
        total, change = (found[0] + found[1]) * 0.25, found[1] - found[0]
        for i in range(16):
            p.put_z(2, 16 * z_half + i, total[8 * i : 8 * i + 8])
            q.put_z(2, 16 * z_half + i, change[8 * i : 8 * i + 8])
    for i in range(8):
        put(p, i, smooth_z(p, i + 2), 2)
        put(q, i, smooth_z(q, i + 2), 2)
    for i in range(8):
        put(s, i, smooth_x(p, i + 2) * weight, 1)
        c_ref[i] = smooth_x(q, i + 2) * weight
    for i in range(8):
        terms, change = gradient_terms(s, i + 1, c_ref[i])
        h_ref[3, i] = change
        for c in range(3):
            h_ref[c, i] = terms[c]
            put(u[c], i, -terms[c] * change, 1)
    for i in range(8):
        for c, value in enumerate(jacobi(u, i + 1, [h_ref[c, i] for c in range(4)])):
            put(v[c], i, value * weight, 1)
    own_lane = iota((NZ, WY), 1)
    rim = (own_lane < 5) | (own_lane >= WY - 5)
    for i in range(8):
        for c, value in enumerate(jacobi(v, i + 1, [h_ref[c, i] for c in range(4)])):
            value = jnp.where((own_lane & 31) < 5, pltpu.roll(value, WY - 22, 1), value)
            for half in range(2):
                x = 8 * half + i
                placed = pltpu.roll(value, WY - 32 * (half + 1) - 5, 1)
                out[c, pl.ds(x, NZ, stride=WX), :] = jnp.where(rim, placed, inner[c, x])


def call(kernel, outs, args, scratch, megabytes, flops, name):
    moved = sum(a.size * a.dtype.itemsize for a in (*args, *outs))
    spec = pl.BlockSpec(memory_space=pltpu.VMEM)
    return pl.pallas_call(
        kernel,
        out_shape=outs,
        in_specs=[spec] * len(args),
        out_specs=tuple([spec] * len(outs)),
        scratch_shapes=scratch,
        compiler_params=pltpu.CompilerParams(vmem_limit_bytes=megabytes << 20),
        cost_estimate=pl.CostEstimate(flops=flops, bytes_accessed=moved, transcendentals=0),
        name=name,
    )(*args)


def shape(*dims, dtype=F32):
    return jax.ShapeDtypeStruct(dims, dtype)


def on_device(frames, trailing):
    own = frames[0]

    def passed(value, axis, step):
        count = lax.axis_size(axis)
        pairs = [(i, i + step) for i in range(count) if 0 <= i + step < count]
        return lax.ppermute(value, axis, pairs)

    arriving = passed(own, "ta", -1)
    nxt = jnp.where(lax.axis_index("ta") == lax.axis_size("ta") - 1, trailing, arriving)
    low = passed(jnp.stack([own[:, WX - EDGE :], nxt[:, WX - EDGE :]]), "gx", 1)
    high = passed(jnp.stack([own[:, :EDGE], nxt[:, :EDGE]]), "gx", -1)
    (packed,) = call(
        pack_own_kernel, (shape(128, 256, dtype=BF16),), (own, nxt), [], 8, 10**8, "pack_own"
    )
    message = shape(128, 128, dtype=BF16)
    to_right, to_left = call(
        pack_rim_kernel, (message, message), (low, high, packed), [], 8, 10**8, "pack_rim"
    )
    from_left, from_right = passed(to_right, "gy", 1), passed(to_left, "gy", -1)
    inner, part, edge_taps = call(
        inner_kernel,
        (shape(3, WX, NZ, WY), shape(2, 2, 128, WY), shape(4, 256, WY, dtype=BF16)),
        (own, nxt, low, high),
        [
            planes_of(32),
            planes_of(32),
            planes_of(22),
            pltpu.VMEM((20, NZ, WY), F32),
            pltpu.VMEM((4, 20, NZ, WY), F32),
            planes_of_3(20),
            planes_of_3(18),
        ],
        16,
        10**9,
        "inner",
    )
    (flow,) = call(
        strip_kernel,
        (shape(3, NZ * WX, WY),),
        (inner, part, edge_taps, from_left, from_right),
        [
            planes_of(12),
            planes_of(12),
            planes_of(10),
            pltpu.VMEM((8, NZ, WY), F32),
            pltpu.VMEM((4, 8, NZ, WY), F32),
            planes_of_3(10),
            planes_of_3(10),
        ],
        16,
        10**8,
        "strip",
    )
    return flow.reshape(1, 3, NZ, WX, WY)


def solution(mesh):
    return jax.shard_map(
        on_device,
        mesh=mesh,
        in_specs=(P("ta", None, "gx", "gy"), P(None, "gx", "gy")),
        out_specs=P("ta", None, None, "gx", "gy"),
        check_vma=False,
    )
```

time: 142 us -> 41.1 us (0.29)
  starting transfers between devices: 65.4 us -> 14.4 us
  waiting for transfers between devices: 42.2 us -> 19.7 us
  other arithmetic: 18.1 us -> 0.05 us
  local copies, waits for them, and re-layouts: 14.9 us -> 0.94 us
  Pallas kernels: 0 us -> 5.62 us
    ppermute x25 -> x5, starting transfers between devices: 65.4 us -> 14.4 us  [passed(): return lax.ppermute(value, axis, pairs)]
    ppermute x25 -> x5, waiting for transfers between devices: 42.2 us -> 19.7 us  [passed(): return lax.ppermute(value, axis, pairs)]
    slice x17 -> x0, local copies, waits for them, and re-layouts: 7.81 us -> none  [the longest x14 6.89 us: padded_2(): lax.slice_in_dim(block, block.shape[dim] - width, None, axis=dim)]
    concatenate x12 -> x0, other arithmetic: 7.02 us -> none  [padded_2(): block = jnp.concatenate([low, block, high], axis=dim)]
    pallas_call x0 -> x4, Pallas kernels: none -> 5.62 us  [call(): pl.pallas_call(kernel, out_shape=outs, in_specs=[spec] * len(args), out_s...]
    ppermute x4 -> x0, local copies, waits for them, and re-layouts: 5.53 us -> none  [the longest x2 4.53 us: padded_2(): lax.ppermute(lax.slice_in_dim(block, 0, width, axis=dim), axis, backward)]
    reduce_sum x3 -> x0, other arithmetic: 2.86 us -> none  [the longest x2 2.76 us: on_device(): jnp.sum(local_grad * mean_flow, axis=0) + crop_rim(change, trim_by)]
    div x3 -> x0, other arithmetic: 2.82 us -> none  [on_device(): (jnp.sum(local_grad * mean_flow, axis=0) + crop_rim(change, trim_by)) / c...]
  transfers between devices with their start and end apart: 25 -> 5, of which waited for: 13 -> 3; matrix products, arithmetic and copies ran while one was open for 2% -> 2% of each run, Pallas kernels for 0% -> 6%
where the time goes in v2:
time: 41.1 us; the launch traced here: 40.9 us
  waiting for transfers between devices  19.7 us (48%)
  starting transfers between devices  14.4 us (35%)
  Pallas kernels  5.62 us (14%)
  local copies, waits for them, and re-layouts  0.94 us (2%)
    ppermute x5, waiting for transfers between devices, passed(): return lax.ppermute(value, axis, pairs)  19.7 us
    ppermute x5, starting transfers between devices, passed(): return lax.ppermute(value, axis, pairs)  14.4 us
    pallas_call x4, Pallas kernels, call(): pl.pallas_call(kernel, out_shape=outs, in_specs=[spec] * len(args), out_s...  5.62 us
    another operation x2, local copies, waits for them, and re-layouts, on_device(): high = passed(jnp.stack([own[:, :EDGE], nxt[:, :EDGE]]), 'gx', -1)  0.93 us
  transfers between devices with their start and end apart: 5, of which 3 were waited for; matrix products, arithmetic and copies ran while one was open for 2% of the time, Pallas kernels for 6%

profile of v2, /device:TPU:31, one launch (start us, length us, event | category | flops | bytes accessed | tf_op | source)
XLA Modules:
  0.0 40.9 jit_solution(17322534510073022625)
XLA Ops:
  0.0 2.4 %collective-permute-start = (bf16[32,16,128]{2,1,0:T(8,128)(2,1)}, bf16[32,16,128]{2,1,0:T(8,128)(2,1)S(1)}, u32[]{:S(2)}, u32[]{:S(2)}) collective-permute-start(bf16[32,16,128]{2,1,0:T(8,128)(2,1)} %bitcast.10), channel_id=1, source_target_pairs={{64,0},{128,64},{192,128},{256,192},{320,256},{384,320},{448,384},... | collective-permute-start | bytes 393224 | tf_op jit(solution)/shard_map/ppermute | solution.py:299
  2.5 0.0 copy-start.1
  2.5 0.9 %slice_bitcast_fusion.1 = (bf16[1,32,8,128]{3,2,1,0:T(8,128)(2,1)S(1)}, bf16[1,32,8,128]{3,2,1,0:T(8,128)(2,1)S(1)}) fusion(bf16[32,16,128]{2,1,0:T(8,128)(2,1)} %bitcast.11), kind=kLoop, calls=%fused_computation.4 | loop fusion | bytes 262144 | tf_op jit(solution)/shard_map/stack | solution.py:304
  3.4 10.6 %collective-permute-done = bf16[32,16,128]{2,1,0:T(8,128)(2,1)S(1)} collective-permute-done((bf16[32,16,128]{2,1,0:T(8,128)(2,1)}, bf16[32,16,128]{2,1,0:T(8,128)(2,1)S(1)}, u32[]{:S(2)}, u32[]{:S(2)}) %collective-permute-start) | collective-permute-done | bytes 131104 | tf_op jit(solution)/shard_map/ppermute | solution.py:299
  13.9 0.0 copy-done.1
  14.0 5.7 %collective-permute-start.1 = (bf16[2,32,8,128]{3,2,1,0:T(8,128)(2,1)S(1)}, bf16[2,32,8,128]{3,2,1,0:T(8,128)(2,1)S(1)}, u32[]{:S(2)}, u32[]{:S(2)}) collective-permute-start(bf16[2,32,8,128]{3,2,1,0:T(8,128)(2,1)S(1)} %pad_maximum_fusion), channel_id=1, source_target_pairs={{0,4},{4,8},{8,12},{12,16},{16,20},{20,24},{24,28},{28,32},{32,36}... | collective-permute-start | bytes 393224 | tf_op jit(solution)/shard_map/ppermute | solution.py:299
  19.7 0.0 copy-start
  19.7 2.1 %collective-permute-start.2 = (bf16[2,32,8,128]{3,2,1,0:T(8,128)(2,1)S(1)}, bf16[2,32,8,128]{3,2,1,0:T(8,128)(2,1)S(1)}, u32[]{:S(2)}, u32[]{:S(2)}) collective-permute-start(bf16[2,32,8,128]{3,2,1,0:T(8,128)(2,1)S(1)} %pad_maximum_fusion.1), channel_id=1, source_target_pairs={{4,0},{8,4},{12,8},{16,12},{20,16},{24,20},{28,24},{32,28},{36,32}... | collective-permute-start | bytes 393224 | tf_op jit(solution)/shard_map/ppermute | solution.py:299
  21.8 0.0 copy-done
  21.8 0.3 pack_own.1.packed
  22.1 0.0 collective-permute-done.1.low
  22.1 5.3 %collective-permute-done.2.high = bf16[2,32,8,128]{3,2,1,0:T(8,128)(2,1)S(1)} collective-permute-done((bf16[2,32,8,128]{3,2,1,0:T(8,128)(2,1)S(1)}, bf16[2,32,8,128]{3,2,1,0:T(8,128)(2,1)S(1)}, u32[]{:S(2)}, u32[]{:S(2)}) %collective-permute-start.2) | collective-permute-done | bytes 131104 | tf_op jit(solution)/shard_map/ppermute | solution.py:299
  27.3 0.3 pack_rim.1
  27.6 3.0 %collective-permute-start.3 = (bf16[128,128]{1,0:T(8,128)(2,1)S(1)}, bf16[128,128]{1,0:T(8,128)(2,1)S(1)}, u32[]{:S(2)}, u32[]{:S(2)}) collective-permute-start(bf16[128,128]{1,0:T(8,128)(2,1)S(1)} %get-tuple-element.13), channel_id=1, source_target_pairs={{0,1},{1,2},{2,3},{4,5},{5,6},{6,7},{8,9},{9,10},{10,11},{12,13},{... | collective-permute-start | bytes 98312 | tf_op jit(solution)/shard_map/ppermute | solution.py:299
  30.6 1.3 %collective-permute-start.4 = (bf16[128,128]{1,0:T(8,128)(2,1)S(1)}, bf16[128,128]{1,0:T(8,128)(2,1)S(1)}, u32[]{:S(2)}, u32[]{:S(2)}) collective-permute-start(bf16[128,128]{1,0:T(8,128)(2,1)S(1)} %get-tuple-element.14), channel_id=1, source_target_pairs={{1,0},{2,1},{3,2},{5,4},{6,5},{7,6},{9,8},{10,9},{11,10},{13,12},{... | collective-permute-start | bytes 98312 | tf_op jit(solution)/shard_map/ppermute | solution.py:299
  31.9 2.0 %inner.1 = (f32[3,16,32,128]{3,2,1,0:T(8,128)S(1)}, f32[2,2,128,128]{3,2,1,0:T(8,128)S(1)}, bf16[4,256,128]{2,1,0:T(8,128)(2,1)S(1)}) custom-call(bf16[32,16,128]{2,1,0:T(8,128)(2,1)S(1)} %bitcast.13, bf16[32,16,128]{2,1,0:T(8,128)(2,1)S(1)} %broadcast_select_fusion.nxt, bf16[2,32,8,128]{3,2,1,0:T(8,128)(2,1)S(1)} %collective-permute-done.1.low, ...), custom_call_target="tpu_custom_call" | custom-call | flops 1000000000 | bytes 1835008 | tf_op jit(solution)/shard_map/inner/pallas_call | solution.py:277
  33.9 0.0 collective-permute-done.3.from_left
  34.0 3.9 %collective-permute-done.4.from_right = bf16[128,128]{1,0:T(8,128)(2,1)S(1)} collective-permute-done((bf16[128,128]{1,0:T(8,128)(2,1)S(1)}, bf16[128,128]{1,0:T(8,128)(2,1)S(1)}, u32[]{:S(2)}, u32[]{:S(2)}) %collective-permute-start.4) | collective-permute-done | bytes 32800 | tf_op jit(solution)/shard_map/ppermute | solution.py:299
  37.8 3.0 %strip.1 = f32[3,512,128]{2,1,0:T(8,128)} custom-call(f32[3,16,32,128]{3,2,1,0:T(8,128)S(1)} %get-tuple-element.10.inner, f32[2,2,128,128]{3,2,1,0:T(8,128)S(1)} %get-tuple-element.11.part, bf16[4,256,128]{2,1,0:T(8,128)(2,1)S(1)} %get-tuple-element.12.edge_taps, bf16[128,128]{1,0:T(8,128)(2,1)S(1)} %collective-permute-done.3.from_left, ...), custom_call_target="tpu_custom_call" | custom-call | flops 100000000 | bytes 2162688 | tf_op jit(solution)/shard_map/strip/pallas_call | solution.py:277
  (4 shorter events, 0.1 us)
Async XLA Ops:
  0.0 13.9 %collective-permute-start = (bf16[32,16,128]{2,1,0:T(8,128)(2,1)}, bf16[32,16,128]{2,1,0:T(8,128)(2,1)S(1)}, u32[]{:S(2)}, u32[]{:S(2)}) collective-permute-start(bf16[32,16,128]{2,1,0:T(8,128)(2,1)} %bitcast.10), channel_id=1, source_target_pairs={{64,0},{128,64},{192,128},{256,192},{320,256},{384,320},{448,384},... | collective-permute-start | bytes 393224 | tf_op jit(solution)/shard_map/ppermute | solution.py:299
  2.5 11.5 %copy-start.1 = (bf16[32,16,128]{2,1,0:T(8,128)(2,1)S(1)}, bf16[32,16,128]{2,1,0:T(8,128)(2,1)}, u32[]{:S(2)}) copy-start(bf16[32,16,128]{2,1,0:T(8,128)(2,1)} %param.3) | copy-start | bytes 393220
  14.0 8.1 %collective-permute-start.1 = (bf16[2,32,8,128]{3,2,1,0:T(8,128)(2,1)S(1)}, bf16[2,32,8,128]{3,2,1,0:T(8,128)(2,1)S(1)}, u32[]{:S(2)}, u32[]{:S(2)}) collective-permute-start(bf16[2,32,8,128]{3,2,1,0:T(8,128)(2,1)S(1)} %pad_maximum_fusion), channel_id=1, source_target_pairs={{0,4},{4,8},{8,12},{12,16},{16,20},{20,24},{24,28},{28,32},{32,36}... | collective-permute-start | bytes 393224 | tf_op jit(solution)/shard_map/ppermute | solution.py:299
  19.7 2.1 %copy-start = (bf16[1,32,16,128]{3,2,1,0:T(8,128)(2,1)S(1)}, bf16[1,32,16,128]{3,2,1,0:T(8,128)(2,1)}, u32[]{:S(2)}) copy-start(bf16[1,32,16,128]{3,2,1,0:T(8,128)(2,1)} %param.2) | copy-start | bytes 393220
  19.7 7.6 %collective-permute-start.2 = (bf16[2,32,8,128]{3,2,1,0:T(8,128)(2,1)S(1)}, bf16[2,32,8,128]{3,2,1,0:T(8,128)(2,1)S(1)}, u32[]{:S(2)}, u32[]{:S(2)}) collective-permute-start(bf16[2,32,8,128]{3,2,1,0:T(8,128)(2,1)S(1)} %pad_maximum_fusion.1), channel_id=1, source_target_pairs={{4,0},{8,4},{12,8},{16,12},{20,16},{24,20},{28,24},{32,28},{36,32}... | collective-permute-start | bytes 393224 | tf_op jit(solution)/shard_map/ppermute | solution.py:299
  27.6 6.3 %collective-permute-start.3 = (bf16[128,128]{1,0:T(8,128)(2,1)S(1)}, bf16[128,128]{1,0:T(8,128)(2,1)S(1)}, u32[]{:S(2)}, u32[]{:S(2)}) collective-permute-start(bf16[128,128]{1,0:T(8,128)(2,1)S(1)} %get-tuple-element.13), channel_id=1, source_target_pairs={{0,1},{1,2},{2,3},{4,5},{5,6},{6,7},{8,9},{9,10},{10,11},{12,13},{... | collective-permute-start | bytes 98312 | tf_op jit(solution)/shard_map/ppermute | solution.py:299
  30.6 7.2 %collective-permute-start.4 = (bf16[128,128]{1,0:T(8,128)(2,1)S(1)}, bf16[128,128]{1,0:T(8,128)(2,1)S(1)}, u32[]{:S(2)}, u32[]{:S(2)}) collective-permute-start(bf16[128,128]{1,0:T(8,128)(2,1)S(1)} %get-tuple-element.14), channel_id=1, source_target_pairs={{1,0},{2,1},{3,2},{5,4},{6,5},{7,6},{9,8},{10,9},{11,10},{13,12},{... | collective-permute-start | bytes 98312 | tf_op jit(solution)/shard_map/ppermute | solution.py:299

commit v3 on v2

--- a/solution.py
+++ b/solution.py
@@ -298,10 +298,17 @@
         pairs = [(i, i + step) for i in range(count) if 0 <= i + step < count]
         return lax.ppermute(value, axis, pairs)
 
+    def swapped(value, axis, first):
+        pairs = [(i, i + 1) for i in range(first, lax.axis_size(axis) - 1, 2)]
+        return lax.ppermute(value, axis, pairs + [(b, a) for a, b in pairs])
+
     arriving = passed(own, "ta", -1)
     nxt = jnp.where(lax.axis_index("ta") == lax.axis_size("ta") - 1, trailing, arriving)
-    low = passed(jnp.stack([own[:, WX - EDGE :], nxt[:, WX - EDGE :]]), "gx", 1)
-    high = passed(jnp.stack([own[:, :EDGE], nxt[:, :EDGE]]), "gx", -1)
+    upper, lower = jnp.stack([own[:, WX - EDGE :], nxt[:, WX - EDGE :]]), jnp.stack([own[:, :EDGE], nxt[:, :EDGE]])
+    even = lax.axis_index("gx") % 2 == 0
+    on_chip = swapped(jnp.where(even, upper, lower), "gx", 0)
+    off_chip = swapped(jnp.where(even, lower, upper), "gx", 1)
+    low, high = jnp.where(even, off_chip, on_chip), jnp.where(even, on_chip, off_chip)
     (packed,) = call(
         pack_own_kernel, (shape(128, 256, dtype=BF16),), (own, nxt), [], 8, 10**8, "pack_own"
     )

time: 41.1 us -> 39.2 us (0.954)
  the two profiles are of different devices: /device:TPU:31 before, /device:TPU:38 now
where the time goes in v3:
time: 39.2 us; the launch traced here: 39 us
  waiting for transfers between devices  20.4 us (52%)
  starting transfers between devices  11.8 us (30%)
  Pallas kernels  5.63 us (14%)
  local copies, waits for them, and re-layouts  0.94 us (2%)
    ppermute x3, waiting for transfers between devices, passed(): return lax.ppermute(value, axis, pairs)  15.7 us
    ppermute x3, starting transfers between devices, passed(): return lax.ppermute(value, axis, pairs)  7.3 us
    pallas_call x4, Pallas kernels, call(): pl.pallas_call(kernel, out_shape=outs, in_specs=[spec] * len(args), out_s...  5.63 us
    ppermute x2, waiting for transfers between devices, swapped(): return lax.ppermute(value, axis, pairs + [(b, a) for a, b in pairs])  4.72 us
    ppermute x2, starting transfers between devices, swapped(): return lax.ppermute(value, axis, pairs + [(b, a) for a, b in pairs])  4.51 us
    another operation x2, local copies, waits for them, and re-layouts, on_device(): jnp.stack([own[:, :EDGE], nxt[:, :EDGE]])  0.93 us
  transfers between devices with their start and end apart: 5, of which 3 were waited for; matrix products, arithmetic and copies ran while one was open for 2% of the time, Pallas kernels for 6%

profile of v3, /device:TPU:38, one launch (start us, length us, event | category | flops | bytes accessed | tf_op | source)
XLA Modules:
  0.0 39.0 jit_solution(14899049591051216321)
XLA Ops:
  0.0 2.7 %collective-permute-start = (bf16[32,16,128]{2,1,0:T(8,128)(2,1)}, bf16[32,16,128]{2,1,0:T(8,128)(2,1)S(1)}, u32[]{:S(2)}, u32[]{:S(2)}) collective-permute-start(bf16[32,16,128]{2,1,0:T(8,128)(2,1)} %bitcast.10), channel_id=1, source_target_pairs={{64,0},{128,64},{192,128},{256,192},{320,256},{384,320},{448,384},... | collective-permute-start | bytes 393224 | tf_op jit(solution)/shard_map/ppermute | solution.py:299
  2.8 0.0 copy-start.1
  2.8 0.9 %slice_bitcast_fusion.3 = (bf16[1,32,8,128]{3,2,1,0:T(8,128)(2,1)S(1)}, bf16[1,32,8,128]{3,2,1,0:T(8,128)(2,1)S(1)}) fusion(bf16[32,16,128]{2,1,0:T(8,128)(2,1)} %bitcast.11), kind=kLoop, calls=%fused_computation.10 | loop fusion | bytes 262144 | tf_op jit(solution)/shard_map/stack | solution.py:307
  3.7 10.9 %collective-permute-done = bf16[32,16,128]{2,1,0:T(8,128)(2,1)S(1)} collective-permute-done((bf16[32,16,128]{2,1,0:T(8,128)(2,1)}, bf16[32,16,128]{2,1,0:T(8,128)(2,1)S(1)}, u32[]{:S(2)}, u32[]{:S(2)}) %collective-permute-start) | collective-permute-done | bytes 131104 | tf_op jit(solution)/shard_map/ppermute | solution.py:299
  14.6 0.0 copy-done.1
  14.7 0.0 copy-start
  14.7 2.1 %collective-permute-start.2 = (bf16[2,32,8,128]{3,2,1,0:T(8,128)(2,1)S(1)}, bf16[2,32,8,128]{3,2,1,0:T(8,128)(2,1)S(1)}, u32[]{:S(2)}, u32[]{:S(2)}) collective-permute-start(bf16[2,32,8,128]{3,2,1,0:T(8,128)(2,1)S(1)} %get-tuple-element.17), channel_id=1, source_target_pairs={{0,4},{8,12},{16,20},{24,28},{32,36},{40,44},{48,52},{56,60},{4,0}... | collective-permute-start | bytes 393224 | tf_op jit(solution)/shard_map/ppermute | solution.py:303
  16.8 2.5 %collective-permute-start.1 = (bf16[2,32,8,128]{3,2,1,0:T(8,128)(2,1)S(1)}, bf16[2,32,8,128]{3,2,1,0:T(8,128)(2,1)S(1)}, u32[]{:S(2)}, u32[]{:S(2)}) collective-permute-start(bf16[2,32,8,128]{3,2,1,0:T(8,128)(2,1)S(1)} %get-tuple-element.18), channel_id=1, source_target_pairs={{4,8},{12,16},{20,24},{28,32},{36,40},{44,48},{52,56},{8,4},{16,12... | collective-permute-start | bytes 393224 | tf_op jit(solution)/shard_map/ppermute | solution.py:303
  19.2 0.0 copy-done
  19.2 0.3 pack_own.1.packed
  19.5 0.0 collective-permute-done.2
  19.6 4.7 %collective-permute-done.1 = bf16[2,32,8,128]{3,2,1,0:T(8,128)(2,1)S(1)} collective-permute-done((bf16[2,32,8,128]{3,2,1,0:T(8,128)(2,1)S(1)}, bf16[2,32,8,128]{3,2,1,0:T(8,128)(2,1)S(1)}, u32[]{:S(2)}, u32[]{:S(2)}) %collective-permute-start.1) | collective-permute-done | bytes 131104 | tf_op jit(solution)/shard_map/ppermute | solution.py:303
  24.3 0.3 pack_rim.1
  24.6 3.3 %collective-permute-start.3 = (bf16[128,128]{1,0:T(8,128)(2,1)S(1)}, bf16[128,128]{1,0:T(8,128)(2,1)S(1)}, u32[]{:S(2)}, u32[]{:S(2)}) collective-permute-start(bf16[128,128]{1,0:T(8,128)(2,1)S(1)} %get-tuple-element.13), channel_id=1, source_target_pairs={{0,1},{1,2},{2,3},{4,5},{5,6},{6,7},{8,9},{9,10},{10,11},{12,13},{... | collective-permute-start | bytes 98312 | tf_op jit(solution)/shard_map/ppermute | solution.py:299
  27.9 1.3 %collective-permute-start.4 = (bf16[128,128]{1,0:T(8,128)(2,1)S(1)}, bf16[128,128]{1,0:T(8,128)(2,1)S(1)}, u32[]{:S(2)}, u32[]{:S(2)}) collective-permute-start(bf16[128,128]{1,0:T(8,128)(2,1)S(1)} %get-tuple-element.14), channel_id=1, source_target_pairs={{1,0},{2,1},{3,2},{5,4},{6,5},{7,6},{9,8},{10,9},{11,10},{13,12},{... | collective-permute-start | bytes 98312 | tf_op jit(solution)/shard_map/ppermute | solution.py:299
  29.2 2.0 %inner.1 = (f32[3,16,32,128]{3,2,1,0:T(8,128)S(1)}, f32[2,2,128,128]{3,2,1,0:T(8,128)S(1)}, bf16[4,256,128]{2,1,0:T(8,128)(2,1)S(1)}) custom-call(bf16[32,16,128]{2,1,0:T(8,128)(2,1)S(1)} %bitcast.13, bf16[32,16,128]{2,1,0:T(8,128)(2,1)S(1)} %broadcast_select_fusion.4.nxt, bf16[2,32,8,128]{3,2,1,0:T(8,128)(2,1)S(1)} %get-tuple-element.16.low, ...), custom_call_target="tpu_custom_call" | custom-call | flops 1000000000 | bytes 1835008 | tf_op jit(solution)/shard_map/inner/pallas_call | solution.py:277
  31.2 0.0 collective-permute-done.3.from_left
  31.2 4.7 %collective-permute-done.4.from_right = bf16[128,128]{1,0:T(8,128)(2,1)S(1)} collective-permute-done((bf16[128,128]{1,0:T(8,128)(2,1)S(1)}, bf16[128,128]{1,0:T(8,128)(2,1)S(1)}, u32[]{:S(2)}, u32[]{:S(2)}) %collective-permute-start.4) | collective-permute-done | bytes 32800 | tf_op jit(solution)/shard_map/ppermute | solution.py:299
  35.9 3.0 %strip.1 = f32[3,512,128]{2,1,0:T(8,128)} custom-call(f32[3,16,32,128]{3,2,1,0:T(8,128)S(1)} %get-tuple-element.10.inner, f32[2,2,128,128]{3,2,1,0:T(8,128)S(1)} %get-tuple-element.11.part, bf16[4,256,128]{2,1,0:T(8,128)(2,1)S(1)} %get-tuple-element.12.edge_taps, bf16[128,128]{1,0:T(8,128)(2,1)S(1)} %collective-permute-done.3.from_left, ...), custom_call_target="tpu_custom_call" | custom-call | flops 100000000 | bytes 2162688 | tf_op jit(solution)/shard_map/strip/pallas_call | solution.py:277
  (4 shorter events, 0.1 us)
Async XLA Ops:
  0.0 14.6 %collective-permute-start = (bf16[32,16,128]{2,1,0:T(8,128)(2,1)}, bf16[32,16,128]{2,1,0:T(8,128)(2,1)S(1)}, u32[]{:S(2)}, u32[]{:S(2)}) collective-permute-start(bf16[32,16,128]{2,1,0:T(8,128)(2,1)} %bitcast.10), channel_id=1, source_target_pairs={{64,0},{128,64},{192,128},{256,192},{320,256},{384,320},{448,384},... | collective-permute-start | bytes 393224 | tf_op jit(solution)/shard_map/ppermute | solution.py:299
  2.8 11.9 %copy-start.1 = (bf16[32,16,128]{2,1,0:T(8,128)(2,1)S(1)}, bf16[32,16,128]{2,1,0:T(8,128)(2,1)}, u32[]{:S(2)}) copy-start(bf16[32,16,128]{2,1,0:T(8,128)(2,1)} %param.3) | copy-start | bytes 393220
  14.7 4.6 %copy-start = (bf16[1,32,16,128]{3,2,1,0:T(8,128)(2,1)S(1)}, bf16[1,32,16,128]{3,2,1,0:T(8,128)(2,1)}, u32[]{:S(2)}) copy-start(bf16[1,32,16,128]{3,2,1,0:T(8,128)(2,1)} %param.2) | copy-start | bytes 393220
  14.7 4.8 %collective-permute-start.2 = (bf16[2,32,8,128]{3,2,1,0:T(8,128)(2,1)S(1)}, bf16[2,32,8,128]{3,2,1,0:T(8,128)(2,1)S(1)}, u32[]{:S(2)}, u32[]{:S(2)}) collective-permute-start(bf16[2,32,8,128]{3,2,1,0:T(8,128)(2,1)S(1)} %get-tuple-element.17), channel_id=1, source_target_pairs={{0,4},{8,12},{16,20},{24,28},{32,36},{40,44},{48,52},{56,60},{4,0}... | collective-permute-start | bytes 393224 | tf_op jit(solution)/shard_map/ppermute | solution.py:303
  16.8 7.5 %collective-permute-start.1 = (bf16[2,32,8,128]{3,2,1,0:T(8,128)(2,1)S(1)}, bf16[2,32,8,128]{3,2,1,0:T(8,128)(2,1)S(1)}, u32[]{:S(2)}, u32[]{:S(2)}) collective-permute-start(bf16[2,32,8,128]{3,2,1,0:T(8,128)(2,1)S(1)} %get-tuple-element.18), channel_id=1, source_target_pairs={{4,8},{12,16},{20,24},{28,32},{36,40},{44,48},{52,56},{8,4},{16,12... | collective-permute-start | bytes 393224 | tf_op jit(solution)/shard_map/ppermute | solution.py:303
  24.6 6.6 %collective-permute-start.3 = (bf16[128,128]{1,0:T(8,128)(2,1)S(1)}, bf16[128,128]{1,0:T(8,128)(2,1)S(1)}, u32[]{:S(2)}, u32[]{:S(2)}) collective-permute-start(bf16[128,128]{1,0:T(8,128)(2,1)S(1)} %get-tuple-element.13), channel_id=1, source_target_pairs={{0,1},{1,2},{2,3},{4,5},{5,6},{6,7},{8,9},{9,10},{10,11},{12,13},{... | collective-permute-start | bytes 98312 | tf_op jit(solution)/shard_map/ppermute | solution.py:299
  27.9 8.1 %collective-permute-start.4 = (bf16[128,128]{1,0:T(8,128)(2,1)S(1)}, bf16[128,128]{1,0:T(8,128)(2,1)S(1)}, u32[]{:S(2)}, u32[]{:S(2)}) collective-permute-start(bf16[128,128]{1,0:T(8,128)(2,1)S(1)} %get-tuple-element.14), channel_id=1, source_target_pairs={{1,0},{2,1},{3,2},{5,4},{6,5},{7,6},{9,8},{10,9},{11,10},{13,12},{... | collective-permute-start | bytes 98312 | tf_op jit(solution)/shard_map/ppermute | solution.py:299

commit v4 on v3

--- a/solution.py
+++ b/solution.py
@@ -271,7 +271,7 @@
                 out[c, pl.ds(x, NZ, stride=WX), :] = jnp.where(rim, placed, inner[c, x])
 
 
-def call(kernel, outs, args, scratch, megabytes, flops, name):
+def call(kernel, outs, args, scratch, megabytes, flops):
     moved = sum(a.size * a.dtype.itemsize for a in (*args, *outs))
     spec = pl.BlockSpec(memory_space=pltpu.VMEM)
     return pl.pallas_call(
@@ -282,7 +282,6 @@
         scratch_shapes=scratch,
         compiler_params=pltpu.CompilerParams(vmem_limit_bytes=megabytes << 20),
         cost_estimate=pl.CostEstimate(flops=flops, bytes_accessed=moved, transcendentals=0),
-        name=name,
     )(*args)
 
 
@@ -309,14 +308,11 @@
     on_chip = swapped(jnp.where(even, upper, lower), "gx", 0)
     off_chip = swapped(jnp.where(even, lower, upper), "gx", 1)
     low, high = jnp.where(even, off_chip, on_chip), jnp.where(even, on_chip, off_chip)
-    (packed,) = call(
-        pack_own_kernel, (shape(128, 256, dtype=BF16),), (own, nxt), [], 8, 10**8, "pack_own"
-    )
+    (packed,) = call(pack_own_kernel, (shape(128, 256, dtype=BF16),), (own, nxt), [], 8, 10**8)
     message = shape(128, 128, dtype=BF16)
-    to_right, to_left = call(
-        pack_rim_kernel, (message, message), (low, high, packed), [], 8, 10**8, "pack_rim"
-    )
-    from_left, from_right = passed(to_right, "gy", 1), passed(to_left, "gy", -1)
+    to_right, to_left = call(pack_rim_kernel, (message, message), (low, high, packed), [], 8, 10**8)
+    from_left = passed(to_right, "gy", 1)
+    from_right = passed(to_left, "gy", -1)
     inner, part, edge_taps = call(
         inner_kernel,
         (shape(3, WX, NZ, WY), shape(2, 2, 128, WY), shape(4, 256, WY, dtype=BF16)),
@@ -332,7 +328,6 @@
         ],
         16,
         10**9,
-        "inner",
     )
     (flow,) = call(
         strip_kernel,
@@ -349,7 +344,6 @@
         ],
         16,
         10**8,
-        "strip",
     )
     return flow.reshape(1, 3, NZ, WX, WY)
 

time: 39.2 us -> 39.2 us (level)
  no operation moved by 1% of the time
where the time goes in v4:
time: 39.2 us; the launch traced here: 39 us
  waiting for transfers between devices  20.4 us (52%)
  starting transfers between devices  11.8 us (30%)
  Pallas kernels  5.63 us (14%)
  local copies, waits for them, and re-layouts  0.94 us (2%)
    ppermute x3, waiting for transfers between devices, passed(): return lax.ppermute(value, axis, pairs)  15.7 us
    ppermute x3, starting transfers between devices, passed(): return lax.ppermute(value, axis, pairs)  7.3 us
    pallas_call x4, Pallas kernels, call(): pl.pallas_call(kernel, out_shape=outs, in_specs=[spec] * len(args), out_s...  5.63 us
    ppermute x2, waiting for transfers between devices, swapped(): return lax.ppermute(value, axis, pairs + [(b, a) for a, b in pairs])  4.72 us
    ppermute x2, starting transfers between devices, swapped(): return lax.ppermute(value, axis, pairs + [(b, a) for a, b in pairs])  4.51 us
    another operation x2, local copies, waits for them, and re-layouts, on_device(): jnp.stack([own[:, :EDGE], nxt[:, :EDGE]])  0.93 us
  transfers between devices with their start and end apart: 5, of which 3 were waited for; matrix products, arithmetic and copies ran while one was open for 2% of the time, Pallas kernels for 6%

profile of v4, /device:TPU:38, one launch (start us, length us, event | category | flops | bytes accessed | tf_op | source)
XLA Modules:
  0.0 39.0 jit_solution(14899049591051216321)
XLA Ops:
  0.0 2.7 %collective-permute-start = (bf16[32,16,128]{2,1,0:T(8,128)(2,1)}, bf16[32,16,128]{2,1,0:T(8,128)(2,1)S(1)}, u32[]{:S(2)}, u32[]{:S(2)}) collective-permute-start(bf16[32,16,128]{2,1,0:T(8,128)(2,1)} %bitcast.10), channel_id=1, source_target_pairs={{64,0},{128,64},{192,128},{256,192},{320,256},{384,320},{448,384},... | collective-permute-start | bytes 393224 | tf_op jit(solution)/shard_map/ppermute | solution.py:298
  2.8 0.0 copy-start.1
  2.8 0.9 %slice_bitcast_fusion.3 = (bf16[1,32,8,128]{3,2,1,0:T(8,128)(2,1)S(1)}, bf16[1,32,8,128]{3,2,1,0:T(8,128)(2,1)S(1)}) fusion(bf16[32,16,128]{2,1,0:T(8,128)(2,1)} %bitcast.11), kind=kLoop, calls=%fused_computation.10 | loop fusion | bytes 262144 | tf_op jit(solution)/shard_map/stack | solution.py:306
  3.7 10.9 %collective-permute-done = bf16[32,16,128]{2,1,0:T(8,128)(2,1)S(1)} collective-permute-done((bf16[32,16,128]{2,1,0:T(8,128)(2,1)}, bf16[32,16,128]{2,1,0:T(8,128)(2,1)S(1)}, u32[]{:S(2)}, u32[]{:S(2)}) %collective-permute-start) | collective-permute-done | bytes 131104 | tf_op jit(solution)/shard_map/ppermute | solution.py:298
  14.6 0.0 copy-done.1
  14.7 0.0 copy-start
  14.7 2.1 %collective-permute-start.2 = (bf16[2,32,8,128]{3,2,1,0:T(8,128)(2,1)S(1)}, bf16[2,32,8,128]{3,2,1,0:T(8,128)(2,1)S(1)}, u32[]{:S(2)}, u32[]{:S(2)}) collective-permute-start(bf16[2,32,8,128]{3,2,1,0:T(8,128)(2,1)S(1)} %get-tuple-element.17), channel_id=1, source_target_pairs={{0,4},{8,12},{16,20},{24,28},{32,36},{40,44},{48,52},{56,60},{4,0}... | collective-permute-start | bytes 393224 | tf_op jit(solution)/shard_map/ppermute | solution.py:302
  16.8 2.5 %collective-permute-start.1 = (bf16[2,32,8,128]{3,2,1,0:T(8,128)(2,1)S(1)}, bf16[2,32,8,128]{3,2,1,0:T(8,128)(2,1)S(1)}, u32[]{:S(2)}, u32[]{:S(2)}) collective-permute-start(bf16[2,32,8,128]{3,2,1,0:T(8,128)(2,1)S(1)} %get-tuple-element.18), channel_id=1, source_target_pairs={{4,8},{12,16},{20,24},{28,32},{36,40},{44,48},{52,56},{8,4},{16,12... | collective-permute-start | bytes 393224 | tf_op jit(solution)/shard_map/ppermute | solution.py:302
  19.2 0.0 copy-done
  19.2 0.3 shard_map.29.packed
  19.5 0.0 collective-permute-done.2
  19.6 4.7 %collective-permute-done.1 = bf16[2,32,8,128]{3,2,1,0:T(8,128)(2,1)S(1)} collective-permute-done((bf16[2,32,8,128]{3,2,1,0:T(8,128)(2,1)S(1)}, bf16[2,32,8,128]{3,2,1,0:T(8,128)(2,1)S(1)}, u32[]{:S(2)}, u32[]{:S(2)}) %collective-permute-start.1) | collective-permute-done | bytes 131104 | tf_op jit(solution)/shard_map/ppermute | solution.py:302
  24.3 0.3 shard_map.30
  24.6 3.3 %collective-permute-start.3 = (bf16[128,128]{1,0:T(8,128)(2,1)S(1)}, bf16[128,128]{1,0:T(8,128)(2,1)S(1)}, u32[]{:S(2)}, u32[]{:S(2)}) collective-permute-start(bf16[128,128]{1,0:T(8,128)(2,1)S(1)} %get-tuple-element.13), channel_id=1, source_target_pairs={{0,1},{1,2},{2,3},{4,5},{5,6},{6,7},{8,9},{9,10},{10,11},{12,13},{... | collective-permute-start | bytes 98312 | tf_op jit(solution)/shard_map/ppermute | solution.py:298
  27.9 1.3 %collective-permute-start.4 = (bf16[128,128]{1,0:T(8,128)(2,1)S(1)}, bf16[128,128]{1,0:T(8,128)(2,1)S(1)}, u32[]{:S(2)}, u32[]{:S(2)}) collective-permute-start(bf16[128,128]{1,0:T(8,128)(2,1)S(1)} %get-tuple-element.14), channel_id=1, source_target_pairs={{1,0},{2,1},{3,2},{5,4},{6,5},{7,6},{9,8},{10,9},{11,10},{13,12},{... | collective-permute-start | bytes 98312 | tf_op jit(solution)/shard_map/ppermute | solution.py:298
  29.2 2.0 %shard_map.28 = (f32[3,16,32,128]{3,2,1,0:T(8,128)S(1)}, f32[2,2,128,128]{3,2,1,0:T(8,128)S(1)}, bf16[4,256,128]{2,1,0:T(8,128)(2,1)S(1)}) custom-call(bf16[32,16,128]{2,1,0:T(8,128)(2,1)S(1)} %bitcast.13, bf16[32,16,128]{2,1,0:T(8,128)(2,1)S(1)} %broadcast_select_fusion.4.nxt, bf16[2,32,8,128]{3,2,1,0:T(8,128)(2,1)S(1)} %get-tuple-element.16.low, ...), custom_call_target="tpu_custom_call" | custom-call | flops 1000000000 | bytes 1835008 | tf_op jit(solution)/shard_map/pallas_call | solution.py:277
  31.2 0.0 collective-permute-done.3.from_left
  31.2 4.7 %collective-permute-done.4.from_right = bf16[128,128]{1,0:T(8,128)(2,1)S(1)} collective-permute-done((bf16[128,128]{1,0:T(8,128)(2,1)S(1)}, bf16[128,128]{1,0:T(8,128)(2,1)S(1)}, u32[]{:S(2)}, u32[]{:S(2)}) %collective-permute-start.4) | collective-permute-done | bytes 32800 | tf_op jit(solution)/shard_map/ppermute | solution.py:298
  35.9 3.0 %shard_map.31 = f32[3,512,128]{2,1,0:T(8,128)} custom-call(f32[3,16,32,128]{3,2,1,0:T(8,128)S(1)} %get-tuple-element.10.inner, f32[2,2,128,128]{3,2,1,0:T(8,128)S(1)} %get-tuple-element.11.part, bf16[4,256,128]{2,1,0:T(8,128)(2,1)S(1)} %get-tuple-element.12.edge_taps, bf16[128,128]{1,0:T(8,128)(2,1)S(1)} %collective-permute-done.3.from_left, ...), custom_call_target="tpu_custom_call" | custom-call | flops 100000000 | bytes 2162688 | tf_op jit(solution)/shard_map/pallas_call | solution.py:277
  (4 shorter events, 0.1 us)
Async XLA Ops:
  0.0 14.6 %collective-permute-start = (bf16[32,16,128]{2,1,0:T(8,128)(2,1)}, bf16[32,16,128]{2,1,0:T(8,128)(2,1)S(1)}, u32[]{:S(2)}, u32[]{:S(2)}) collective-permute-start(bf16[32,16,128]{2,1,0:T(8,128)(2,1)} %bitcast.10), channel_id=1, source_target_pairs={{64,0},{128,64},{192,128},{256,192},{320,256},{384,320},{448,384},... | collective-permute-start | bytes 393224 | tf_op jit(solution)/shard_map/ppermute | solution.py:298
  2.8 11.9 %copy-start.1 = (bf16[32,16,128]{2,1,0:T(8,128)(2,1)S(1)}, bf16[32,16,128]{2,1,0:T(8,128)(2,1)}, u32[]{:S(2)}) copy-start(bf16[32,16,128]{2,1,0:T(8,128)(2,1)} %param.3) | copy-start | bytes 393220
  14.7 4.6 %copy-start = (bf16[1,32,16,128]{3,2,1,0:T(8,128)(2,1)S(1)}, bf16[1,32,16,128]{3,2,1,0:T(8,128)(2,1)}, u32[]{:S(2)}) copy-start(bf16[1,32,16,128]{3,2,1,0:T(8,128)(2,1)} %param.2) | copy-start | bytes 393220
  14.7 4.8 %collective-permute-start.2 = (bf16[2,32,8,128]{3,2,1,0:T(8,128)(2,1)S(1)}, bf16[2,32,8,128]{3,2,1,0:T(8,128)(2,1)S(1)}, u32[]{:S(2)}, u32[]{:S(2)}) collective-permute-start(bf16[2,32,8,128]{3,2,1,0:T(8,128)(2,1)S(1)} %get-tuple-element.17), channel_id=1, source_target_pairs={{0,4},{8,12},{16,20},{24,28},{32,36},{40,44},{48,52},{56,60},{4,0}... | collective-permute-start | bytes 393224 | tf_op jit(solution)/shard_map/ppermute | solution.py:302
  16.8 7.5 %collective-permute-start.1 = (bf16[2,32,8,128]{3,2,1,0:T(8,128)(2,1)S(1)}, bf16[2,32,8,128]{3,2,1,0:T(8,128)(2,1)S(1)}, u32[]{:S(2)}, u32[]{:S(2)}) collective-permute-start(bf16[2,32,8,128]{3,2,1,0:T(8,128)(2,1)S(1)} %get-tuple-element.18), channel_id=1, source_target_pairs={{4,8},{12,16},{20,24},{28,32},{36,40},{44,48},{52,56},{8,4},{16,12... | collective-permute-start | bytes 393224 | tf_op jit(solution)/shard_map/ppermute | solution.py:302
  24.6 6.6 %collective-permute-start.3 = (bf16[128,128]{1,0:T(8,128)(2,1)S(1)}, bf16[128,128]{1,0:T(8,128)(2,1)S(1)}, u32[]{:S(2)}, u32[]{:S(2)}) collective-permute-start(bf16[128,128]{1,0:T(8,128)(2,1)S(1)} %get-tuple-element.13), channel_id=1, source_target_pairs={{0,1},{1,2},{2,3},{4,5},{5,6},{6,7},{8,9},{9,10},{10,11},{12,13},{... | collective-permute-start | bytes 98312 | tf_op jit(solution)/shard_map/ppermute | solution.py:298
  27.9 8.1 %collective-permute-start.4 = (bf16[128,128]{1,0:T(8,128)(2,1)S(1)}, bf16[128,128]{1,0:T(8,128)(2,1)S(1)}, u32[]{:S(2)}, u32[]{:S(2)}) collective-permute-start(bf16[128,128]{1,0:T(8,128)(2,1)S(1)} %get-tuple-element.14), channel_id=1, source_target_pairs={{1,0},{2,1},{3,2},{5,4},{6,5},{7,6},{9,8},{10,9},{11,10},{13,12},{... | collective-permute-start | bytes 98312 | tf_op jit(solution)/shard_map/ppermute | solution.py:298

commit v5 on v4

--- a/solution.py
+++ b/solution.py
@@ -216,7 +216,7 @@
             inner[c, x] = value
 
 
-def strip_kernel(inner, part, edge_taps, from_left, from_right, out, p_ref, q_ref, s_ref, c_ref, h_ref, u_ref, v_ref):
+def strip_kernel(inner, part, edge_taps, from_left, from_right, out, p_ref, q_ref, s_ref, c_ref, h_ref, u_ref, v_ref, w_ref, done_ref, sems):
     x_low, x_high, y_low, y_high = inside()
     lane = iota((1, WY), 1)
     column = strip_column(lane)
@@ -260,25 +260,40 @@
     for i in range(8):
         for c, value in enumerate(jacobi(u, i + 1, [h_ref[c, i] for c in range(4)])):
             put(v[c], i, value * weight, 1)
+    for i in range(8):
+        for c, value in enumerate(jacobi(v, i + 1, [h_ref[c, i] for c in range(4)])):
+            w_ref[c, NZ * i : NZ * i + NZ, :] = value
+    row, lane = iota((WY, 256), 0), iota((WY, 256), 1)
+    place, to = row & 31, lane & 127
+    pick = ((row >> 5) - 1 == (lane >> 7)) & ((to == place - 5) | (to == place + 101))
+    pick = jnp.where(pick, 1.0, 0.0).astype(BF16)
     own_lane = iota((NZ, WY), 1)
     rim = (own_lane < 5) | (own_lane >= WY - 5)
-    for i in range(8):
-        for c, value in enumerate(jacobi(v, i + 1, [h_ref[c, i] for c in range(4)])):
-            value = jnp.where((own_lane & 31) < 5, pltpu.roll(value, WY - 22, 1), value)
+    for c in range(3):
+        rest = w_ref[c]
+        placed = jnp.zeros((8 * NZ, 256), F32)
+        for _ in range(3):
+            term = rest.astype(BF16)
+            rest = rest - term.astype(F32)
+            placed = placed + dot(term, pick)
+        for i in range(8):
             for half in range(2):
                 x = 8 * half + i
-                placed = pltpu.roll(value, WY - 32 * (half + 1) - 5, 1)
-                out[c, pl.ds(x, NZ, stride=WX), :] = jnp.where(rim, placed, inner[c, x])
-
-
-def call(kernel, outs, args, scratch, megabytes, flops):
+                found = placed[NZ * i : NZ * i + NZ, 128 * half : 128 * half + 128]
+                done_ref[c, pl.ds(x, NZ, stride=WX), :] = jnp.where(rim, found, inner[c, x])
+        pltpu.make_async_copy(done_ref.at[c], out.at[c], sems.at[c]).start()
+    for c in range(3):
+        pltpu.make_async_copy(done_ref.at[c], out.at[c], sems.at[c]).wait()
+
+
+def call(kernel, outs, args, scratch, megabytes, flops, out_space=pltpu.VMEM):
     moved = sum(a.size * a.dtype.itemsize for a in (*args, *outs))
     spec = pl.BlockSpec(memory_space=pltpu.VMEM)
     return pl.pallas_call(
         kernel,
         out_shape=outs,
         in_specs=[spec] * len(args),
-        out_specs=tuple([spec] * len(outs)),
+        out_specs=tuple([pl.BlockSpec(memory_space=out_space)] * len(outs)),
         scratch_shapes=scratch,
         compiler_params=pltpu.CompilerParams(vmem_limit_bytes=megabytes << 20),
         cost_estimate=pl.CostEstimate(flops=flops, bytes_accessed=moved, transcendentals=0),
@@ -341,9 +356,13 @@
             pltpu.VMEM((4, 8, NZ, WY), F32),
             planes_of_3(10),
             planes_of_3(10),
+            pltpu.VMEM((3, 8 * NZ, WY), F32),
+            pltpu.VMEM((3, NZ * WX, WY), F32),
+            pltpu.SemaphoreType.DMA((3,)),
         ],
         16,
         10**8,
+        pl.ANY,
     )
     return flow.reshape(1, 3, NZ, WX, WY)
 

time: 39.2 us -> 38.4 us (0.980)
  Pallas kernels: 5.63 us -> 4.79 us
    pallas_call x4, Pallas kernels: 5.63 us -> 4.79 us  [call(): pl.pallas_call(kernel, out_shape=outs, in_specs=[spec] * len(args), out_s...]
where the time goes in v5:
time: 38.4 us; the launch traced here: 38.1 us
  waiting for transfers between devices  20.4 us (53%)
  starting transfers between devices  11.8 us (31%)
  Pallas kernels  4.79 us (12%)
  local copies, waits for them, and re-layouts  0.94 us (2%)
    ppermute x3, waiting for transfers between devices, passed(): return lax.ppermute(value, axis, pairs)  15.7 us
    ppermute x3, starting transfers between devices, passed(): return lax.ppermute(value, axis, pairs)  7.3 us
    pallas_call x4, Pallas kernels, call(): pl.pallas_call(kernel, out_shape=outs, in_specs=[spec] * len(args), out_s...  4.79 us
    ppermute x2, waiting for transfers between devices, swapped(): return lax.ppermute(value, axis, pairs + [(b, a) for a, b in pairs])  4.72 us
    ppermute x2, starting transfers between devices, swapped(): return lax.ppermute(value, axis, pairs + [(b, a) for a, b in pairs])  4.51 us
    another operation x2, local copies, waits for them, and re-layouts, on_device(): jnp.stack([own[:, :EDGE], nxt[:, :EDGE]])  0.93 us
  transfers between devices with their start and end apart: 5, of which 3 were waited for; matrix products, arithmetic and copies ran while one was open for 2% of the time, Pallas kernels for 6%

profile of v5, /device:TPU:38, one launch (start us, length us, event | category | flops | bytes accessed | tf_op | source)
XLA Modules:
  0.0 38.1 jit_solution(8396340717871503453)
XLA Ops:
  0.0 2.7 %collective-permute-start = (bf16[32,16,128]{2,1,0:T(8,128)(2,1)}, bf16[32,16,128]{2,1,0:T(8,128)(2,1)S(1)}, u32[]{:S(2)}, u32[]{:S(2)}) collective-permute-start(bf16[32,16,128]{2,1,0:T(8,128)(2,1)} %bitcast.10), channel_id=1, source_target_pairs={{64,0},{128,64},{192,128},{256,192},{320,256},{384,320},{448,384},... | collective-permute-start | bytes 393224 | tf_op jit(solution)/shard_map/ppermute | solution.py:313
  2.8 0.0 copy-start.1
  2.8 0.9 %slice_bitcast_fusion.3 = (bf16[1,32,8,128]{3,2,1,0:T(8,128)(2,1)S(1)}, bf16[1,32,8,128]{3,2,1,0:T(8,128)(2,1)S(1)}) fusion(bf16[32,16,128]{2,1,0:T(8,128)(2,1)} %bitcast.11), kind=kLoop, calls=%fused_computation.10 | loop fusion | bytes 262144 | tf_op jit(solution)/shard_map/stack | solution.py:321
  3.7 10.9 %collective-permute-done = bf16[32,16,128]{2,1,0:T(8,128)(2,1)S(1)} collective-permute-done((bf16[32,16,128]{2,1,0:T(8,128)(2,1)}, bf16[32,16,128]{2,1,0:T(8,128)(2,1)S(1)}, u32[]{:S(2)}, u32[]{:S(2)}) %collective-permute-start) | collective-permute-done | bytes 131104 | tf_op jit(solution)/shard_map/ppermute | solution.py:313
  14.6 0.0 copy-done.1
  14.7 0.0 copy-start
  14.7 2.1 %collective-permute-start.2 = (bf16[2,32,8,128]{3,2,1,0:T(8,128)(2,1)S(1)}, bf16[2,32,8,128]{3,2,1,0:T(8,128)(2,1)S(1)}, u32[]{:S(2)}, u32[]{:S(2)}) collective-permute-start(bf16[2,32,8,128]{3,2,1,0:T(8,128)(2,1)S(1)} %get-tuple-element.17), channel_id=1, source_target_pairs={{0,4},{8,12},{16,20},{24,28},{32,36},{40,44},{48,52},{56,60},{4,0}... | collective-permute-start | bytes 393224 | tf_op jit(solution)/shard_map/ppermute | solution.py:317
  16.8 2.5 %collective-permute-start.1 = (bf16[2,32,8,128]{3,2,1,0:T(8,128)(2,1)S(1)}, bf16[2,32,8,128]{3,2,1,0:T(8,128)(2,1)S(1)}, u32[]{:S(2)}, u32[]{:S(2)}) collective-permute-start(bf16[2,32,8,128]{3,2,1,0:T(8,128)(2,1)S(1)} %get-tuple-element.18), channel_id=1, source_target_pairs={{4,8},{12,16},{20,24},{28,32},{36,40},{44,48},{52,56},{8,4},{16,12... | collective-permute-start | bytes 393224 | tf_op jit(solution)/shard_map/ppermute | solution.py:317
  19.2 0.0 copy-done
  19.2 0.3 shard_map.29.packed
  19.5 0.0 collective-permute-done.2
  19.6 4.7 %collective-permute-done.1 = bf16[2,32,8,128]{3,2,1,0:T(8,128)(2,1)S(1)} collective-permute-done((bf16[2,32,8,128]{3,2,1,0:T(8,128)(2,1)S(1)}, bf16[2,32,8,128]{3,2,1,0:T(8,128)(2,1)S(1)}, u32[]{:S(2)}, u32[]{:S(2)}) %collective-permute-start.1) | collective-permute-done | bytes 131104 | tf_op jit(solution)/shard_map/ppermute | solution.py:317
  24.3 0.3 shard_map.30
  24.6 3.3 %collective-permute-start.3 = (bf16[128,128]{1,0:T(8,128)(2,1)S(1)}, bf16[128,128]{1,0:T(8,128)(2,1)S(1)}, u32[]{:S(2)}, u32[]{:S(2)}) collective-permute-start(bf16[128,128]{1,0:T(8,128)(2,1)S(1)} %get-tuple-element.13), channel_id=1, source_target_pairs={{0,1},{1,2},{2,3},{4,5},{5,6},{6,7},{8,9},{9,10},{10,11},{12,13},{... | collective-permute-start | bytes 98312 | tf_op jit(solution)/shard_map/ppermute | solution.py:313
  27.9 1.3 %collective-permute-start.4 = (bf16[128,128]{1,0:T(8,128)(2,1)S(1)}, bf16[128,128]{1,0:T(8,128)(2,1)S(1)}, u32[]{:S(2)}, u32[]{:S(2)}) collective-permute-start(bf16[128,128]{1,0:T(8,128)(2,1)S(1)} %get-tuple-element.14), channel_id=1, source_target_pairs={{1,0},{2,1},{3,2},{5,4},{6,5},{7,6},{9,8},{10,9},{11,10},{13,12},{... | collective-permute-start | bytes 98312 | tf_op jit(solution)/shard_map/ppermute | solution.py:313
  29.2 2.0 %shard_map.28 = (f32[3,16,32,128]{3,2,1,0:T(8,128)S(1)}, f32[2,2,128,128]{3,2,1,0:T(8,128)S(1)}, bf16[4,256,128]{2,1,0:T(8,128)(2,1)S(1)}) custom-call(bf16[32,16,128]{2,1,0:T(8,128)(2,1)S(1)} %bitcast.13, bf16[32,16,128]{2,1,0:T(8,128)(2,1)S(1)} %broadcast_select_fusion.4.nxt, bf16[2,32,8,128]{3,2,1,0:T(8,128)(2,1)S(1)} %get-tuple-element.16.low, ...), custom_call_target="tpu_custom_call" | custom-call | flops 1000000000 | bytes 1835008 | tf_op jit(solution)/shard_map/pallas_call | solution.py:292
  31.2 0.0 collective-permute-done.3.from_left
  31.2 4.7 %collective-permute-done.4.from_right = bf16[128,128]{1,0:T(8,128)(2,1)S(1)} collective-permute-done((bf16[128,128]{1,0:T(8,128)(2,1)S(1)}, bf16[128,128]{1,0:T(8,128)(2,1)S(1)}, u32[]{:S(2)}, u32[]{:S(2)}) %collective-permute-start.4) | collective-permute-done | bytes 32800 | tf_op jit(solution)/shard_map/ppermute | solution.py:313
  35.9 2.2 %shard_map.31 = f32[3,512,128]{2,1,0:T(8,128)} custom-call(f32[3,16,32,128]{3,2,1,0:T(8,128)S(1)} %get-tuple-element.10.inner, f32[2,2,128,128]{3,2,1,0:T(8,128)S(1)} %get-tuple-element.11.part, bf16[4,256,128]{2,1,0:T(8,128)(2,1)S(1)} %get-tuple-element.12.edge_taps, bf16[128,128]{1,0:T(8,128)(2,1)S(1)} %collective-permute-done.3.from_left, ...), custom_call_target="tpu_custom_call" | custom-call | flops 100000000 | bytes 2162688 | tf_op jit(solution)/shard_map/pallas_call | solution.py:292
  (4 shorter events, 0.1 us)
Async XLA Ops:
  0.0 14.6 %collective-permute-start = (bf16[32,16,128]{2,1,0:T(8,128)(2,1)}, bf16[32,16,128]{2,1,0:T(8,128)(2,1)S(1)}, u32[]{:S(2)}, u32[]{:S(2)}) collective-permute-start(bf16[32,16,128]{2,1,0:T(8,128)(2,1)} %bitcast.10), channel_id=1, source_target_pairs={{64,0},{128,64},{192,128},{256,192},{320,256},{384,320},{448,384},... | collective-permute-start | bytes 393224 | tf_op jit(solution)/shard_map/ppermute | solution.py:313
  2.8 11.9 %copy-start.1 = (bf16[32,16,128]{2,1,0:T(8,128)(2,1)S(1)}, bf16[32,16,128]{2,1,0:T(8,128)(2,1)}, u32[]{:S(2)}) copy-start(bf16[32,16,128]{2,1,0:T(8,128)(2,1)} %param.3) | copy-start | bytes 393220
  14.7 4.6 %copy-start = (bf16[1,32,16,128]{3,2,1,0:T(8,128)(2,1)S(1)}, bf16[1,32,16,128]{3,2,1,0:T(8,128)(2,1)}, u32[]{:S(2)}) copy-start(bf16[1,32,16,128]{3,2,1,0:T(8,128)(2,1)} %param.2) | copy-start | bytes 393220
  14.7 4.8 %collective-permute-start.2 = (bf16[2,32,8,128]{3,2,1,0:T(8,128)(2,1)S(1)}, bf16[2,32,8,128]{3,2,1,0:T(8,128)(2,1)S(1)}, u32[]{:S(2)}, u32[]{:S(2)}) collective-permute-start(bf16[2,32,8,128]{3,2,1,0:T(8,128)(2,1)S(1)} %get-tuple-element.17), channel_id=1, source_target_pairs={{0,4},{8,12},{16,20},{24,28},{32,36},{40,44},{48,52},{56,60},{4,0}... | collective-permute-start | bytes 393224 | tf_op jit(solution)/shard_map/ppermute | solution.py:317
  16.8 7.5 %collective-permute-start.1 = (bf16[2,32,8,128]{3,2,1,0:T(8,128)(2,1)S(1)}, bf16[2,32,8,128]{3,2,1,0:T(8,128)(2,1)S(1)}, u32[]{:S(2)}, u32[]{:S(2)}) collective-permute-start(bf16[2,32,8,128]{3,2,1,0:T(8,128)(2,1)S(1)} %get-tuple-element.18), channel_id=1, source_target_pairs={{4,8},{12,16},{20,24},{28,32},{36,40},{44,48},{52,56},{8,4},{16,12... | collective-permute-start | bytes 393224 | tf_op jit(solution)/shard_map/ppermute | solution.py:317
  24.6 6.6 %collective-permute-start.3 = (bf16[128,128]{1,0:T(8,128)(2,1)S(1)}, bf16[128,128]{1,0:T(8,128)(2,1)S(1)}, u32[]{:S(2)}, u32[]{:S(2)}) collective-permute-start(bf16[128,128]{1,0:T(8,128)(2,1)S(1)} %get-tuple-element.13), channel_id=1, source_target_pairs={{0,1},{1,2},{2,3},{4,5},{5,6},{6,7},{8,9},{9,10},{10,11},{12,13},{... | collective-permute-start | bytes 98312 | tf_op jit(solution)/shard_map/ppermute | solution.py:313
  27.9 8.1 %collective-permute-start.4 = (bf16[128,128]{1,0:T(8,128)(2,1)S(1)}, bf16[128,128]{1,0:T(8,128)(2,1)S(1)}, u32[]{:S(2)}, u32[]{:S(2)}) collective-permute-start(bf16[128,128]{1,0:T(8,128)(2,1)S(1)} %get-tuple-element.14), channel_id=1, source_target_pairs={{1,0},{2,1},{3,2},{5,4},{6,5},{7,6},{9,8},{10,9},{11,10},{13,12},{... | collective-permute-start | bytes 98312 | tf_op jit(solution)/shard_map/ppermute | solution.py:313

commit v6 on v5

--- a/solution.py
+++ b/solution.py
@@ -36,10 +36,7 @@
     return jnp.where(place < 16, place - 5, place + 101)
 
 
-def edge_columns(blocks):
-    row, lane = iota((WY, 256), 0), iota((WY, 256), 1)
-    column = (lane & 7) + jnp.where(lane < 128, WY - EDGE, 0)
-    pick = jnp.where(row == column, 1.0, 0.0).astype(BF16)
+def edge_columns(blocks, pick):
     group = (iota((128, 256), 1) & 127) >> 3
     packed = jnp.zeros((128, 256), F32)
     for (octet, frame), block in blocks.items():
@@ -49,21 +46,37 @@
     return packed.astype(BF16)
 
 
-def pack_own_kernel(own, nxt, packed):
-    packed[...] = edge_columns(
-        {
-            (octet, frame): block[:, 8 * octet - 8 : 8 * octet, :]
-            for octet in (1, 2)
-            for frame, block in enumerate((own, nxt))
-        }
-    )
-
-
-def pack_rim_kernel(low, high, packed, to_right, to_left):
-    rim = edge_columns(
-        {(octet, frame): block[frame] for octet, block in ((0, low), (3, high)) for frame in range(2)}
-    )
-    both = packed[...] + rim
+def own_octets(block, frame):
+    return {(octet, frame): block[:, 8 * octet - 8 : 8 * octet, :] for octet in (1, 2)}
+
+
+def front_kernel(own, packed, pick, taps, octet_taps, edge_taps, place):
+    row, lane = iota((WY, 256), 0), iota((WY, 256), 1)
+    column = (lane & 7) + jnp.where(lane < 128, WY - EDGE, 0)
+    pick[...] = jnp.where(row == column, 1.0, 0.0).astype(BF16)
+    packed[...] = edge_columns(own_octets(own, 0), pick[...])
+
+    at, to = row & 31, lane & 127
+    hit = ((row >> 5) - 1 == (lane >> 7)) & ((to == at - 5) | (to == at + 101))
+    place[...] = jnp.where(hit, 1.0, 0.0).astype(BF16)
+
+    row, lane = iota((WY, WY), 0), iota((WY, WY), 1)
+    taps[...] = y_taps(lane - row).astype(BF16)
+    strip_taps = y_taps(strip_column(lane) - row)
+    for octet in range(4):
+        octet_taps[WY * octet : WY * octet + WY, :] = jnp.where((lane >> 5) == octet, strip_taps, 0.0).astype(BF16)
+
+    row, lane = iota((256, WY), 0), iota((256, WY), 1)
+    column = (row & 7) + jnp.where(row < 128, -EDGE, WY)
+    edge = jnp.where(((row & 127) >> 5) == (lane >> 5), y_taps(strip_column(lane) - column), 0.0)
+    for group in range(4):
+        edge_taps[group] = jnp.where(((row >> 3) & 3) == group, edge, 0.0).astype(BF16)
+
+
+def pack_kernel(nxt, low, high, packed, pick, to_right, to_left):
+    blocks = own_octets(nxt, 1)
+    blocks |= {(octet, frame): block[frame] for octet, block in ((0, low), (3, high)) for frame in range(2)}
+    both = packed[...] + edge_columns(blocks, pick[...])
     to_right[...] = both[:, :128]
     to_left[...] = both[:, 128:]
 
@@ -142,7 +155,7 @@
     return faces
 
 
-def inner_kernel(own, nxt, low, high, inner, part, edge_taps, p_ref, q_ref, s_ref, c_ref, h_ref, u_ref, v_ref):
+def inner_kernel(own, nxt, low, high, taps, octet_taps, inner, part, p_ref, q_ref, s_ref, c_ref, h_ref, u_ref, v_ref):
     x_low, x_high, _, _ = inside()
 
     def weight(x):
@@ -159,19 +172,6 @@
     for c in range(3):
         u[c].clear(1, 18)
         v[c].clear(1, 16)
-
-    row, lane = iota((WY, WY), 0), iota((WY, WY), 1)
-    taps = y_taps(lane - row).astype(BF16)
-    strip_taps = y_taps(strip_column(lane) - row)
-    octet_taps = jnp.concatenate(
-        [jnp.where((lane >> 5) == octet, strip_taps, 0.0) for octet in range(4)], axis=0
-    ).astype(BF16)
-
-    row, lane = iota((256, WY), 0), iota((256, WY), 1)
-    column = (row & 7) + jnp.where(row < 128, -EDGE, WY)
-    edge = jnp.where(((row & 127) >> 5) == (lane >> 5), y_taps(strip_column(lane) - column), 0.0)
-    for group in range(4):
-        edge_taps[group] = jnp.where(((row >> 3) & 3) == group, edge, 0.0).astype(BF16)
 
     for z_half in range(2):
         octets = [[], []]
@@ -185,13 +185,13 @@
                 )
                 rows = block.astype(F32).reshape(128, WY).astype(BF16)
                 octets[frame].append(rows)
-                found.append(dot(rows, taps))
+                found.append(dot(rows, taps[...]))
             total, change = (found[0] + found[1]) * 0.25, found[1] - found[0]
             for i in range(16):
                 p.put_z(8 * octet, 16 * z_half + i, total[8 * i : 8 * i + 8])
                 q.put_z(8 * octet, 16 * z_half + i, change[8 * i : 8 * i + 8])
         for frame in range(2):
-            part[frame, z_half] = dot(jnp.concatenate(octets[frame], axis=1), octet_taps)
+            part[frame, z_half] = dot(jnp.concatenate(octets[frame], axis=1), octet_taps[...])
 
     for k in range(3, 29):
         p.put(k, smooth_z(p, k))
@@ -216,7 +216,7 @@
             inner[c, x] = value
 
 
-def strip_kernel(inner, part, edge_taps, from_left, from_right, out, p_ref, q_ref, s_ref, c_ref, h_ref, u_ref, v_ref, w_ref, done_ref, sems):
+def strip_kernel(inner, part, edge_taps, place, from_left, from_right, out, p_ref, q_ref, s_ref, c_ref, h_ref, u_ref, v_ref, w_ref, done_ref, sems):
     x_low, x_high, y_low, y_high = inside()
     lane = iota((1, WY), 1)
     column = strip_column(lane)
@@ -263,10 +263,6 @@
     for i in range(8):
         for c, value in enumerate(jacobi(v, i + 1, [h_ref[c, i] for c in range(4)])):
             w_ref[c, NZ * i : NZ * i + NZ, :] = value
-    row, lane = iota((WY, 256), 0), iota((WY, 256), 1)
-    place, to = row & 31, lane & 127
-    pick = ((row >> 5) - 1 == (lane >> 7)) & ((to == place - 5) | (to == place + 101))
-    pick = jnp.where(pick, 1.0, 0.0).astype(BF16)
     own_lane = iota((NZ, WY), 1)
     rim = (own_lane < 5) | (own_lane >= WY - 5)
     for c in range(3):
@@ -275,7 +271,7 @@
         for _ in range(3):
             term = rest.astype(BF16)
             rest = rest - term.astype(F32)
-            placed = placed + dot(term, pick)
+            placed = placed + dot(term, place[...])
         for i in range(8):
             for half in range(2):
                 x = 8 * half + i
@@ -317,21 +313,33 @@
         return lax.ppermute(value, axis, pairs + [(b, a) for a, b in pairs])
 
     arriving = passed(own, "ta", -1)
+    packed, pick, taps, octet_taps, edge_taps, place = call(
+        front_kernel,
+        tuple(
+            shape(*dims, dtype=BF16)
+            for dims in ((128, 256), (WY, 256), (WY, WY), (4 * WY, WY), (4, 256, WY), (WY, 256))
+        ),
+        (own,),
+        [],
+        8,
+        10**8,
+    )
     nxt = jnp.where(lax.axis_index("ta") == lax.axis_size("ta") - 1, trailing, arriving)
     upper, lower = jnp.stack([own[:, WX - EDGE :], nxt[:, WX - EDGE :]]), jnp.stack([own[:, :EDGE], nxt[:, :EDGE]])
     even = lax.axis_index("gx") % 2 == 0
-    on_chip = swapped(jnp.where(even, upper, lower), "gx", 0)
     off_chip = swapped(jnp.where(even, lower, upper), "gx", 1)
+    pairs = [[i, i + 1] for i in range(0, lax.axis_size("gx"), 2)]
+    both = lax.all_gather(jnp.where(even, upper, lower), "gx", axis_index_groups=pairs)
+    on_chip = jnp.where(even, both[1], both[0])
     low, high = jnp.where(even, off_chip, on_chip), jnp.where(even, on_chip, off_chip)
-    (packed,) = call(pack_own_kernel, (shape(128, 256, dtype=BF16),), (own, nxt), [], 8, 10**8)
     message = shape(128, 128, dtype=BF16)
-    to_right, to_left = call(pack_rim_kernel, (message, message), (low, high, packed), [], 8, 10**8)
+    to_right, to_left = call(pack_kernel, (message, message), (nxt, low, high, packed, pick), [], 8, 10**8)
     from_left = passed(to_right, "gy", 1)
     from_right = passed(to_left, "gy", -1)
-    inner, part, edge_taps = call(
+    inner, part = call(
         inner_kernel,
-        (shape(3, WX, NZ, WY), shape(2, 2, 128, WY), shape(4, 256, WY, dtype=BF16)),
-        (own, nxt, low, high),
+        (shape(3, WX, NZ, WY), shape(2, 2, 128, WY)),
+        (own, nxt, low, high, taps, octet_taps),
         [
             planes_of(32),
             planes_of(32),
@@ -347,7 +355,7 @@
     (flow,) = call(
         strip_kernel,
         (shape(3, NZ * WX, WY),),
-        (inner, part, edge_taps, from_left, from_right),
+        (inner, part, edge_taps, place, from_left, from_right),
         [
             planes_of(12),
             planes_of(12),

time: 38.4 us -> 36.4 us (0.948)
  starting transfers between devices: 11.8 us -> 9.22 us
  blocking collectives: 0 us -> 2.41 us
  waiting for transfers between devices: 20.4 us -> 18 us
  local copies, waits for them, and re-layouts: 0.94 us -> 1.39 us
    ppermute x2 -> x1, starting transfers between devices: 4.51 us -> 1.92 us  [swapped(): return lax.ppermute(value, axis, pairs + [(b, a) for a, b in pairs])]
    all_gather x0 -> x1, blocking collectives: none -> 2.41 us  [on_device(): lax.all_gather(jnp.where(even, upper, lower), 'gx', axis_index_groups=pairs)]
    ppermute x2 -> x1, waiting for transfers between devices: 4.72 us -> 3.13 us  [swapped(): return lax.ppermute(value, axis, pairs + [(b, a) for a, b in pairs])]
    unnamed x4 -> x6, local copies, waits for them, and re-layouts: 0.01 us -> 1.32 us
    another operation x2, local copies, waits for them, and re-layouts: 0.93 us -> 0.07 us  [on_device(): jnp.stack([own[:, :EDGE], nxt[:, :EDGE]])]
    ppermute x3, waiting for transfers between devices: 15.7 us -> 14.9 us  [passed(): return lax.ppermute(value, axis, pairs)]
  transfers between devices with their start and end apart: 5 -> 4, of which waited for: 3 -> 3; matrix products, arithmetic and copies ran while one was open for 2% -> 0% of each run, Pallas kernels for 6% -> 6%
where the time goes in v6:
time: 36.4 us; the launch traced here: 36.2 us
  waiting for transfers between devices  18 us (49%)
  starting transfers between devices  9.22 us (25%)
  Pallas kernels  4.88 us (13%)
  blocking collectives  2.41 us (7%)
  local copies, waits for them, and re-layouts  1.39 us (4%)
    ppermute x3, waiting for transfers between devices, passed(): return lax.ppermute(value, axis, pairs)  14.9 us
    ppermute x3, starting transfers between devices, passed(): return lax.ppermute(value, axis, pairs)  7.3 us
    pallas_call x4, Pallas kernels, call(): pl.pallas_call(kernel, out_shape=outs, in_specs=[spec] * len(args), out_s...  4.88 us
    ppermute x1, waiting for transfers between devices, swapped(): return lax.ppermute(value, axis, pairs + [(b, a) for a, b in pairs])  3.13 us
    all_gather x1, blocking collectives, on_device(): lax.all_gather(jnp.where(even, upper, lower), 'gx', axis_index_groups=pairs)  2.41 us
    ppermute x1, starting transfers between devices, swapped(): return lax.ppermute(value, axis, pairs + [(b, a) for a, b in pairs])  1.92 us
    unnamed x6, local copies, waits for them, and re-layouts  1.32 us
  transfers between devices with their start and end apart: 4, of which 3 were waited for; matrix products, arithmetic and copies ran while one was open for 0% of the time, Pallas kernels for 6%

profile of v6, /device:TPU:38, one launch (start us, length us, event | category | flops | bytes accessed | tf_op | source)
XLA Modules:
  0.0 36.2 jit_solution(6317564980249670163)
XLA Ops:
  0.0 2.7 %collective-permute-start = (bf16[32,16,128]{2,1,0:T(8,128)(2,1)}, bf16[32,16,128]{2,1,0:T(8,128)(2,1)S(1)}, u32[]{:S(2)}, u32[]{:S(2)}) collective-permute-start(bf16[32,16,128]{2,1,0:T(8,128)(2,1)} %bitcast.24), channel_id=1, source_target_pairs={{64,0},{128,64},{192,128},{256,192},{320,256},{384,320},{448,384},... | collective-permute-start | bytes 393224 | tf_op jit(solution)/shard_map/ppermute | solution.py:309
  2.7 0.0 copy-start
  2.8 0.9 %copy-done = bf16[1,32,16,128]{3,2,1,0:T(8,128)(2,1)S(1)} copy-done((bf16[1,32,16,128]{3,2,1,0:T(8,128)(2,1)S(1)}, bf16[1,32,16,128]{3,2,1,0:T(8,128)(2,1)}, u32[]{:S(2)}) %copy-start) | copy-done | bytes 131096
  3.6 0.0 copy-start.1
  3.7 0.5 %shard_map.28 = (bf16[128,256]{1,0:T(8,128)(2,1)S(1)}, bf16[128,256]{1,0:T(8,128)(2,1)S(1)}, bf16[128,128]{1,0:T(8,128)(2,1)S(1)}, bf16[512,128]{1,0:T(8,128)(2,...) custom-call(bf16[32,16,128]{2,1,0:T(8,128)(2,1)S(1)} %bitcast.25), custom_call_target="tpu_custom_call" | custom-call | flops 100000000 | bytes 753664 | tf_op jit(solution)/shard_map/pallas_call | solution.py:288
  4.1 0.4 %copy-done.1 = bf16[1,32,16,128]{3,2,1,0:T(8,128)(2,1)S(1)} copy-done((bf16[1,32,16,128]{3,2,1,0:T(8,128)(2,1)S(1)}, bf16[1,32,16,128]{3,2,1,0:T(8,128)(2,1)}, u32[]{:S(2)}) %copy-start.1) | copy-done | bytes 131096
  4.6 0.0 copy-start.2
  4.6 10.0 %collective-permute-done = bf16[32,16,128]{2,1,0:T(8,128)(2,1)S(1)} collective-permute-done((bf16[32,16,128]{2,1,0:T(8,128)(2,1)}, bf16[32,16,128]{2,1,0:T(8,128)(2,1)S(1)}, u32[]{:S(2)}, u32[]{:S(2)}) %collective-permute-start) | collective-permute-done | bytes 131104 | tf_op jit(solution)/shard_map/ppermute | solution.py:309
  14.6 0.0 copy-done.2
  14.7 1.9 %collective-permute-start.1 = (bf16[2,32,8,128]{3,2,1,0:T(8,128)(2,1)S(1)}, bf16[2,32,8,128]{3,2,1,0:T(8,128)(2,1)S(1)}, u32[]{:S(2)}, u32[]{:S(2)}) collective-permute-start(bf16[2,32,8,128]{3,2,1,0:T(8,128)(2,1)S(1)} %maximum_select_fusion), channel_id=1, source_target_pairs={{4,8},{12,16},{20,24},{28,32},{36,40},{44,48},{52,56},{8,4},{16,12... | collective-permute-start | bytes 393224 | tf_op jit(solution)/shard_map/ppermute | solution.py:313
  16.7 2.4 %all_gather.4 = bf16[2,2,32,8,128]{4,3,2,1,0:T(8,128)(2,1)S(1)} all-gather(bf16[1,2,32,8,128]{4,3,2,1,0:T(8,128)(2,1)S(1)} %maximum_select_fusion.1), channel_id=1, replica_groups={{0,4},{8,12},{16,20},{24,28},{32,36},{40,44},{48,52},{56,60},{1,5},{9,1..., dimensions={0}, use_global_device_ids=true | all-gather | bytes 393216 | tf_op jit(solution)/shard_map/all_gather | solution.py:332
  19.1 3.1 %collective-permute-done.1 = bf16[2,32,8,128]{3,2,1,0:T(8,128)(2,1)S(1)} collective-permute-done((bf16[2,32,8,128]{3,2,1,0:T(8,128)(2,1)S(1)}, bf16[2,32,8,128]{3,2,1,0:T(8,128)(2,1)S(1)}, u32[]{:S(2)}, u32[]{:S(2)}) %collective-permute-start.1) | collective-permute-done | bytes 131104 | tf_op jit(solution)/shard_map/ppermute | solution.py:313
  22.2 0.4 shard_map.30
  22.6 3.3 %collective-permute-start.2 = (bf16[128,128]{1,0:T(8,128)(2,1)S(1)}, bf16[128,128]{1,0:T(8,128)(2,1)S(1)}, u32[]{:S(2)}, u32[]{:S(2)}) collective-permute-start(bf16[128,128]{1,0:T(8,128)(2,1)S(1)} %get-tuple-element.23), channel_id=1, source_target_pairs={{0,1},{1,2},{2,3},{4,5},{5,6},{6,7},{8,9},{9,10},{10,11},{12,13},{... | collective-permute-start | bytes 98312 | tf_op jit(solution)/shard_map/ppermute | solution.py:309
  25.9 1.3 %collective-permute-start.3 = (bf16[128,128]{1,0:T(8,128)(2,1)S(1)}, bf16[128,128]{1,0:T(8,128)(2,1)S(1)}, u32[]{:S(2)}, u32[]{:S(2)}) collective-permute-start(bf16[128,128]{1,0:T(8,128)(2,1)S(1)} %get-tuple-element.24), channel_id=1, source_target_pairs={{1,0},{2,1},{3,2},{5,4},{6,5},{7,6},{9,8},{10,9},{11,10},{13,12},{... | collective-permute-start | bytes 98312 | tf_op jit(solution)/shard_map/ppermute | solution.py:309
  27.2 1.9 %shard_map.29 = (f32[3,16,32,128]{3,2,1,0:T(8,128)S(1)}, f32[2,2,128,128]{3,2,1,0:T(8,128)S(1)}) custom-call(bf16[32,16,128]{2,1,0:T(8,128)(2,1)S(1)} %bitcast.27, bf16[32,16,128]{2,1,0:T(8,128)(2,1)S(1)} %broadcast_select_fusion.2.nxt, bf16[2,32,8,128]{3,2,1,0:T(8,128)(2,1)S(1)} %get-tuple-element.26.low, ...), custom_call_target="tpu_custom_call" | custom-call | flops 1000000000 | bytes 1736704 | tf_op jit(solution)/shard_map/pallas_call | solution.py:288
  29.1 0.0 collective-permute-done.2.from_left
  29.1 4.9 %collective-permute-done.3.from_right = bf16[128,128]{1,0:T(8,128)(2,1)S(1)} collective-permute-done((bf16[128,128]{1,0:T(8,128)(2,1)S(1)}, bf16[128,128]{1,0:T(8,128)(2,1)S(1)}, u32[]{:S(2)}, u32[]{:S(2)}) %collective-permute-start.3) | collective-permute-done | bytes 32800 | tf_op jit(solution)/shard_map/ppermute | solution.py:309
  34.0 2.2 %shard_map.31 = f32[3,512,128]{2,1,0:T(8,128)} custom-call(f32[3,16,32,128]{3,2,1,0:T(8,128)S(1)} %get-tuple-element.17.inner, f32[2,2,128,128]{3,2,1,0:T(8,128)S(1)} %get-tuple-element.18.part, bf16[4,256,128]{2,1,0:T(8,128)(2,1)S(1)} %get-tuple-element.19.edge_taps, bf16[128,256]{1,0:T(8,128)(2,1)S(1)} %get-tuple-element.20.place, ...), custom_call_target="tpu_custom_call" | custom-call | flops 100000000 | bytes 2228224 | tf_op jit(solution)/shard_map/pallas_call | solution.py:288
  (6 shorter events, 0.2 us)
Async XLA Ops:
  0.0 14.6 %collective-permute-start = (bf16[32,16,128]{2,1,0:T(8,128)(2,1)}, bf16[32,16,128]{2,1,0:T(8,128)(2,1)S(1)}, u32[]{:S(2)}, u32[]{:S(2)}) collective-permute-start(bf16[32,16,128]{2,1,0:T(8,128)(2,1)} %bitcast.24), channel_id=1, source_target_pairs={{64,0},{128,64},{192,128},{256,192},{320,256},{384,320},{448,384},... | collective-permute-start | bytes 393224 | tf_op jit(solution)/shard_map/ppermute | solution.py:309
  2.7 0.9 %copy-start = (bf16[1,32,16,128]{3,2,1,0:T(8,128)(2,1)S(1)}, bf16[1,32,16,128]{3,2,1,0:T(8,128)(2,1)}, u32[]{:S(2)}) copy-start(bf16[1,32,16,128]{3,2,1,0:T(8,128)(2,1)} %param.2) | copy-start | bytes 393220
  3.6 0.9 %copy-start.1 = (bf16[1,32,16,128]{3,2,1,0:T(8,128)(2,1)S(1)}, bf16[1,32,16,128]{3,2,1,0:T(8,128)(2,1)}, u32[]{:S(2)}) copy-start(bf16[1,32,16,128]{3,2,1,0:T(8,128)(2,1)} %param.2) | copy-start | bytes 393220
  4.6 10.1 %copy-start.2 = (bf16[32,16,128]{2,1,0:T(8,128)(2,1)S(1)}, bf16[32,16,128]{2,1,0:T(8,128)(2,1)}, u32[]{:S(2)}) copy-start(bf16[32,16,128]{2,1,0:T(8,128)(2,1)} %param.3) | copy-start | bytes 393220
  14.7 7.5 %collective-permute-start.1 = (bf16[2,32,8,128]{3,2,1,0:T(8,128)(2,1)S(1)}, bf16[2,32,8,128]{3,2,1,0:T(8,128)(2,1)S(1)}, u32[]{:S(2)}, u32[]{:S(2)}) collective-permute-start(bf16[2,32,8,128]{3,2,1,0:T(8,128)(2,1)S(1)} %maximum_select_fusion), channel_id=1, source_target_pairs={{4,8},{12,16},{20,24},{28,32},{36,40},{44,48},{52,56},{8,4},{16,12... | collective-permute-start | bytes 393224 | tf_op jit(solution)/shard_map/ppermute | solution.py:313
  22.6 6.5 %collective-permute-start.2 = (bf16[128,128]{1,0:T(8,128)(2,1)S(1)}, bf16[128,128]{1,0:T(8,128)(2,1)S(1)}, u32[]{:S(2)}, u32[]{:S(2)}) collective-permute-start(bf16[128,128]{1,0:T(8,128)(2,1)S(1)} %get-tuple-element.23), channel_id=1, source_target_pairs={{0,1},{1,2},{2,3},{4,5},{5,6},{6,7},{8,9},{9,10},{10,11},{12,13},{... | collective-permute-start | bytes 98312 | tf_op jit(solution)/shard_map/ppermute | solution.py:309
  25.9 8.1 %collective-permute-start.3 = (bf16[128,128]{1,0:T(8,128)(2,1)S(1)}, bf16[128,128]{1,0:T(8,128)(2,1)S(1)}, u32[]{:S(2)}, u32[]{:S(2)}) collective-permute-start(bf16[128,128]{1,0:T(8,128)(2,1)S(1)} %get-tuple-element.24), channel_id=1, source_target_pairs={{1,0},{2,1},{3,2},{5,4},{6,5},{7,6},{9,8},{10,9},{11,10},{13,12},{... | collective-permute-start | bytes 98312 | tf_op jit(solution)/shard_map/ppermute | solution.py:309

commit v7 on v6

--- a/solution.py
+++ b/solution.py
@@ -50,11 +50,13 @@
     return {(octet, frame): block[:, 8 * octet - 8 : 8 * octet, :] for octet in (1, 2)}
 
 
-def front_kernel(own, packed, pick, taps, octet_taps, edge_taps, place):
+def front_kernel(
+    own, low, high, packed, pick, taps, octet_taps, edge_taps, place, smooth, part, p_ref
+):
     row, lane = iota((WY, 256), 0), iota((WY, 256), 1)
     column = (lane & 7) + jnp.where(lane < 128, WY - EDGE, 0)
     pick[...] = jnp.where(row == column, 1.0, 0.0).astype(BF16)
-    packed[...] = edge_columns(own_octets(own, 0), pick[...])
+    packed[...] = edge_columns(own_octets(own, 0) | {(0, 0): low, (3, 0): high}, pick[...])
 
     at, to = row & 31, lane & 127
     hit = ((row >> 5) - 1 == (lane >> 7)) & ((to == at - 5) | (to == at + 101))
@@ -72,11 +74,14 @@
     for group in range(4):
         edge_taps[group] = jnp.where(((row >> 3) & 3) == group, edge, 0.0).astype(BF16)
 
+    p = Planes(p_ref)
+    smooth_yz(p, own, low, high, taps, octet_taps, part)
+    for k in range(22):
+        smooth[k] = smooth_x(p, k + 5)
+
 
 def pack_kernel(nxt, low, high, packed, pick, to_right, to_left):
-    blocks = own_octets(nxt, 1)
-    blocks |= {(octet, frame): block[frame] for octet, block in ((0, low), (3, high)) for frame in range(2)}
-    both = packed[...] + edge_columns(blocks, pick[...])
+    both = packed[...] + edge_columns(own_octets(nxt, 1) | {(0, 1): low, (3, 1): high}, pick[...])
     to_right[...] = both[:, :128]
     to_left[...] = both[:, 128:]
 
@@ -147,6 +152,25 @@
     return [mean - term * common for mean, term in zip(means, terms)]
 
 
+def smooth_yz(p, frame, low, high, taps, octet_taps, part):
+    p.clear(3, 28)
+    for z_half in range(2):
+        zs = slice(16 * z_half, 16 * z_half + 16)
+        octets = []
+        for octet in range(4):
+            block = (
+                frame[zs, 8 * octet - 8 : 8 * octet, :] if octet in (1, 2) else (low if octet == 0 else high)[zs]
+            )
+            rows = block.astype(F32).reshape(128, WY).astype(BF16)
+            octets.append(rows)
+            found = dot(rows, taps[...])
+            for i in range(16):
+                p.put_z(8 * octet, 16 * z_half + i, found[8 * i : 8 * i + 8])
+        part[z_half] = dot(jnp.concatenate(octets, axis=1), octet_taps[...])
+    for k in range(3, 29):
+        p.put(k, smooth_z(p, k))
+
+
 def inside():
     faces = []
     for axis in ("gx", "gy"):
@@ -155,7 +179,9 @@
     return faces
 
 
-def inner_kernel(own, nxt, low, high, taps, octet_taps, inner, part, p_ref, q_ref, s_ref, c_ref, h_ref, u_ref, v_ref):
+def inner_kernel(
+    nxt, low, high, taps, octet_taps, smooth, inner, part, p_ref, s_ref, c_ref, h_ref, u_ref, v_ref
+):
     x_low, x_high, _, _ = inside()
 
     def weight(x):
@@ -164,42 +190,19 @@
     def weighed(value, x):
         return value if weight(x) is None else value * weight(x)
 
-    p, q, s = Planes(p_ref), Planes(q_ref), Planes(s_ref)
+    p, s = Planes(p_ref), Planes(s_ref)
     u, v = [Planes(u_ref, c) for c in range(3)], [Planes(v_ref, c) for c in range(3)]
-    p.clear(3, 28)
-    q.clear(3, 28)
     s.clear(1, 20)
     for c in range(3):
         u[c].clear(1, 18)
         v[c].clear(1, 16)
-
-    for z_half in range(2):
-        octets = [[], []]
-        for octet in range(4):
-            found = []
-            for frame, centre in enumerate((own, nxt)):
-                block = (
-                    (low if octet == 0 else high)[frame, 16 * z_half : 16 * z_half + 16]
-                    if octet in (0, 3)
-                    else centre[16 * z_half : 16 * z_half + 16, 8 * octet - 8 : 8 * octet, :]
-                )
-                rows = block.astype(F32).reshape(128, WY).astype(BF16)
-                octets[frame].append(rows)
-                found.append(dot(rows, taps[...]))
-            total, change = (found[0] + found[1]) * 0.25, found[1] - found[0]
-            for i in range(16):
-                p.put_z(8 * octet, 16 * z_half + i, total[8 * i : 8 * i + 8])
-                q.put_z(8 * octet, 16 * z_half + i, change[8 * i : 8 * i + 8])
-        for frame in range(2):
-            part[frame, z_half] = dot(jnp.concatenate(octets[frame], axis=1), octet_taps[...])
-
-    for k in range(3, 29):
-        p.put(k, smooth_z(p, k))
-        q.put(k, smooth_z(q, k))
+    smooth_yz(p, nxt, low, high, taps, octet_taps, part)
+
     for k in range(22):
-        s.put(k, weighed(smooth_x(p, k + 5), k - 3))
+        first, second = smooth[k], smooth_x(p, k + 5)
+        s.put(k, weighed((first + second) * 0.25, k - 3))
         if 1 <= k <= 20:
-            c_ref[k - 1] = weighed(smooth_x(q, k + 5), k - 3)
+            c_ref[k - 1] = weighed(second - first, k - 3)
 
     for k in range(20):
         terms, change = gradient_terms(s, k + 1, c_ref[k])
@@ -216,7 +219,10 @@
             inner[c, x] = value
 
 
-def strip_kernel(inner, part, edge_taps, place, from_left, from_right, out, p_ref, q_ref, s_ref, c_ref, h_ref, u_ref, v_ref, w_ref, done_ref, sems):
+def strip_kernel(
+    inner, part_own, part_nxt, edge_taps, place, from_left, from_right, out,
+    p_ref, q_ref, s_ref, c_ref, h_ref, u_ref, v_ref, w_ref, done_ref, sems,
+):
     x_low, x_high, y_low, y_high = inside()
     lane = iota((1, WY), 1)
     column = strip_column(lane)
@@ -240,7 +246,10 @@
 
     edges = jnp.concatenate([from_left[...], from_right[...]], axis=1)
     for z_half in range(2):
-        found = [part[frame, z_half] + dot(edges, edge_taps[2 * frame + z_half]) for frame in range(2)]
+        found = [
+            part[z_half] + dot(edges, edge_taps[2 * frame + z_half])
+            for frame, part in enumerate((part_own, part_nxt))
+        ]
         total, change = (found[0] + found[1]) * 0.25, found[1] - found[0]
         for i in range(16):
             p.put_z(2, 16 * z_half + i, total[8 * i : 8 * i + 8])
@@ -313,35 +322,40 @@
         return lax.ppermute(value, axis, pairs + [(b, a) for a, b in pairs])
 
     arriving = passed(own, "ta", -1)
-    packed, pick, taps, octet_taps, edge_taps, place = call(
+    nxt = jnp.where(lax.axis_index("ta") == lax.axis_size("ta") - 1, trailing, arriving)
+    even = lax.axis_index("gx") % 2 == 0
+
+    def rims(frame):
+        upper, lower = frame[:, WX - EDGE :], frame[:, :EDGE]
+        off_chip = swapped(jnp.where(even, lower, upper), "gx", 1)
+        pairs = [[i, i + 1] for i in range(0, lax.axis_size("gx"), 2)]
+        both = lax.all_gather(jnp.where(even, upper, lower), "gx", axis_index_groups=pairs)
+        on_chip = jnp.where(even, both[1], both[0])
+        return jnp.where(even, off_chip, on_chip), jnp.where(even, on_chip, off_chip)
+
+    low_own, high_own = rims(own)
+    packed, pick, taps, octet_taps, edge_taps, place, smooth, part_own = call(
         front_kernel,
         tuple(
             shape(*dims, dtype=BF16)
             for dims in ((128, 256), (WY, 256), (WY, WY), (4 * WY, WY), (4, 256, WY), (WY, 256))
-        ),
-        (own,),
-        [],
-        8,
+        )
+        + (shape(22, NZ, WY), shape(2, 128, WY)),
+        (own, low_own, high_own),
+        [planes_of(32)],
+        12,
         10**8,
     )
-    nxt = jnp.where(lax.axis_index("ta") == lax.axis_size("ta") - 1, trailing, arriving)
-    upper, lower = jnp.stack([own[:, WX - EDGE :], nxt[:, WX - EDGE :]]), jnp.stack([own[:, :EDGE], nxt[:, :EDGE]])
-    even = lax.axis_index("gx") % 2 == 0
-    off_chip = swapped(jnp.where(even, lower, upper), "gx", 1)
-    pairs = [[i, i + 1] for i in range(0, lax.axis_size("gx"), 2)]
-    both = lax.all_gather(jnp.where(even, upper, lower), "gx", axis_index_groups=pairs)
-    on_chip = jnp.where(even, both[1], both[0])
-    low, high = jnp.where(even, off_chip, on_chip), jnp.where(even, on_chip, off_chip)
+    low, high = rims(nxt)
     message = shape(128, 128, dtype=BF16)
     to_right, to_left = call(pack_kernel, (message, message), (nxt, low, high, packed, pick), [], 8, 10**8)
     from_left = passed(to_right, "gy", 1)
     from_right = passed(to_left, "gy", -1)
-    inner, part = call(
+    inner, part_nxt = call(
         inner_kernel,
-        (shape(3, WX, NZ, WY), shape(2, 2, 128, WY)),
-        (own, nxt, low, high, taps, octet_taps),
+        (shape(3, WX, NZ, WY), shape(2, 128, WY)),
+        (nxt, low, high, taps, octet_taps, smooth),
         [
-            planes_of(32),
             planes_of(32),
             planes_of(22),
             pltpu.VMEM((20, NZ, WY), F32),
@@ -355,7 +369,7 @@
     (flow,) = call(
         strip_kernel,
         (shape(3, NZ * WX, WY),),
-        (inner, part, edge_taps, place, from_left, from_right),
+        (inner, part_own, part_nxt, edge_taps, place, from_left, from_right),
         [
             planes_of(12),
             planes_of(12),

time: 36.4 us -> 36.1 us (level)
  the two profiles are of different devices: /device:TPU:38 before, /device:TPU:30 now
where the time goes in v7:
time: 36.1 us; the launch traced here: 35.8 us
  starting transfers between devices  11.4 us (32%)
  waiting for transfers between devices  9.58 us (27%)
  blocking collectives  8.88 us (25%)
  Pallas kernels  4.85 us (13%)
  other arithmetic  0.95 us (3%)
    ppermute x3, waiting for transfers between devices, passed(): return lax.ppermute(value, axis, pairs)  9.57 us
    all_gather x2, blocking collectives, rims(): lax.all_gather(jnp.where(even, upper, lower), 'gx', axis_index_groups=pairs)  8.88 us
    ppermute x3, starting transfers between devices, passed(): return lax.ppermute(value, axis, pairs)  7.3 us
    pallas_call x4, Pallas kernels, call(): pl.pallas_call(kernel, out_shape=outs, in_specs=[spec] * len(args), out_s...  4.85 us
    ppermute x2, starting transfers between devices, swapped(): return lax.ppermute(value, axis, pairs + [(b, a) for a, b in pairs])  4.1 us
    select_n x2, other arithmetic, rims(): jnp.where(even, upper, lower)  0.9 us
  transfers between devices with their start and end apart: 5, of which 2 were waited for; matrix products, arithmetic and copies ran while one was open for 3% of the time, Pallas kernels for 7%

profile of v7, /device:TPU:30, one launch (start us, length us, event | category | flops | bytes accessed | tf_op | source)
XLA Modules:
  0.0 35.8 jit_solution(15478691809936436696)
XLA Ops:
  0.0 2.7 %collective-permute-start = (bf16[32,16,128]{2,1,0:T(8,128)(2,1)}, bf16[32,16,128]{2,1,0:T(8,128)(2,1)S(1)}, u32[]{:S(2)}, u32[]{:S(2)}) collective-permute-start(bf16[32,16,128]{2,1,0:T(8,128)(2,1)} %bitcast.2), channel_id=1, source_target_pairs={{64,0},{128,64},{192,128},{256,192},{320,256},{384,320},{448,384},... | collective-permute-start | bytes 393224 | tf_op jit(solution)/shard_map/ppermute | solution.py:318
  2.7 0.9 %broadcast_select_fusion.3 = (bf16[32,8,128]{2,1,0:T(8,128)(2,1)S(1)}, bf16[32,8,128]{2,1,0:T(8,128)(2,1)S(1)}) fusion(pred[]{:T(512)S(6)} %eq.9, bf16[32,16,128]{2,1,0:T(8,128)(2,1)} %bitcast.3), kind=kLoop, calls=%fused_computation.5 | loop fusion | flops 65536 | bytes 262145 | tf_op jit(solution)/shard_map/jit(_where)/select_n | solution.py:332
  3.6 0.0 copy-start.1
  3.7 2.1 %collective-permute-start.2 = (bf16[32,8,128]{2,1,0:T(8,128)(2,1)S(1)}, bf16[32,8,128]{2,1,0:T(8,128)(2,1)S(1)}, u32[]{:S(2)}, u32[]{:S(2)}) collective-permute-start(bf16[32,8,128]{2,1,0:T(8,128)(2,1)S(1)} %get-tuple-element.34), channel_id=1, source_target_pairs={{4,8},{12,16},{20,24},{28,32},{36,40},{44,48},{52,56},{8,4},{16,12... | collective-permute-start | bytes 196616 | tf_op jit(solution)/shard_map/ppermute | solution.py:322
  5.7 4.4 %all-gather.1 = bf16[64,8,128]{2,1,0:T(8,128)(2,1)S(1)} all-gather(bf16[32,8,128]{2,1,0:T(8,128)(2,1)S(1)} %get-tuple-element.33), channel_id=3, replica_groups={{0,4},{8,12},{16,20},{24,28},{32,36},{40,44},{48,52},{56,60},{1,5},{9,1..., dimensions={0}, use_global_device_ids=true | all-gather | bytes 196608 | tf_op jit(solution)/shard_map/all_gather | solution.py:332
  10.2 4.5 %collective-permute-done = bf16[32,16,128]{2,1,0:T(8,128)(2,1)S(1)} collective-permute-done((bf16[32,16,128]{2,1,0:T(8,128)(2,1)}, bf16[32,16,128]{2,1,0:T(8,128)(2,1)S(1)}, u32[]{:S(2)}, u32[]{:S(2)}) %collective-permute-start) | collective-permute-done | bytes 131104 | tf_op jit(solution)/shard_map/ppermute | solution.py:318
  14.6 0.0 copy-done.1
  14.7 0.0 copy-start
  14.7 2.1 %collective-permute-start.1 = (bf16[32,8,128]{2,1,0:T(8,128)(2,1)S(1)}, bf16[32,8,128]{2,1,0:T(8,128)(2,1)S(1)}, u32[]{:S(2)}, u32[]{:S(2)}) collective-permute-start(bf16[32,8,128]{2,1,0:T(8,128)(2,1)S(1)} %get-tuple-element.36), channel_id=1, source_target_pairs={{4,8},{12,16},{20,24},{28,32},{36,40},{44,48},{52,56},{8,4},{16,12... | collective-permute-start | bytes 196616 | tf_op jit(solution)/shard_map/ppermute | solution.py:322
  16.7 0.0 collective-permute-done.2
  16.8 0.0 copy-done
  16.8 0.7 %shard_map.28 = (bf16[128,256]{1,0:T(8,128)(2,1)S(1)}, bf16[128,256]{1,0:T(8,128)(2,1)S(1)}, bf16[128,128]{1,0:T(8,128)(2,1)S(1)}, bf16[512,128]{1,0:T(8,128)(2,...) custom-call(bf16[32,16,128]{2,1,0:T(8,128)(2,1)S(1)} %bitcast.4, ...), custom_call_target="tpu_custom_call" | custom-call | flops 100000000 | bytes 1376256 | tf_op jit(solution)/shard_map/pallas_call | solution.py:297
  17.5 4.4 %all-gather = bf16[64,8,128]{2,1,0:T(8,128)(2,1)S(1)} all-gather(bf16[32,8,128]{2,1,0:T(8,128)(2,1)S(1)} %get-tuple-element.35), channel_id=2, replica_groups={{0,4},{8,12},{16,20},{24,28},{32,36},{40,44},{48,52},{56,60},{1,5},{9,1..., dimensions={0}, use_global_device_ids=true | all-gather | bytes 196608 | tf_op jit(solution)/shard_map/all_gather | solution.py:332
  22.0 0.0 collective-permute-done.1
  22.0 0.3 shard_map.30
  22.3 3.3 %collective-permute-start.3 = (bf16[128,128]{1,0:T(8,128)(2,1)S(1)}, bf16[128,128]{1,0:T(8,128)(2,1)S(1)}, u32[]{:S(2)}, u32[]{:S(2)}) collective-permute-start(bf16[128,128]{1,0:T(8,128)(2,1)S(1)} %get-tuple-element.27), channel_id=1, source_target_pairs={{0,1},{1,2},{2,3},{4,5},{5,6},{6,7},{8,9},{9,10},{10,11},{12,13},{... | collective-permute-start | bytes 98312 | tf_op jit(solution)/shard_map/ppermute | solution.py:318
  25.6 1.3 %collective-permute-start.4 = (bf16[128,128]{1,0:T(8,128)(2,1)S(1)}, bf16[128,128]{1,0:T(8,128)(2,1)S(1)}, u32[]{:S(2)}, u32[]{:S(2)}) collective-permute-start(bf16[128,128]{1,0:T(8,128)(2,1)S(1)} %get-tuple-element.28), channel_id=1, source_target_pairs={{1,0},{2,1},{3,2},{5,4},{6,5},{7,6},{9,8},{10,9},{11,10},{13,12},{... | collective-permute-start | bytes 98312 | tf_op jit(solution)/shard_map/ppermute | solution.py:318
  26.9 1.6 %shard_map.29 = (f32[3,16,32,128]{3,2,1,0:T(8,128)S(1)}, f32[2,128,128]{2,1,0:T(8,128)S(1)}) custom-call(bf16[32,16,128]{2,1,0:T(8,128)(2,1)S(1)} %broadcast_select_fusion.nxt, bf16[32,8,128]{2,1,0:T(8,128)(2,1)S(1)} %get-tuple-element.32.low, bf16[32,8,128]{2,1,0:T(8,128)(2,1)S(1)} %get-tuple-element.31.high, bf16[128,128]{1,0:T(8,128)(2,1)S(1)} %get-tuple-element.17.taps, ...), custom_call_target="tpu_custom_call" | custom-call | flops 1000000000 | bytes 1703936 | tf_op jit(solution)/shard_map/pallas_call | solution.py:297
  28.5 0.0 collective-permute-done.3.from_left
  28.5 5.1 %collective-permute-done.4.from_right = bf16[128,128]{1,0:T(8,128)(2,1)S(1)} collective-permute-done((bf16[128,128]{1,0:T(8,128)(2,1)S(1)}, bf16[128,128]{1,0:T(8,128)(2,1)S(1)}, u32[]{:S(2)}, u32[]{:S(2)}) %collective-permute-start.4) | collective-permute-done | bytes 32800 | tf_op jit(solution)/shard_map/ppermute | solution.py:318
  33.6 2.2 %shard_map.31 = f32[3,512,128]{2,1,0:T(8,128)} custom-call(f32[3,16,32,128]{3,2,1,0:T(8,128)S(1)} %get-tuple-element.20.inner, f32[2,128,128]{2,1,0:T(8,128)S(1)} %get-tuple-element.21.part_own, f32[2,128,128]{2,1,0:T(8,128)S(1)} %get-tuple-element.22.part_nxt, bf16[4,256,128]{2,1,0:T(8,128)(2,1)S(1)} %get-tuple-element.23.edge_taps, ...), custom_call_target="tpu_custom_call" | custom-call | flops 100000000 | bytes 2228224 | tf_op jit(solution)/shard_map/pallas_call | solution.py:297
  (4 shorter events, 0.1 us)
Async XLA Ops:
  0.0 14.6 %collective-permute-start = (bf16[32,16,128]{2,1,0:T(8,128)(2,1)}, bf16[32,16,128]{2,1,0:T(8,128)(2,1)S(1)}, u32[]{:S(2)}, u32[]{:S(2)}) collective-permute-start(bf16[32,16,128]{2,1,0:T(8,128)(2,1)} %bitcast.2), channel_id=1, source_target_pairs={{64,0},{128,64},{192,128},{256,192},{320,256},{384,320},{448,384},... | collective-permute-start | bytes 393224 | tf_op jit(solution)/shard_map/ppermute | solution.py:318
  3.6 11.0 %copy-start.1 = (bf16[32,16,128]{2,1,0:T(8,128)(2,1)S(1)}, bf16[32,16,128]{2,1,0:T(8,128)(2,1)}, u32[]{:S(2)}) copy-start(bf16[32,16,128]{2,1,0:T(8,128)(2,1)} %param.3) | copy-start | bytes 393220
  3.7 13.1 %collective-permute-start.2 = (bf16[32,8,128]{2,1,0:T(8,128)(2,1)S(1)}, bf16[32,8,128]{2,1,0:T(8,128)(2,1)S(1)}, u32[]{:S(2)}, u32[]{:S(2)}) collective-permute-start(bf16[32,8,128]{2,1,0:T(8,128)(2,1)S(1)} %get-tuple-element.34), channel_id=1, source_target_pairs={{4,8},{12,16},{20,24},{28,32},{36,40},{44,48},{52,56},{8,4},{16,12... | collective-permute-start | bytes 196616 | tf_op jit(solution)/shard_map/ppermute | solution.py:322
  14.7 2.1 %copy-start = (bf16[1,32,16,128]{3,2,1,0:T(8,128)(2,1)S(1)}, bf16[1,32,16,128]{3,2,1,0:T(8,128)(2,1)}, u32[]{:S(2)}) copy-start(bf16[1,32,16,128]{3,2,1,0:T(8,128)(2,1)} %param.2) | copy-start | bytes 393220
  14.7 7.3 %collective-permute-start.1 = (bf16[32,8,128]{2,1,0:T(8,128)(2,1)S(1)}, bf16[32,8,128]{2,1,0:T(8,128)(2,1)S(1)}, u32[]{:S(2)}, u32[]{:S(2)}) collective-permute-start(bf16[32,8,128]{2,1,0:T(8,128)(2,1)S(1)} %get-tuple-element.36), channel_id=1, source_target_pairs={{4,8},{12,16},{20,24},{28,32},{36,40},{44,48},{52,56},{8,4},{16,12... | collective-permute-start | bytes 196616 | tf_op jit(solution)/shard_map/ppermute | solution.py:322
  22.3 6.2 %collective-permute-start.3 = (bf16[128,128]{1,0:T(8,128)(2,1)S(1)}, bf16[128,128]{1,0:T(8,128)(2,1)S(1)}, u32[]{:S(2)}, u32[]{:S(2)}) collective-permute-start(bf16[128,128]{1,0:T(8,128)(2,1)S(1)} %get-tuple-element.27), channel_id=1, source_target_pairs={{0,1},{1,2},{2,3},{4,5},{5,6},{6,7},{8,9},{9,10},{10,11},{12,13},{... | collective-permute-start | bytes 98312 | tf_op jit(solution)/shard_map/ppermute | solution.py:318
  25.6 8.1 %collective-permute-start.4 = (bf16[128,128]{1,0:T(8,128)(2,1)S(1)}, bf16[128,128]{1,0:T(8,128)(2,1)S(1)}, u32[]{:S(2)}, u32[]{:S(2)}) collective-permute-start(bf16[128,128]{1,0:T(8,128)(2,1)S(1)} %get-tuple-element.28), channel_id=1, source_target_pairs={{1,0},{2,1},{3,2},{5,4},{6,5},{7,6},{9,8},{10,9},{11,10},{13,12},{... | collective-permute-start | bytes 98312 | tf_op jit(solution)/shard_map/ppermute | solution.py:318

commit v8 on v7

--- a/solution.py
+++ b/solution.py
@@ -75,13 +75,21 @@
         edge_taps[group] = jnp.where(((row >> 3) & 3) == group, edge, 0.0).astype(BF16)
 
     p = Planes(p_ref)
-    smooth_yz(p, own, low, high, taps, octet_taps, part)
+    smooth_yz(p, own_blocks(own) | {0: low[...], 3: high[...]}, taps, octet_taps, part)
     for k in range(22):
         smooth[k] = smooth_x(p, k + 5)
 
 
-def pack_kernel(nxt, low, high, packed, pick, to_right, to_left):
-    both = packed[...] + edge_columns(own_octets(nxt, 1) | {(0, 1): low, (3, 1): high}, pick[...])
+def middle_kernel(nxt, own_packed, pick, taps, octet_taps, packed, middle, part, p_ref):
+    packed[...] = own_packed[...] + edge_columns(own_octets(nxt, 1), pick[...])
+    p = Planes(p_ref)
+    smooth_yz(p, own_blocks(nxt), taps, octet_taps, part)
+    for x in range(WX):
+        middle[x] = p.get(x + 8)
+
+
+def pack_kernel(low, high, packed, pick, to_right, to_left):
+    both = packed[...] + edge_columns({(0, 1): low, (3, 1): high}, pick[...])
     to_right[...] = both[:, :128]
     to_left[...] = both[:, 128:]
 
@@ -106,6 +114,14 @@
     def clear(self, first, last):
         for plane in range(first, last + 2):
             self.ref[self.rows(PITCH * plane, 8)] = jnp.zeros((8, WY), F32)
+
+
+class Rows:
+    def __init__(self, planes, middle):
+        self.planes, self.middle = planes, middle
+
+    def get(self, plane):
+        return self.middle[plane - 8] if 8 <= plane < 24 else self.planes.get(plane)
 
 
 def planes_of(count):
@@ -152,23 +168,26 @@
     return [mean - term * common for mean, term in zip(means, terms)]
 
 
-def smooth_yz(p, frame, low, high, taps, octet_taps, part):
-    p.clear(3, 28)
+def smooth_yz(p, blocks, taps, octet_taps, part, more=None):
+    planes = [8 * octet + i for octet in blocks for i in range(8) if 3 <= 8 * octet + i < 29]
+    for k in planes:
+        p.clear(k, k)
     for z_half in range(2):
-        zs = slice(16 * z_half, 16 * z_half + 16)
-        octets = []
-        for octet in range(4):
-            block = (
-                frame[zs, 8 * octet - 8 : 8 * octet, :] if octet in (1, 2) else (low if octet == 0 else high)[zs]
-            )
-            rows = block.astype(F32).reshape(128, WY).astype(BF16)
-            octets.append(rows)
+        given = None if more is None else more[z_half]
+        for octet, block in blocks.items():
+            rows = octet_rows(block, z_half)
             found = dot(rows, taps[...])
             for i in range(16):
                 p.put_z(8 * octet, 16 * z_half + i, found[8 * i : 8 * i + 8])
-        part[z_half] = dot(jnp.concatenate(octets, axis=1), octet_taps[...])
-    for k in range(3, 29):
+            gives = dot(rows, octet_taps[WY * octet : WY * octet + WY, :])
+            given = gives if given is None else given + gives
+        part[z_half] = given
+    for k in planes:
         p.put(k, smooth_z(p, k))
+
+
+def own_blocks(frame):
+    return {octet: frame[:, 8 * octet - 8 : 8 * octet, :] for octet in (1, 2)}
 
 
 def inside():
@@ -180,7 +199,7 @@
 
 
 def inner_kernel(
-    nxt, low, high, taps, octet_taps, smooth, inner, part, p_ref, s_ref, c_ref, h_ref, u_ref, v_ref
+    low, high, taps, octet_taps, smooth, middle, more, inner, part, p_ref, s_ref, c_ref, h_ref, u_ref, v_ref
 ):
     x_low, x_high, _, _ = inside()
 
@@ -196,10 +215,11 @@
     for c in range(3):
         u[c].clear(1, 18)
         v[c].clear(1, 16)
-    smooth_yz(p, nxt, low, high, taps, octet_taps, part)
+    smooth_yz(p, {0: low[...], 3: high[...]}, taps, octet_taps, part, more)
+    rows = Rows(p, middle)
 
     for k in range(22):
-        first, second = smooth[k], smooth_x(p, k + 5)
+        first, second = smooth[k], smooth_x(rows, k + 5)
         s.put(k, weighed((first + second) * 0.25, k - 3))
         if 1 <= k <= 20:
             c_ref[k - 1] = weighed(second - first, k - 3)
@@ -347,14 +367,22 @@
         10**8,
     )
     low, high = rims(nxt)
+    packed, middle, more = call(
+        middle_kernel,
+        (shape(128, 256, dtype=BF16), shape(WX, NZ, WY), shape(2, 128, WY)),
+        (nxt, packed, pick, taps, octet_taps),
+        [planes_of(32)],
+        8,
+        10**8,
+    )
     message = shape(128, 128, dtype=BF16)
-    to_right, to_left = call(pack_kernel, (message, message), (nxt, low, high, packed, pick), [], 8, 10**8)
+    to_right, to_left = call(pack_kernel, (message, message), (low, high, packed, pick), [], 8, 10**8)
     from_left = passed(to_right, "gy", 1)
     from_right = passed(to_left, "gy", -1)
     inner, part_nxt = call(
         inner_kernel,
         (shape(3, WX, NZ, WY), shape(2, 128, WY)),
-        (nxt, low, high, taps, octet_taps, smooth),
+        (low, high, taps, octet_taps, smooth, middle, more),
         [
             planes_of(32),
             planes_of(22),

time: 36.1 us -> 36.3 us (level)
    pallas_call x4 -> x5, Pallas kernels: 4.85 us -> 4.78 us  [call(): pl.pallas_call(kernel, out_shape=outs, in_specs=[spec] * len(args), out_s...]
where the time goes in v8:
time: 36.3 us; the launch traced here: 36 us
  starting transfers between devices  11.4 us (31%)
  waiting for transfers between devices  9.87 us (27%)
  blocking collectives  8.87 us (24%)
  Pallas kernels  4.78 us (13%)
  other arithmetic  0.95 us (3%)
    ppermute x3, waiting for transfers between devices, passed(): return lax.ppermute(value, axis, pairs)  9.87 us
    all_gather x2, blocking collectives, rims(): lax.all_gather(jnp.where(even, upper, lower), 'gx', axis_index_groups=pairs)  8.87 us
    ppermute x3, starting transfers between devices, passed(): return lax.ppermute(value, axis, pairs)  7.29 us
    pallas_call x5, Pallas kernels, call(): pl.pallas_call(kernel, out_shape=outs, in_specs=[spec] * len(args), out_s...  4.78 us
    ppermute x2, starting transfers between devices, swapped(): return lax.ppermute(value, axis, pairs + [(b, a) for a, b in pairs])  4.1 us
    select_n x2, other arithmetic, rims(): jnp.where(even, upper, lower)  0.9 us
  transfers between devices with their start and end apart: 5, of which 2 were waited for; matrix products, arithmetic and copies ran while one was open for 3% of the time, Pallas kernels for 7%

profile of v8, /device:TPU:30, one launch (start us, length us, event | category | flops | bytes accessed | tf_op | source)
XLA Modules:
  0.0 36.0 jit_solution(12356288337219153998)
XLA Ops:
  0.0 2.7 %collective-permute-start = (bf16[32,16,128]{2,1,0:T(8,128)(2,1)}, bf16[32,16,128]{2,1,0:T(8,128)(2,1)S(1)}, u32[]{:S(2)}, u32[]{:S(2)}) collective-permute-start(bf16[32,16,128]{2,1,0:T(8,128)(2,1)} %bitcast.2), channel_id=1, source_target_pairs={{64,0},{128,64},{192,128},{256,192},{320,256},{384,320},{448,384},... | collective-permute-start | bytes 393224 | tf_op jit(solution)/shard_map/ppermute | solution.py:338
  2.7 0.9 %broadcast_select_fusion.3 = (bf16[32,8,128]{2,1,0:T(8,128)(2,1)S(1)}, bf16[32,8,128]{2,1,0:T(8,128)(2,1)S(1)}) fusion(pred[]{:T(512)S(6)} %eq.8, bf16[32,16,128]{2,1,0:T(8,128)(2,1)} %bitcast.3), kind=kLoop, calls=%fused_computation.5 | loop fusion | flops 65536 | bytes 262145 | tf_op jit(solution)/shard_map/jit(_where)/select_n | solution.py:352
  3.6 0.0 copy-start.1
  3.7 2.1 %collective-permute-start.2 = (bf16[32,8,128]{2,1,0:T(8,128)(2,1)S(1)}, bf16[32,8,128]{2,1,0:T(8,128)(2,1)S(1)}, u32[]{:S(2)}, u32[]{:S(2)}) collective-permute-start(bf16[32,8,128]{2,1,0:T(8,128)(2,1)S(1)} %get-tuple-element.40), channel_id=1, source_target_pairs={{4,8},{12,16},{20,24},{28,32},{36,40},{44,48},{52,56},{8,4},{16,12... | collective-permute-start | bytes 196616 | tf_op jit(solution)/shard_map/ppermute | solution.py:342
  5.7 4.4 %all-gather.1 = bf16[64,8,128]{2,1,0:T(8,128)(2,1)S(1)} all-gather(bf16[32,8,128]{2,1,0:T(8,128)(2,1)S(1)} %get-tuple-element.39), channel_id=3, replica_groups={{0,4},{8,12},{16,20},{24,28},{32,36},{40,44},{48,52},{56,60},{1,5},{9,1..., dimensions={0}, use_global_device_ids=true | all-gather | bytes 196608 | tf_op jit(solution)/shard_map/all_gather | solution.py:352
  10.2 4.5 %collective-permute-done = bf16[32,16,128]{2,1,0:T(8,128)(2,1)S(1)} collective-permute-done((bf16[32,16,128]{2,1,0:T(8,128)(2,1)}, bf16[32,16,128]{2,1,0:T(8,128)(2,1)S(1)}, u32[]{:S(2)}, u32[]{:S(2)}) %collective-permute-start) | collective-permute-done | bytes 131104 | tf_op jit(solution)/shard_map/ppermute | solution.py:338
  14.6 0.0 copy-done.1
  14.7 0.0 copy-start
  14.7 2.1 %collective-permute-start.1 = (bf16[32,8,128]{2,1,0:T(8,128)(2,1)S(1)}, bf16[32,8,128]{2,1,0:T(8,128)(2,1)S(1)}, u32[]{:S(2)}, u32[]{:S(2)}) collective-permute-start(bf16[32,8,128]{2,1,0:T(8,128)(2,1)S(1)} %get-tuple-element.42), channel_id=1, source_target_pairs={{4,8},{12,16},{20,24},{28,32},{36,40},{44,48},{52,56},{8,4},{16,12... | collective-permute-start | bytes 196616 | tf_op jit(solution)/shard_map/ppermute | solution.py:342
  16.7 0.0 collective-permute-done.2
  16.8 0.0 copy-done
  16.8 0.7 %shard_map.28 = (bf16[128,256]{1,0:T(8,128)(2,1)S(1)}, bf16[128,256]{1,0:T(8,128)(2,1)S(1)}, bf16[128,128]{1,0:T(8,128)(2,1)S(1)}, bf16[512,128]{1,0:T(8,128)(2,...) custom-call(bf16[32,16,128]{2,1,0:T(8,128)(2,1)S(1)} %bitcast.4, ...), custom_call_target="tpu_custom_call" | custom-call | flops 100000000 | bytes 1376256 | tf_op jit(solution)/shard_map/pallas_call | solution.py:317
  17.5 0.3 shard_map.29
  17.8 4.4 %all-gather = bf16[64,8,128]{2,1,0:T(8,128)(2,1)S(1)} all-gather(bf16[32,8,128]{2,1,0:T(8,128)(2,1)S(1)} %get-tuple-element.41), channel_id=2, replica_groups={{0,4},{8,12},{16,20},{24,28},{32,36},{40,44},{48,52},{56,60},{1,5},{9,1..., dimensions={0}, use_global_device_ids=true | all-gather | bytes 196608 | tf_op jit(solution)/shard_map/all_gather | solution.py:352
  22.3 0.0 collective-permute-done.1
  22.3 0.2 shard_map.31
  22.5 3.3 %collective-permute-start.3 = (bf16[128,128]{1,0:T(8,128)(2,1)S(1)}, bf16[128,128]{1,0:T(8,128)(2,1)S(1)}, u32[]{:S(2)}, u32[]{:S(2)}) collective-permute-start(bf16[128,128]{1,0:T(8,128)(2,1)S(1)} %get-tuple-element.33), channel_id=1, source_target_pairs={{0,1},{1,2},{2,3},{4,5},{5,6},{6,7},{8,9},{9,10},{10,11},{12,13},{... | collective-permute-start | bytes 98312 | tf_op jit(solution)/shard_map/ppermute | solution.py:338
  25.8 1.3 %collective-permute-start.4 = (bf16[128,128]{1,0:T(8,128)(2,1)S(1)}, bf16[128,128]{1,0:T(8,128)(2,1)S(1)}, u32[]{:S(2)}, u32[]{:S(2)}) collective-permute-start(bf16[128,128]{1,0:T(8,128)(2,1)S(1)} %get-tuple-element.34), channel_id=1, source_target_pairs={{1,0},{2,1},{3,2},{5,4},{6,5},{7,6},{9,8},{10,9},{11,10},{13,12},{... | collective-permute-start | bytes 98312 | tf_op jit(solution)/shard_map/ppermute | solution.py:338
  27.1 1.3 %shard_map.30 = (f32[3,16,32,128]{3,2,1,0:T(8,128)S(1)}, f32[2,128,128]{2,1,0:T(8,128)S(1)}) custom-call(bf16[32,8,128]{2,1,0:T(8,128)(2,1)S(1)} %get-tuple-element.38.low, bf16[32,8,128]{2,1,0:T(8,128)(2,1)S(1)} %get-tuple-element.37.high, bf16[128,128]{1,0:T(8,128)(2,1)S(1)} %get-tuple-element.20.taps, bf16[512,128]{1,0:T(8,128)(2,1)S(1)} %get-tuple-element.21.octet_taps, ...), custom_call_target="tpu_custom_call" | custom-call | flops 1000000000 | bytes 1966080 | tf_op jit(solution)/shard_map/pallas_call | solution.py:317
  28.4 0.0 collective-permute-done.3.from_left
  28.4 5.4 %collective-permute-done.4.from_right = bf16[128,128]{1,0:T(8,128)(2,1)S(1)} collective-permute-done((bf16[128,128]{1,0:T(8,128)(2,1)S(1)}, bf16[128,128]{1,0:T(8,128)(2,1)S(1)}, u32[]{:S(2)}, u32[]{:S(2)}) %collective-permute-start.4) | collective-permute-done | bytes 32800 | tf_op jit(solution)/shard_map/ppermute | solution.py:338
  33.8 2.2 %shard_map.32 = f32[3,512,128]{2,1,0:T(8,128)} custom-call(f32[3,16,32,128]{3,2,1,0:T(8,128)S(1)} %get-tuple-element.27.inner, f32[2,128,128]{2,1,0:T(8,128)S(1)} %get-tuple-element.28.part_own, f32[2,128,128]{2,1,0:T(8,128)S(1)} %get-tuple-element.29.part_nxt, bf16[4,256,128]{2,1,0:T(8,128)(2,1)S(1)} %get-tuple-element.30.edge_taps, ...), custom_call_target="tpu_custom_call" | custom-call | flops 100000000 | bytes 2228224 | tf_op jit(solution)/shard_map/pallas_call | solution.py:317
  (4 shorter events, 0.1 us)
Async XLA Ops:
  0.0 14.6 %collective-permute-start = (bf16[32,16,128]{2,1,0:T(8,128)(2,1)}, bf16[32,16,128]{2,1,0:T(8,128)(2,1)S(1)}, u32[]{:S(2)}, u32[]{:S(2)}) collective-permute-start(bf16[32,16,128]{2,1,0:T(8,128)(2,1)} %bitcast.2), channel_id=1, source_target_pairs={{64,0},{128,64},{192,128},{256,192},{320,256},{384,320},{448,384},... | collective-permute-start | bytes 393224 | tf_op jit(solution)/shard_map/ppermute | solution.py:338
  3.6 11.0 %copy-start.1 = (bf16[32,16,128]{2,1,0:T(8,128)(2,1)S(1)}, bf16[32,16,128]{2,1,0:T(8,128)(2,1)}, u32[]{:S(2)}) copy-start(bf16[32,16,128]{2,1,0:T(8,128)(2,1)} %param.3) | copy-start | bytes 393220
  3.7 13.1 %collective-permute-start.2 = (bf16[32,8,128]{2,1,0:T(8,128)(2,1)S(1)}, bf16[32,8,128]{2,1,0:T(8,128)(2,1)S(1)}, u32[]{:S(2)}, u32[]{:S(2)}) collective-permute-start(bf16[32,8,128]{2,1,0:T(8,128)(2,1)S(1)} %get-tuple-element.40), channel_id=1, source_target_pairs={{4,8},{12,16},{20,24},{28,32},{36,40},{44,48},{52,56},{8,4},{16,12... | collective-permute-start | bytes 196616 | tf_op jit(solution)/shard_map/ppermute | solution.py:342
  14.7 2.1 %copy-start = (bf16[1,32,16,128]{3,2,1,0:T(8,128)(2,1)S(1)}, bf16[1,32,16,128]{3,2,1,0:T(8,128)(2,1)}, u32[]{:S(2)}) copy-start(bf16[1,32,16,128]{3,2,1,0:T(8,128)(2,1)} %param.2) | copy-start | bytes 393220
  14.7 7.6 %collective-permute-start.1 = (bf16[32,8,128]{2,1,0:T(8,128)(2,1)S(1)}, bf16[32,8,128]{2,1,0:T(8,128)(2,1)S(1)}, u32[]{:S(2)}, u32[]{:S(2)}) collective-permute-start(bf16[32,8,128]{2,1,0:T(8,128)(2,1)S(1)} %get-tuple-element.42), channel_id=1, source_target_pairs={{4,8},{12,16},{20,24},{28,32},{36,40},{44,48},{52,56},{8,4},{16,12... | collective-permute-start | bytes 196616 | tf_op jit(solution)/shard_map/ppermute | solution.py:342
  22.5 5.9 %collective-permute-start.3 = (bf16[128,128]{1,0:T(8,128)(2,1)S(1)}, bf16[128,128]{1,0:T(8,128)(2,1)S(1)}, u32[]{:S(2)}, u32[]{:S(2)}) collective-permute-start(bf16[128,128]{1,0:T(8,128)(2,1)S(1)} %get-tuple-element.33), channel_id=1, source_target_pairs={{0,1},{1,2},{2,3},{4,5},{5,6},{6,7},{8,9},{9,10},{10,11},{12,13},{... | collective-permute-start | bytes 98312 | tf_op jit(solution)/shard_map/ppermute | solution.py:338
  25.8 8.1 %collective-permute-start.4 = (bf16[128,128]{1,0:T(8,128)(2,1)S(1)}, bf16[128,128]{1,0:T(8,128)(2,1)S(1)}, u32[]{:S(2)}, u32[]{:S(2)}) collective-permute-start(bf16[128,128]{1,0:T(8,128)(2,1)S(1)} %get-tuple-element.34), channel_id=1, source_target_pairs={{1,0},{2,1},{3,2},{5,4},{6,5},{7,6},{9,8},{10,9},{11,10},{13,12},{... | collective-permute-start | bytes 98312 | tf_op jit(solution)/shard_map/ppermute | solution.py:338

commit v9 on v8

--- a/solution.py
+++ b/solution.py
@@ -163,7 +163,7 @@
         y_next, y_prev = y_pair(planes.get(k))
         total = (planes.get(k + 1) + planes.get(k - 1)) + (y_next + y_prev)
         total = total + (planes.get(k, 1) + planes.get(k, -1))
-        means.append(total * (1.0 / 6.0))
+        means.append(total)
     common = terms[3] + terms[0] * means[0] + terms[1] * means[1] + terms[2] * means[2]
     return [mean - term * common for mean, term in zip(means, terms)]
 
@@ -226,7 +226,7 @@
 
     for k in range(20):
         terms, change = gradient_terms(s, k + 1, c_ref[k])
-        h_ref[3, k] = change
+        h_ref[3, k] = 6.0 * change
         for c in range(3):
             h_ref[c, k] = terms[c]
             u[c].put(k, -terms[c] * change)
@@ -235,8 +235,8 @@
         for c, value in enumerate(jacobi(u, k + 1, [h_ref[c, k + 1] for c in range(4)])):
             v[c].put(k, weighed(value, k - 1))
     for x in range(WX):
-        for c, value in enumerate(jacobi(v, x + 1, [h_ref[c, x + 2] for c in range(4)])):
-            inner[c, x] = value
+        for c, value in enumerate(jacobi(v, x + 1, [h_ref[c, x + 2] for c in range(3)] + [6.0 * h_ref[3, x + 2]])):
+            inner[c, x] = value * (1.0 / 36.0)
 
 
 def strip_kernel(
@@ -282,7 +282,7 @@
         c_ref[i] = smooth_x(q, i + 2) * weight
     for i in range(8):
         terms, change = gradient_terms(s, i + 1, c_ref[i])
-        h_ref[3, i] = change
+        h_ref[3, i] = 6.0 * change
         for c in range(3):
             h_ref[c, i] = terms[c]
             put(u[c], i, -terms[c] * change, 1)
@@ -290,8 +290,8 @@
         for c, value in enumerate(jacobi(u, i + 1, [h_ref[c, i] for c in range(4)])):
             put(v[c], i, value * weight, 1)
     for i in range(8):
-        for c, value in enumerate(jacobi(v, i + 1, [h_ref[c, i] for c in range(4)])):
-            w_ref[c, NZ * i : NZ * i + NZ, :] = value
+        for c, value in enumerate(jacobi(v, i + 1, [h_ref[c, i] for c in range(3)] + [6.0 * h_ref[3, i]])):
+            w_ref[c, NZ * i : NZ * i + NZ, :] = value * (1.0 / 36.0)
     own_lane = iota((NZ, WY), 1)
     rim = (own_lane < 5) | (own_lane >= WY - 5)
     for c in range(3):

time: 36.3 us -> 36.3 us (level)
  no operation moved by 1% of the time
where the time goes in v9:
time: 36.3 us; the launch traced here: 36 us
  starting transfers between devices  11.4 us (31%)
  waiting for transfers between devices  9.88 us (27%)
  blocking collectives  8.87 us (24%)
  Pallas kernels  4.75 us (13%)
  other arithmetic  0.95 us (3%)
    ppermute x3, waiting for transfers between devices, passed(): return lax.ppermute(value, axis, pairs)  9.87 us
    all_gather x2, blocking collectives, rims(): lax.all_gather(jnp.where(even, upper, lower), 'gx', axis_index_groups=pairs)  8.87 us
    ppermute x3, starting transfers between devices, passed(): return lax.ppermute(value, axis, pairs)  7.29 us
    pallas_call x5, Pallas kernels, call(): pl.pallas_call(kernel, out_shape=outs, in_specs=[spec] * len(args), out_s...  4.75 us
    ppermute x2, starting transfers between devices, swapped(): return lax.ppermute(value, axis, pairs + [(b, a) for a, b in pairs])  4.1 us
    select_n x2, other arithmetic, rims(): jnp.where(even, upper, lower)  0.9 us
  transfers between devices with their start and end apart: 5, of which 2 were waited for; matrix products, arithmetic and copies ran while one was open for 3% of the time, Pallas kernels for 7%

profile of v9, /device:TPU:30, one launch (start us, length us, event | category | flops | bytes accessed | tf_op | source)
XLA Modules:
  0.0 36.0 jit_solution(11168452695022753361)
XLA Ops:
  0.0 2.7 %collective-permute-start = (bf16[32,16,128]{2,1,0:T(8,128)(2,1)}, bf16[32,16,128]{2,1,0:T(8,128)(2,1)S(1)}, u32[]{:S(2)}, u32[]{:S(2)}) collective-permute-start(bf16[32,16,128]{2,1,0:T(8,128)(2,1)} %bitcast.2), channel_id=1, source_target_pairs={{64,0},{128,64},{192,128},{256,192},{320,256},{384,320},{448,384},... | collective-permute-start | bytes 393224 | tf_op jit(solution)/shard_map/ppermute | solution.py:338
  2.7 0.9 %broadcast_select_fusion.3 = (bf16[32,8,128]{2,1,0:T(8,128)(2,1)S(1)}, bf16[32,8,128]{2,1,0:T(8,128)(2,1)S(1)}) fusion(pred[]{:T(512)S(6)} %eq.8, bf16[32,16,128]{2,1,0:T(8,128)(2,1)} %bitcast.3), kind=kLoop, calls=%fused_computation.5 | loop fusion | flops 65536 | bytes 262145 | tf_op jit(solution)/shard_map/jit(_where)/select_n | solution.py:352
  3.6 0.0 copy-start.1
  3.7 2.1 %collective-permute-start.2 = (bf16[32,8,128]{2,1,0:T(8,128)(2,1)S(1)}, bf16[32,8,128]{2,1,0:T(8,128)(2,1)S(1)}, u32[]{:S(2)}, u32[]{:S(2)}) collective-permute-start(bf16[32,8,128]{2,1,0:T(8,128)(2,1)S(1)} %get-tuple-element.40), channel_id=1, source_target_pairs={{4,8},{12,16},{20,24},{28,32},{36,40},{44,48},{52,56},{8,4},{16,12... | collective-permute-start | bytes 196616 | tf_op jit(solution)/shard_map/ppermute | solution.py:342
  5.7 4.4 %all-gather.1 = bf16[64,8,128]{2,1,0:T(8,128)(2,1)S(1)} all-gather(bf16[32,8,128]{2,1,0:T(8,128)(2,1)S(1)} %get-tuple-element.39), channel_id=3, replica_groups={{0,4},{8,12},{16,20},{24,28},{32,36},{40,44},{48,52},{56,60},{1,5},{9,1..., dimensions={0}, use_global_device_ids=true | all-gather | bytes 196608 | tf_op jit(solution)/shard_map/all_gather | solution.py:352
  10.2 4.5 %collective-permute-done = bf16[32,16,128]{2,1,0:T(8,128)(2,1)S(1)} collective-permute-done((bf16[32,16,128]{2,1,0:T(8,128)(2,1)}, bf16[32,16,128]{2,1,0:T(8,128)(2,1)S(1)}, u32[]{:S(2)}, u32[]{:S(2)}) %collective-permute-start) | collective-permute-done | bytes 131104 | tf_op jit(solution)/shard_map/ppermute | solution.py:338
  14.6 0.0 copy-done.1
  14.7 0.0 copy-start
  14.7 2.1 %collective-permute-start.1 = (bf16[32,8,128]{2,1,0:T(8,128)(2,1)S(1)}, bf16[32,8,128]{2,1,0:T(8,128)(2,1)S(1)}, u32[]{:S(2)}, u32[]{:S(2)}) collective-permute-start(bf16[32,8,128]{2,1,0:T(8,128)(2,1)S(1)} %get-tuple-element.42), channel_id=1, source_target_pairs={{4,8},{12,16},{20,24},{28,32},{36,40},{44,48},{52,56},{8,4},{16,12... | collective-permute-start | bytes 196616 | tf_op jit(solution)/shard_map/ppermute | solution.py:342
  16.7 0.0 collective-permute-done.2
  16.8 0.0 copy-done
  16.8 0.7 %shard_map.28 = (bf16[128,256]{1,0:T(8,128)(2,1)S(1)}, bf16[128,256]{1,0:T(8,128)(2,1)S(1)}, bf16[128,128]{1,0:T(8,128)(2,1)S(1)}, bf16[512,128]{1,0:T(8,128)(2,...) custom-call(bf16[32,16,128]{2,1,0:T(8,128)(2,1)S(1)} %bitcast.4, ...), custom_call_target="tpu_custom_call" | custom-call | flops 100000000 | bytes 1376256 | tf_op jit(solution)/shard_map/pallas_call | solution.py:317
  17.5 0.3 shard_map.29
  17.8 4.4 %all-gather = bf16[64,8,128]{2,1,0:T(8,128)(2,1)S(1)} all-gather(bf16[32,8,128]{2,1,0:T(8,128)(2,1)S(1)} %get-tuple-element.41), channel_id=2, replica_groups={{0,4},{8,12},{16,20},{24,28},{32,36},{40,44},{48,52},{56,60},{1,5},{9,1..., dimensions={0}, use_global_device_ids=true | all-gather | bytes 196608 | tf_op jit(solution)/shard_map/all_gather | solution.py:352
  22.3 0.0 collective-permute-done.1
  22.3 0.2 shard_map.31
  22.5 3.3 %collective-permute-start.3 = (bf16[128,128]{1,0:T(8,128)(2,1)S(1)}, bf16[128,128]{1,0:T(8,128)(2,1)S(1)}, u32[]{:S(2)}, u32[]{:S(2)}) collective-permute-start(bf16[128,128]{1,0:T(8,128)(2,1)S(1)} %get-tuple-element.33), channel_id=1, source_target_pairs={{0,1},{1,2},{2,3},{4,5},{5,6},{6,7},{8,9},{9,10},{10,11},{12,13},{... | collective-permute-start | bytes 98312 | tf_op jit(solution)/shard_map/ppermute | solution.py:338
  25.8 1.3 %collective-permute-start.4 = (bf16[128,128]{1,0:T(8,128)(2,1)S(1)}, bf16[128,128]{1,0:T(8,128)(2,1)S(1)}, u32[]{:S(2)}, u32[]{:S(2)}) collective-permute-start(bf16[128,128]{1,0:T(8,128)(2,1)S(1)} %get-tuple-element.34), channel_id=1, source_target_pairs={{1,0},{2,1},{3,2},{5,4},{6,5},{7,6},{9,8},{10,9},{11,10},{13,12},{... | collective-permute-start | bytes 98312 | tf_op jit(solution)/shard_map/ppermute | solution.py:338
  27.1 1.3 %shard_map.30 = (f32[3,16,32,128]{3,2,1,0:T(8,128)S(1)}, f32[2,128,128]{2,1,0:T(8,128)S(1)}) custom-call(bf16[32,8,128]{2,1,0:T(8,128)(2,1)S(1)} %get-tuple-element.38.low, bf16[32,8,128]{2,1,0:T(8,128)(2,1)S(1)} %get-tuple-element.37.high, bf16[128,128]{1,0:T(8,128)(2,1)S(1)} %get-tuple-element.20.taps, bf16[512,128]{1,0:T(8,128)(2,1)S(1)} %get-tuple-element.21.octet_taps, ...), custom_call_target="tpu_custom_call" | custom-call | flops 1000000000 | bytes 1966080 | tf_op jit(solution)/shard_map/pallas_call | solution.py:317
  28.4 0.0 collective-permute-done.3.from_left
  28.4 5.4 %collective-permute-done.4.from_right = bf16[128,128]{1,0:T(8,128)(2,1)S(1)} collective-permute-done((bf16[128,128]{1,0:T(8,128)(2,1)S(1)}, bf16[128,128]{1,0:T(8,128)(2,1)S(1)}, u32[]{:S(2)}, u32[]{:S(2)}) %collective-permute-start.4) | collective-permute-done | bytes 32800 | tf_op jit(solution)/shard_map/ppermute | solution.py:338
  33.8 2.2 %shard_map.32 = f32[3,512,128]{2,1,0:T(8,128)} custom-call(f32[3,16,32,128]{3,2,1,0:T(8,128)S(1)} %get-tuple-element.27.inner, f32[2,128,128]{2,1,0:T(8,128)S(1)} %get-tuple-element.28.part_own, f32[2,128,128]{2,1,0:T(8,128)S(1)} %get-tuple-element.29.part_nxt, bf16[4,256,128]{2,1,0:T(8,128)(2,1)S(1)} %get-tuple-element.30.edge_taps, ...), custom_call_target="tpu_custom_call" | custom-call | flops 100000000 | bytes 2228224 | tf_op jit(solution)/shard_map/pallas_call | solution.py:317
  (4 shorter events, 0.1 us)
Async XLA Ops:
  0.0 14.6 %collective-permute-start = (bf16[32,16,128]{2,1,0:T(8,128)(2,1)}, bf16[32,16,128]{2,1,0:T(8,128)(2,1)S(1)}, u32[]{:S(2)}, u32[]{:S(2)}) collective-permute-start(bf16[32,16,128]{2,1,0:T(8,128)(2,1)} %bitcast.2), channel_id=1, source_target_pairs={{64,0},{128,64},{192,128},{256,192},{320,256},{384,320},{448,384},... | collective-permute-start | bytes 393224 | tf_op jit(solution)/shard_map/ppermute | solution.py:338
  3.6 11.0 %copy-start.1 = (bf16[32,16,128]{2,1,0:T(8,128)(2,1)S(1)}, bf16[32,16,128]{2,1,0:T(8,128)(2,1)}, u32[]{:S(2)}) copy-start(bf16[32,16,128]{2,1,0:T(8,128)(2,1)} %param.3) | copy-start | bytes 393220
  3.7 13.1 %collective-permute-start.2 = (bf16[32,8,128]{2,1,0:T(8,128)(2,1)S(1)}, bf16[32,8,128]{2,1,0:T(8,128)(2,1)S(1)}, u32[]{:S(2)}, u32[]{:S(2)}) collective-permute-start(bf16[32,8,128]{2,1,0:T(8,128)(2,1)S(1)} %get-tuple-element.40), channel_id=1, source_target_pairs={{4,8},{12,16},{20,24},{28,32},{36,40},{44,48},{52,56},{8,4},{16,12... | collective-permute-start | bytes 196616 | tf_op jit(solution)/shard_map/ppermute | solution.py:342
  14.7 2.1 %copy-start = (bf16[1,32,16,128]{3,2,1,0:T(8,128)(2,1)S(1)}, bf16[1,32,16,128]{3,2,1,0:T(8,128)(2,1)}, u32[]{:S(2)}) copy-start(bf16[1,32,16,128]{3,2,1,0:T(8,128)(2,1)} %param.2) | copy-start | bytes 393220
  14.7 7.6 %collective-permute-start.1 = (bf16[32,8,128]{2,1,0:T(8,128)(2,1)S(1)}, bf16[32,8,128]{2,1,0:T(8,128)(2,1)S(1)}, u32[]{:S(2)}, u32[]{:S(2)}) collective-permute-start(bf16[32,8,128]{2,1,0:T(8,128)(2,1)S(1)} %get-tuple-element.42), channel_id=1, source_target_pairs={{4,8},{12,16},{20,24},{28,32},{36,40},{44,48},{52,56},{8,4},{16,12... | collective-permute-start | bytes 196616 | tf_op jit(solution)/shard_map/ppermute | solution.py:342
  22.5 5.9 %collective-permute-start.3 = (bf16[128,128]{1,0:T(8,128)(2,1)S(1)}, bf16[128,128]{1,0:T(8,128)(2,1)S(1)}, u32[]{:S(2)}, u32[]{:S(2)}) collective-permute-start(bf16[128,128]{1,0:T(8,128)(2,1)S(1)} %get-tuple-element.33), channel_id=1, source_target_pairs={{0,1},{1,2},{2,3},{4,5},{5,6},{6,7},{8,9},{9,10},{10,11},{12,13},{... | collective-permute-start | bytes 98312 | tf_op jit(solution)/shard_map/ppermute | solution.py:338
  25.8 8.1 %collective-permute-start.4 = (bf16[128,128]{1,0:T(8,128)(2,1)S(1)}, bf16[128,128]{1,0:T(8,128)(2,1)S(1)}, u32[]{:S(2)}, u32[]{:S(2)}) collective-permute-start(bf16[128,128]{1,0:T(8,128)(2,1)S(1)} %get-tuple-element.34), channel_id=1, source_target_pairs={{1,0},{2,1},{3,2},{5,4},{6,5},{7,6},{9,8},{10,9},{11,10},{13,12},{... | collective-permute-start | bytes 98312 | tf_op jit(solution)/shard_map/ppermute | solution.py:338
